TPU v7x, 32 devices: a whole 2x2x4 slice. The times are simulated.
32 devices in a mesh: section: 2 (over x), dp: 8 (over z, y), rep: 2 (over core).
Axes of the slice: x: 2, y: 2, z: 4, core: 2. Of those that a mesh axis runs over, the one named last changes fastest.
Arguments:
- boundary: bfloat16 [2, 48, 196, 768], P('section', ('dp', 'rep')), may hold values from -6 to 6
- keep_index: int32 [48, 196], P(('dp', 'rep')), may hold values from 0 to 195, each once within a row
- keep_count: int32 [48], P(('dp', 'rep')), may hold values from 49 to 196, as said below
- gain_one: bfloat16 [2, 768], P('section'), may hold values from 0.099609375 to 1.8984375
- shift_one: bfloat16 [2, 768], P('section'), may hold values from -1.5 to 1.5
- w_qkv: bfloat16 [2, 768, 2304], P('section'), may hold values from -0.3125 to 0.3125
- bias_query: bfloat16 [2, 768], P('section'), may hold values from -2.5 to 2.5
- bias_value: bfloat16 [2, 768], P('section'), may hold values from -2.5 to 2.5
- w_out: bfloat16 [2, 768, 768], P('section'), may hold values from -0.625 to 0.625
- bias_out: bfloat16 [2, 768], P('section'), may hold values from -1.5 to 1.5
- gain_two: bfloat16 [2, 768], P('section'), may hold values from 0.099609375 to 1.8984375
- shift_two: bfloat16 [2, 768], P('section'), may hold values from -1.5 to 1.5
- w_up: bfloat16 [2, 768, 3072], P('section'), may hold values from -0.21875 to 0.21875
- bias_up: bfloat16 [2, 3072], P('section'), may hold values from -2.5 to 2.5
- w_down: bfloat16 [2, 3072, 768], P('section'), may hold values from -0.109375 to 0.109375
- bias_down: bfloat16 [2, 768], P('section'), may hold values from -1.5 to 1.5
Outputs:
- section_outputs: bfloat16 [2, 48, 196, 768], P('section', ('dp', 'rep'))
- input_grads: bfloat16 [2, 48, 196, 768], P('section', ('dp', 'rep'))
- grad_gain_one: float32 [2, 768], P('section')
- grad_shift_one: float32 [2, 768], P('section')
- grad_w_qkv: float32 [2, 768, 2304], P('section')
- grad_bias_query: float32 [2, 768], P('section')
- grad_bias_value: float32 [2, 768], P('section')
- grad_w_out: float32 [2, 768, 768], P('section')
- grad_bias_out: float32 [2, 768], P('section')
- grad_gain_two: float32 [2, 768], P('section')
- grad_shift_two: float32 [2, 768], P('section')
- grad_w_up: float32 [2, 768, 3072], P('section')
- grad_bias_up: float32 [2, 3072], P('section')
- grad_w_down: float32 [2, 3072, 768], P('section')
- grad_bias_down: float32 [2, 768], P('section')
Inputs may be any that keep to these rules, and one draw needn't show every extreme that they name: `keep_count`: among the images of each index of dp and rep one keeps all 196 patches. `keep_index`: each row is a permutation of the patches.
All inputs are finite; a program needn't handle non-finite values.
Results may differ from a plain program's by a relative error of at most 0.025.
The roundings to bfloat16 on the way count: a program that leaves them out, or rounds other values in their place, can miss the bound.
Values may be sent and summed in bfloat16 or wider, within the bound.
No kernel may reach another device: no remote copies, remote signals or barrier semaphores. Data moves between devices by JAX's collectives and lax.ppermute only.
A program may use at most 256 MiB of HBM per device.

v0:
```python
from functools import partial
import math

import jax
import jax.numpy as jnp
from jax import lax
from jax.sharding import PartitionSpec as P

HEAD_DIM = 64
MICRO = 3


norm_eps = 1e-06
masked_score = -1e30


def from_behind(value, axis, by):
    length = lax.axis_size(axis)
    pairs = [(i, i + by) for i in range(length) if 0 <= i + by < length]
    return lax.ppermute(value, axis, pairs)


def layer_norm(values, gain, shift):
    row_mean = jnp.mean(values, axis=-1, keepdims=True)
    centred = values - row_mean
    variance = jnp.mean(centred * centred, axis=-1, keepdims=True)
    return centred * lax.rsqrt(variance + norm_eps) * gain + shift


def skipped(live, function, *operands):

    def blanks(*inner):
        return jax.tree.map(jnp.zeros_like, function(*inner))

    return lax.cond(live, function, blanks, *operands)


def forward(layer_in, valid_rows, params):
    (
        gain_one,
        shift_one,
        w_qkv,
        bias_query,
        bias_value,
        w_out,
        bias_out,
        gain_two,
        shift_two,
        w_up,
        bias_up,
        w_down,
        bias_down,
    ) = params
    batch_size, row_count, model_width = layer_in.shape
    head_count = model_width // HEAD_DIM
    heads_shape = (batch_size, row_count, head_count, HEAD_DIM)
    inputs = layer_in.astype(jnp.float32)
    normed = layer_norm(inputs, gain_one.astype(jnp.float32), shift_one.astype(jnp.float32)).astype(
        jnp.bfloat16
    )
    packed = jnp.dot(normed, w_qkv, preferred_element_type=jnp.float32)
    queries = (
        (packed[..., :model_width] + bias_query.astype(jnp.float32))
        .astype(jnp.bfloat16)
        .reshape(heads_shape)
    )
    key_rows = packed[..., model_width : 2 * model_width].astype(jnp.bfloat16).reshape(heads_shape)
    values = (
        (packed[..., 2 * model_width :] + bias_value.astype(jnp.float32))
        .astype(jnp.bfloat16)
        .reshape(heads_shape)
    )
    score_scale = 1.0 / math.sqrt(HEAD_DIM)
    scores = (
        jnp.einsum("bqhd,bkhd->bhqk", queries, key_rows, preferred_element_type=jnp.float32)
        * score_scale
    )
    scores = jnp.where(valid_rows[:, None, None, :] > 0, scores, masked_score)
    attention = jax.nn.softmax(scores, axis=-1).astype(jnp.bfloat16)
    attended = jnp.einsum("bhqk,bkhd->bqhd", attention, values, preferred_element_type=jnp.float32)
    attended = attended.reshape(batch_size, row_count, model_width).astype(jnp.bfloat16)
    residual = inputs + (
        jnp.dot(attended, w_out, preferred_element_type=jnp.float32) + bias_out.astype(jnp.float32)
    )
    normed_two = layer_norm(
        residual, gain_two.astype(jnp.float32), shift_two.astype(jnp.float32)
    ).astype(jnp.bfloat16)
    pre_gelu = jnp.dot(normed_two, w_up, preferred_element_type=jnp.float32) + bias_up.astype(
        jnp.float32
    )
    hidden = jax.nn.gelu(pre_gelu, approximate=False).astype(jnp.bfloat16)
    branch_two = jnp.dot(hidden, w_down, preferred_element_type=jnp.float32) + bias_down.astype(
        jnp.float32
    )
    output = (residual + branch_two) * valid_rows[..., None]
    saved_state = (
        inputs,
        normed,
        queries,
        key_rows,
        values,
        scores,
        attention,
        attended,
        residual,
        normed_two,
        pre_gelu,
        hidden,
    )
    return (output, saved_state)


def back_input(saved_state, valid_rows, grad_in, params):
    (
        gain_one,
        shift_one,
        w_qkv,
        bias_query,
        bias_value,
        w_out,
        bias_out,
        gain_two,
        shift_two,
        w_up,
        bias_up,
        w_down,
        bias_down,
    ) = params
    (
        inputs,
        normed,
        queries,
        key_rows,
        values,
        scores,
        attention,
        attended,
        residual,
        normed_two,
        pre_gelu,
        hidden,
    ) = saved_state
    batch_size, row_count, model_width = inputs.shape
    flat_shape = (batch_size, row_count, model_width)
    heads_shape = queries.shape
    score_scale = 1.0 / math.sqrt(HEAD_DIM)
    grad_out = grad_in.astype(jnp.float32) * valid_rows[..., None]
    grad_branch_two = grad_out.astype(jnp.bfloat16)
    grad_hidden = jnp.einsum(
        "bro,io->bri", grad_branch_two, w_down, preferred_element_type=jnp.float32
    )
    _, gelu_back = jax.vjp(partial(jax.nn.gelu, approximate=False), pre_gelu)
    grad_pre = gelu_back(grad_hidden)[0].astype(jnp.bfloat16)
    grad_normed_two = jnp.einsum("brf,df->brd", grad_pre, w_up, preferred_element_type=jnp.float32)
    _, second_norm_back = jax.vjp(
        layer_norm, residual, gain_two.astype(jnp.float32), shift_two.astype(jnp.float32)
    )
    grad_part, grad_gain_two, grad_shift_two = second_norm_back(grad_normed_two)
    grad_residual = grad_out + grad_part
    grad_branch = grad_residual.astype(jnp.bfloat16)
    grad_attended = jnp.einsum(
        "bre,de->brd", grad_branch, w_out, preferred_element_type=jnp.float32
    )
    grad_attended = grad_attended.astype(jnp.bfloat16).reshape(heads_shape)
    grad_attention = jnp.einsum(
        "bqhd,bkhd->bhqk", grad_attended, values, preferred_element_type=jnp.float32
    )
    grad_values = jnp.einsum(
        "bhqk,bqhd->bkhd", attention, grad_attended, preferred_element_type=jnp.float32
    )
    grad_values = grad_values.astype(jnp.bfloat16).reshape(flat_shape)
    _, soft_back = jax.vjp(partial(jax.nn.softmax, axis=-1), scores)
    grad_scores = jnp.where(
        valid_rows[:, None, None, :] > 0, soft_back(grad_attention)[0], 0.0
    ).astype(jnp.bfloat16)
    grad_queries = (
        (
            jnp.einsum("bhqk,bkhd->bqhd", grad_scores, key_rows, preferred_element_type=jnp.float32)
            * score_scale
        )
        .astype(jnp.bfloat16)
        .reshape(flat_shape)
    )
    grad_keys = (
        (
            jnp.einsum("bhqk,bqhd->bkhd", grad_scores, queries, preferred_element_type=jnp.float32)
            * score_scale
        )
        .astype(jnp.bfloat16)
        .reshape(flat_shape)
    )
    grad_packed = jnp.concatenate([grad_queries, grad_keys, grad_values], axis=-1)
    grad_normed = jnp.einsum("bre,de->brd", grad_packed, w_qkv, preferred_element_type=jnp.float32)
    _, first_norm_back = jax.vjp(
        layer_norm, inputs, gain_one.astype(jnp.float32), shift_one.astype(jnp.float32)
    )
    grad_input_part, grad_gain_one, grad_shift_one = first_norm_back(grad_normed)
    grad_input = grad_residual + grad_input_part
    pending = (
        normed,
        attended,
        normed_two,
        hidden,
        grad_branch_two,
        grad_pre,
        grad_branch,
        grad_packed,
    )
    norm_grads = (grad_gain_one, grad_shift_one, grad_gain_two, grad_shift_two)
    return (grad_input, pending, norm_grads)


def back_weights(pending):
    normed, attended, normed_two, hidden, grad_branch_two, grad_pre, grad_branch, grad_packed = (
        pending
    )
    model_width = normed.shape[2]
    grad_w_down = jnp.einsum(
        "bri,bro->io", hidden, grad_branch_two, preferred_element_type=jnp.float32
    )
    grad_bias_down = jnp.sum(grad_branch_two.astype(jnp.float32), axis=(0, 1))
    grad_w_up = jnp.einsum("brd,brf->df", normed_two, grad_pre, preferred_element_type=jnp.float32)
    grad_bias_up = jnp.sum(grad_pre.astype(jnp.float32), axis=(0, 1))
    grad_w_out = jnp.einsum(
        "brd,bre->de", attended, grad_branch, preferred_element_type=jnp.float32
    )
    grad_bias_out = jnp.sum(grad_branch.astype(jnp.float32), axis=(0, 1))
    grad_w_qkv = jnp.einsum("brd,bre->de", normed, grad_packed, preferred_element_type=jnp.float32)
    packed_sums = jnp.sum(grad_packed.astype(jnp.float32), axis=(0, 1))
    grad_bias_query = packed_sums[:model_width]
    grad_bias_value = packed_sums[2 * model_width :]
    return (
        grad_w_qkv,
        grad_bias_query,
        grad_bias_value,
        grad_w_out,
        grad_bias_out,
        grad_w_up,
        grad_bias_up,
        grad_w_down,
        grad_bias_down,
    )


def shards(
    boundary,
    keep_index,
    keep_count,
    gain_one,
    shift_one,
    w_qkv,
    bias_query,
    bias_value,
    w_out,
    bias_out,
    gain_two,
    shift_two,
    w_up,
    bias_up,
    w_down,
    bias_down,
):
    params = tuple(
        (
            weight[0]
            for weight in (
                gain_one,
                shift_one,
                w_qkv,
                bias_query,
                bias_value,
                w_out,
                bias_out,
                gain_two,
                shift_two,
                w_up,
                bias_up,
                w_down,
                bias_down,
            )
        )
    )
    first_section = lax.axis_index("section") == 0
    image_count, slot_count = keep_index.shape
    per_batch = image_count // MICRO
    slot_iota = lax.broadcasted_iota(jnp.int32, (image_count, slot_count), 1)
    valid_rows = (slot_iota < keep_count[:, None]).astype(jnp.float32)
    source = boundary[0]
    kept_rows = jnp.take_along_axis(source, keep_index[:, :, None], axis=1) * valid_rows[
        ..., None
    ].astype(jnp.bfloat16)
    inverse = jnp.argsort(keep_index, axis=1)

    def rows_of(array, index):
        return array[index * per_batch : (index + 1) * per_batch]

    def clamped(index):
        return min(max(index, 0), MICRO - 1)

    zero_rows = jnp.zeros((per_batch, slot_count, source.shape[2]), jnp.bfloat16)
    incoming = zero_rows
    returning = zero_rows
    forward_inputs = []
    forward_outputs = []
    backward_outputs = [zero_rows]
    grad_totals = tuple((jnp.zeros(weight.shape, jnp.float32) for weight in params))
    for tick_index in range(MICRO + 2):
        first_batch = clamped(tick_index)
        second_batch = clamped(tick_index - 1)
        late_batch = clamped(tick_index - 2)
        fresh = None
        if tick_index <= MICRO:
            live_forward = jnp.where(first_section, tick_index < MICRO, tick_index >= 1)
            layer_in = jnp.where(first_section, rows_of(kept_rows, first_batch), incoming)
            forward_valid = jnp.where(
                first_section, rows_of(valid_rows, first_batch), rows_of(valid_rows, second_batch)
            )
            output, fresh = skipped(live_forward, forward, layer_in, forward_valid, params)
            output = output.astype(jnp.bfloat16)
            if tick_index < MICRO:
                incoming = from_behind(output, "section", 1)
            forward_inputs.append(layer_in)
            forward_outputs.append(output)
        if tick_index == 0:
            continue
        live_back = jnp.where(first_section, tick_index >= 2, tick_index <= MICRO)
        back_valid = jnp.where(
            first_section, rows_of(valid_rows, late_batch), rows_of(valid_rows, second_batch)
        )
        grad_in = jnp.where(first_section, returning, rows_of(boundary[1], second_batch))
        if tick_index < 2:
            saved_state = fresh
        else:

            def recompute():
                return forward(forward_inputs[late_batch], back_valid, params)[1]

            if fresh is None:
                saved_state = recompute()
            else:

                def reuse():
                    return fresh

                saved_state = lax.cond(first_section, recompute, reuse)
        grad_input, pending, norm_grads = skipped(
            live_back, back_input, saved_state, back_valid, grad_in, params
        )
        grad_low = grad_input.astype(jnp.bfloat16)
        if tick_index <= MICRO:
            returning = from_behind(grad_low, "section", -1)
        backward_outputs.append(grad_low)
        weight_grads = skipped(live_back, back_weights, pending)
        full_grads = (
            norm_grads[0],
            norm_grads[1],
            weight_grads[0],
            weight_grads[1],
            weight_grads[2],
            weight_grads[3],
            weight_grads[4],
            norm_grads[2],
            norm_grads[3],
            weight_grads[5],
            weight_grads[6],
            weight_grads[7],
            weight_grads[8],
        )
        grad_totals = tuple((total + grad for total, grad in zip(grad_totals, full_grads)))
    act_rows = []
    grad_rows = []
    for batch_index in range(MICRO):
        act_rows.append(
            jnp.where(first_section, forward_outputs[batch_index], forward_outputs[batch_index + 1])
        )
        masked_grad = backward_outputs[batch_index + 2] * rows_of(valid_rows, batch_index)[
            ..., None
        ].astype(jnp.bfloat16)
        patch_order = jnp.take_along_axis(
            masked_grad, rows_of(inverse, batch_index)[:, :, None], axis=1
        )
        grad_rows.append(jnp.where(first_section, patch_order, backward_outputs[batch_index + 1]))
    section_outputs = jnp.concatenate(act_rows, axis=0)[None]
    input_grads = jnp.concatenate(grad_rows, axis=0)[None]
    total_images = image_count * lax.axis_size(("dp", "rep"))
    shares = (
        lax.psum_scatter(grad_totals[0], ("dp", "rep"), scatter_dimension=0, tiled=True),
        lax.psum_scatter(grad_totals[1], ("dp", "rep"), scatter_dimension=0, tiled=True),
        lax.psum_scatter(grad_totals[2], ("dp", "rep"), scatter_dimension=0, tiled=True),
        lax.psum_scatter(grad_totals[3], ("dp", "rep"), scatter_dimension=0, tiled=True),
        lax.psum_scatter(grad_totals[4], ("dp", "rep"), scatter_dimension=0, tiled=True),
        lax.psum_scatter(grad_totals[5], ("dp", "rep"), scatter_dimension=0, tiled=True),
        lax.psum_scatter(grad_totals[6], ("dp", "rep"), scatter_dimension=0, tiled=True),
        lax.psum_scatter(grad_totals[7], ("dp", "rep"), scatter_dimension=0, tiled=True),
        lax.psum_scatter(grad_totals[8], ("dp", "rep"), scatter_dimension=0, tiled=True),
        lax.psum_scatter(grad_totals[9], ("dp", "rep"), scatter_dimension=0, tiled=True),
        lax.psum_scatter(grad_totals[10], ("dp", "rep"), scatter_dimension=0, tiled=True),
        lax.psum_scatter(grad_totals[11], ("dp", "rep"), scatter_dimension=0, tiled=True),
        lax.psum_scatter(grad_totals[12], ("dp", "rep"), scatter_dimension=0, tiled=True),
    )
    scaled = tuple((share / total_images for share in shares))
    whole = (
        lax.all_gather(scaled[0].astype(jnp.bfloat16), ("dp", "rep"), axis=0, tiled=True).astype(
            jnp.float32
        ),
        lax.all_gather(scaled[1].astype(jnp.bfloat16), ("dp", "rep"), axis=0, tiled=True).astype(
            jnp.float32
        ),
        lax.all_gather(scaled[2].astype(jnp.bfloat16), ("dp", "rep"), axis=0, tiled=True).astype(
            jnp.float32
        ),
        lax.all_gather(scaled[3].astype(jnp.bfloat16), ("dp", "rep"), axis=0, tiled=True).astype(
            jnp.float32
        ),
        lax.all_gather(scaled[4].astype(jnp.bfloat16), ("dp", "rep"), axis=0, tiled=True).astype(
            jnp.float32
        ),
        lax.all_gather(scaled[5].astype(jnp.bfloat16), ("dp", "rep"), axis=0, tiled=True).astype(
            jnp.float32
        ),
        lax.all_gather(scaled[6].astype(jnp.bfloat16), ("dp", "rep"), axis=0, tiled=True).astype(
            jnp.float32
        ),
        lax.all_gather(scaled[7].astype(jnp.bfloat16), ("dp", "rep"), axis=0, tiled=True).astype(
            jnp.float32
        ),
        lax.all_gather(scaled[8].astype(jnp.bfloat16), ("dp", "rep"), axis=0, tiled=True).astype(
            jnp.float32
        ),
        lax.all_gather(scaled[9].astype(jnp.bfloat16), ("dp", "rep"), axis=0, tiled=True).astype(
            jnp.float32
        ),
        lax.all_gather(scaled[10].astype(jnp.bfloat16), ("dp", "rep"), axis=0, tiled=True).astype(
            jnp.float32
        ),
        lax.all_gather(scaled[11].astype(jnp.bfloat16), ("dp", "rep"), axis=0, tiled=True).astype(
            jnp.float32
        ),
        lax.all_gather(scaled[12].astype(jnp.bfloat16), ("dp", "rep"), axis=0, tiled=True).astype(
            jnp.float32
        ),
    )
    return (section_outputs, input_grads) + tuple((grad[None] for grad in whole))


def solution(mesh):
    placed = (
        P("section", ("dp", "rep"), None, None),
        P(("dp", "rep"), None),
        P(("dp", "rep")),
        P("section", None),
        P("section", None),
        P("section", None, None),
        P("section", None),
        P("section", None),
        P("section", None, None),
        P("section", None),
        P("section", None),
        P("section", None),
        P("section", None, None),
        P("section", None),
        P("section", None, None),
        P("section", None),
    )
    return jax.shard_map(
        shards,
        mesh=mesh,
        in_specs=placed,
        out_specs=(
            P("section", ("dp", "rep"), None, None),
            P("section", ("dp", "rep"), None, None),
            P("section", None),
            P("section", None),
            P("section", None, None),
            P("section", None),
            P("section", None),
            P("section", None, None),
            P("section", None),
            P("section", None),
            P("section", None),
            P("section", None, None),
            P("section", None),
            P("section", None, None),
            P("section", None),
        ),
        check_vma=False,
    )
```

profile of v0, /device:TPU:0, one launch (start us, length us, event | category | flops | bytes accessed | tf_op | source)
XLA Modules:
  0.0 1085.5 jit_solution(6425598387851248435)
XLA Ops:
  8.7 16.1 %gather_fusion = bf16[588,768]{1,0:T(8,128)(2,1)S(1)} fusion(bf16[3,196,768]{2,1,0:T(8,128)(2,1)} %bitcast.792, s32[588]{0:T(1024)S(1)} %reshape.3247), kind=kCustom, calls=%fused_computation.3 | custom fusion | bytes 1811040 | tf_op jit(solution)/shard_map/jit(take_along_axis)/gather | solution.py:289
  27.8 28.8 %conditional.8 = (bf16[1,196,768]{2,1,0:T(8,128)(2,1)S(1)}) conditional(s32[]{:T(128)} %convert_element_type.1017, () %tuple.155, (bf16[1,196,768]{2,1,0:T(8,128)(2,1)}, bf16[768]{0:T(1024)(128)(2,1)S(1)}, bf16[768]{0:T(1024)(128)(2,1)S(1)}, bf16[768,2304]{1,0:T(8,128)(2,1)}, bf16[768]{0:T(1024)(128)(2,1)S(1)}, /*index=5*/f32[1,196]{1,0:T(1,128)}, ...), branch_computations={%region_0.0_spmd, %region_1.8_spmd} | conditional | flops 2940028928 | bytes 36034156 | solution.py:35
  45.8 10.8 fusion.31
  85.3 8.8 fusion.257
  103.9 10.8 conditional.10
  116.0 12.8 %conditional.14 = (f32[768,2304]{1,0:T(8,128)}, f32[768]{0:T(1024)S(1)}, f32[768]{0:T(1024)S(1)}, f32[768,768]{1,0:T(8,128)S(1)}, f32[768]{0:T(1024)S(1)}, /*ind...) conditional(s32[]{:T(128)} %convert_element_type.1049, () %tuple.167, ...), branch_computations={%region_111.113_spmd, %region_112.0_spmd} | conditional | flops 2777234688 | bytes 38888548 | solution.py:35
  156.3 8.5 fusion.260
  168.1 56.7 %collective-permute-start.2 = (bf16[1,196,768]{2,1,0:T(8,128)(2,1)}, bf16[1,196,768]{2,1,0:T(8,128)(2,1)}, u32[]{:S(2)}, u32[]{:S(2)}) collective-permute-start(bf16[1,196,768]{2,1,0:T(8,128)(2,1)} %fusion.332), channel_id=1, source_target_pairs={{0,16},{1,17},{2,18},{3,19},{4,20},{5,21},{6,22},{7,23},{8,24},{9,... | collective-permute-start | bytes 903176 | tf_op jit(solution)/shard_map/ppermute | solution.py:20
  224.9 32.5 %conditional.11 = (f32[1,196,768]{2,1,0:T(8,128)S(1)}, f32[1,196,768]{2,1,0:T(8,128)S(1)}, bf16[12,196,196]{1,2,0:T(8,128)(2,1)}, bf16[196,3072]{1,0:T(8,128)(2,...) conditional(s32[]{:T(128)} %convert_element_type.1017, ...), branch_computations={%region_45.46_spmd, %region_46.53_spmd} | conditional | flops 2073908736 | bytes 60585436 | solution.py:345
  246.0 9.0 fusion.210
  260.6 9.6 convert_reduce_fusion.10
  302.2 8.4 fusion.273
  310.7 12.0 %conditional.9 = (f32[1,196,768]{2,1,0:T(8,128)S(1)}, bf16[1,196,768]{2,1,0:T(8,128)(2,1)}, bf16[1,196,12,64]{1,3,2,0:T(8,128)(2,1)}, bf16[1,196,12,64]{1,3,2,0:...) conditional(s32[]{:T(128)} %convert_element_type.1049, ...), branch_computations={%region_20.21_spmd, %region_21.28_spmd} | conditional | flops 3000578560 | bytes 111472856 | solution.py:35
  322.7 40.5 %conditional.12 = (f32[1,196,768]{2,1,0:T(8,128)S(1)}, f32[1,12,196,196]{2,3,1,0:T(8,128)}, f32[1,196,768]{2,1,0:T(8,128)}, f32[1,196,3072]{2,1,0:T(8,128)}, bf1...) conditional(s32[]{:T(128)} %convert_element_type.1017, ...), branch_computations={%region_65.67_spmd, %region_66.74_spmd} | conditional | flops 2074059264 | bytes 53359876 | solution.py:345
  355.3 7.5 fusion.229
  367.9 9.4 convert_reduce_fusion.9
  404.1 8.4 collective-permute-done.5
  412.5 40.9 %conditional.13 = (bf16[1,196,768]{2,1,0:T(8,128)(2,1)}, bf16[1,196,768]{1,2,0:T(8,128)(2,1)}, bf16[1,196,768]{2,1,0:T(8,128)(2,1)}, bf16[1,196,3072]{2,1,0:T(8,...) conditional(s32[]{:T(128)} %convert_element_type.1017, ...), branch_computations={%region_88.90_spmd, %region_89.106_spmd} | conditional | flops 3070269440 | bytes 108854240 | solution.py:35
  413.9 8.8 fusion.158
  453.5 23.4 %conditional.15 = (f32[768,2304]{1,0:T(8,128)}, f32[768]{0:T(1024)S(1)}, f32[768]{0:T(1024)S(1)}, f32[768,768]{1,0:T(8,128)S(1)}, f32[768]{0:T(1024)S(1)}, /*ind...) conditional(s32[]{:T(128)} %convert_element_type.1017, () %tuple.169, ...), branch_computations={%region_117.119_spmd, %region_118.0_spmd} | conditional | flops 2777234688 | bytes 38888548 | solution.py:35
  485.3 7.5 add_add_fusion.8
  495.9 13.1 %add_add_fusion.7 = f32[768,3072]{1,0:T(8,128)} fusion(f32[768,3072]{1,0:T(8,128)} %get-tuple-element.994, f32[768,3072]{1,0:T(8,128)} %get-tuple-element.991, f32[768,3072]{1,0:T(8,128)S(1)} %fusion.358, bf16[1,196,3072]{2,1,0:T(8,128)(2,1)S(1)} %copy-done.130, bf16[1,196,768]{2,1,0:T(8,128)(2,1)} %get-tuple-element.993), kind=kOutput, calls=%fused_computation.434 | convolution fusion | flops 931921920 | bytes 39254016 | tf_op jit(solution)/shard_map/cond/branch_1_fun/brd,brf->df/dot_general | solution.py:222
  512.9 12.8 %add_add_fusion.6 = f32[3072,768]{1,0:T(8,128)} fusion(f32[3072,768]{1,0:T(8,128)} %get-tuple-element.1000, f32[3072,768]{1,0:T(8,128)} %get-tuple-element.997, f32[3072,768]{1,0:T(8,128)S(1)} %fusion.375, bf16[196,3072]{1,0:T(8,128)(2,1)} %get-tuple-element.999, bf16[1,196,768]{2,1,0:T(8,128)(2,1)S(1)} %copy-done.57, f32[196]{0:T(256)S(1)} %bitcast.890), kind=kOutput, calls=%fused_computation.433 | convolution fusion | flops 932373504 | bytes 39254800 | tf_op jit(solution)/shard_map/cond/branch_1_fun/bri,bro->io/dot_general | solution.py:218
  525.7 19.4 %reduce-scatter.7.cloned.1.call-done = f32[48,768]{1,0:T(8,128)} async-done(((f32[768,768]{1,0:T(8,128)}), f32[48,768]{1,0:T(8,128)}) %reduce-scatter.7.cloned.1.call-update) | async-done | bytes 147472 | tf_op jit(solution)/shard_map/reduce_scatter | solution.py:392
  546.8 92.6 %reduce-scatter.5.cloned.1.call-done = f32[48,2304]{1,0:T(8,128)} async-done(((f32[768,2304]{1,0:T(8,128)}), f32[48,2304]{1,0:T(8,128)}) %reduce-scatter.5.cloned.1.call-update) | async-done | bytes 442384 | tf_op jit(solution)/shard_map/reduce_scatter | solution.py:389
  641.2 113.8 %reduce-scatter.9.cloned.1.call-done = f32[48,3072]{1,0:T(8,128)} async-done(((f32[768,3072]{1,0:T(8,128)}), f32[48,3072]{1,0:T(8,128)}) %reduce-scatter.9.cloned.1.call-update) | async-done | bytes 589840 | tf_op jit(solution)/shard_map/reduce_scatter | solution.py:396
  756.9 114.3 %reduce-scatter.11.cloned.1.call-done = f32[192,768]{1,0:T(8,128)} async-done(((f32[3072,768]{1,0:T(8,128)}), f32[192,768]{1,0:T(8,128)}) %reduce-scatter.11.cloned.1.call-update) | async-done | bytes 589840 | tf_op jit(solution)/shard_map/reduce_scatter | solution.py:398
  891.7 61.1 %all-reduce.18 = (f32[768]{0:T(1024)S(1)}, f32[768]{0:T(1024)S(1)}, f32[768]{0:T(1024)S(1)}, f32[768]{0:T(1024)S(1)}, f32[768]{0:T(1024)S(1)}, /*index=5*/f32[76...) all-reduce(f32[768]{0:T(1024)S(1)} %get-tuple-element.1474, ...), channel_id=2, replica_groups=mesh['section'=2,'dp'=8,'rep'=2] {'dp','rep'}, use_global_device_ids=true, to_apply=%region_107.109.clone | all-reduce | flops 9216 | bytes 73728
  967.4 59.0 %all-reduce.19 = (bf16[768]{0:T(1024)(128)(2,1)S(1)}, bf16[768]{0:T(1024)(128)(2,1)S(1)}, bf16[768]{0:T(1024)(128)(2,1)S(1)}, bf16[768]{0:T(1024)(128)(2,1)S(1)}...) all-reduce(bf16[768]{0:T(1024)(128)(2,1)S(1)} %dynamic-update-slice, ...), channel_id=1, replica_groups=mesh['section'=2,'dp'=8,'rep'=2] {'dp','rep'}, use_global_device_ids=true, to_apply=%add | all-reduce | flops 9216 | bytes 36864
  1043.3 7.5 bitcast_convert_fusion.1
  1050.8 20.5 %all-gather.11.cloned.1.call-done = bf16[3072,768]{1,0:T(8,128)(2,1)} async-done(((bf16[192,768]{1,0:T(8,128)(2,1)}), bf16[3072,768]{1,0:T(8,128)(2,1)}) %all-gather.11.cloned.1.call-update) | async-done | bytes 4718608 | tf_op jit(solution)/shard_map/all_gather | solution.py:436
  1071.3 6.8 bitcast_convert_fusion
  (796 shorter events, 372.6 us)
Async XLA Ops:
  7.2 538.0 %reduce-scatter.7.cloned.1.call-start = ((), (), s32[]{:S(2)}) async-start(), calls=%async_computation.6 | async-start | bytes 2506752 | tf_op jit(solution)/shard_map/reduce_scatter | solution.py:392
  27.0 197.8 %copy-start.131 = (bf16[768]{0:T(1024)(128)(2,1)}, bf16[768]{0:T(1024)(128)(2,1)S(1)}, u32[]{:S(2)}) copy-start(bf16[768]{0:T(1024)(128)(2,1)S(1)} %reduce.216) | copy-start | bytes 4612
  27.1 197.7 %copy-start.133 = (bf16[768]{0:T(1024)(128)(2,1)}, bf16[768]{0:T(1024)(128)(2,1)S(1)}, u32[]{:S(2)}) copy-start(bf16[768]{0:T(1024)(128)(2,1)S(1)} %reduce.218) | copy-start | bytes 4612
  27.8 38.2 %copy-start.6 = (bf16[1,3,196,768]{3,2,1,0:T(8,128)(2,1)S(1)}, bf16[1,3,196,768]{3,2,1,0:T(8,128)(2,1)}, u32[]{:S(2)}) copy-start(bf16[1,3,196,768]{3,2,1,0:T(8,128)(2,1)} %param.34) | copy-start | bytes 2709508
  56.6 10.1 collective-permute-start
  58.3 27.0 %copy-start.156 = (f32[3072]{0:T(1024)}, f32[3072]{0:T(1024)S(1)}, u32[]{:S(2)}) copy-start(f32[3072]{0:T(1024)S(1)} %convert_element_type.1035) | copy-start | bytes 36868
  59.0 35.1 %copy-start.171 = (f32[768]{0:T(1024)}, f32[768]{0:T(1024)S(1)}, u32[]{:S(2)}) copy-start(f32[768]{0:T(1024)S(1)} %convert_element_type.1037) | copy-start | bytes 9220
  97.4 31.5 %collective-permute-start.1 = (bf16[1,196,768]{2,1,0:T(8,128)(2,1)}, bf16[1,196,768]{2,1,0:T(8,128)(2,1)}, u32[]{:S(2)}, u32[]{:S(2)}) collective-permute-start(bf16[1,196,768]{2,1,0:T(8,128)(2,1)} %fusion.333), channel_id=1, source_target_pairs={{0,16},{1,17},{2,18},{3,19},{4,20},{5,21},{6,22},{7,23},{8,24},{9,... | collective-permute-start | bytes 903176 | tf_op jit(solution)/shard_map/ppermute | solution.py:20
  114.7 144.0 %collective-permute-start.3 = (bf16[1,196,768]{2,1,0:T(8,128)(2,1)}, bf16[1,196,768]{2,1,0:T(8,128)(2,1)}, u32[]{:S(2)}, u32[]{:S(2)}) collective-permute-start(bf16[1,196,768]{2,1,0:T(8,128)(2,1)} %get-tuple-element.919), channel_id=1, source_target_pairs={{16,0},{17,1},{18,2},{19,3},{20,4},{21,5},{22,6},{23,7},{24,8},{25... | collective-permute-start | bytes 903176 | tf_op jit(solution)/shard_map/ppermute | solution.py:20
  134.9 90.0 %copy-start.58 = (bf16[1,196,768]{2,1,0:T(8,128)(2,1)}, bf16[1,196,768]{2,1,0:T(8,128)(2,1)S(1)}, u32[]{:S(2)}) copy-start(bf16[1,196,768]{2,1,0:T(8,128)(2,1)S(1)} %get-tuple-element.1693) | copy-start | bytes 903172
  164.8 60.0 %copy-start.21 = (f32[1,196,768]{2,1,0:T(8,128)S(1)}, f32[1,196,768]{2,1,0:T(8,128)}, u32[]{:S(2)}) copy-start(f32[1,196,768]{2,1,0:T(8,128)} %get-tuple-element.1695) | copy-start | bytes 1806340
  164.8 60.0 %copy-start.50 = (bf16[1,196,768]{2,1,0:T(8,128)(2,1)S(1)}, bf16[1,196,768]{2,1,0:T(8,128)(2,1)}, u32[]{:S(2)}) copy-start(bf16[1,196,768]{2,1,0:T(8,128)(2,1)} %copy-done.49) | copy-start | bytes 903172
  164.8 60.0 %copy-start.62 = (bf16[1,196,768]{2,1,0:T(8,128)(2,1)S(1)}, bf16[1,196,768]{2,1,0:T(8,128)(2,1)}, u32[]{:S(2)}) copy-start(bf16[1,196,768]{2,1,0:T(8,128)(2,1)} %copy-done.61) | copy-start | bytes 903172
  164.8 60.0 %copy-start.67 = (bf16[1,196,768]{2,1,0:T(8,128)(2,1)S(1)}, bf16[1,196,768]{2,1,0:T(8,128)(2,1)}, u32[]{:S(2)}) copy-start(bf16[1,196,768]{2,1,0:T(8,128)(2,1)} %copy-done.66) | copy-start | bytes 903172
  164.8 60.0 %copy-start.139 = (f32[1,196]{1,0:T(1,128)S(1)}, f32[1,196]{1,0:T(1,128)}, u32[]{:S(2)}) copy-start(f32[1,196]{1,0:T(1,128)} %get-tuple-element.1427) | copy-start | bytes 2356
  168.1 142.5 %collective-permute-start.2 = (bf16[1,196,768]{2,1,0:T(8,128)(2,1)}, bf16[1,196,768]{2,1,0:T(8,128)(2,1)}, u32[]{:S(2)}, u32[]{:S(2)}) collective-permute-start(bf16[1,196,768]{2,1,0:T(8,128)(2,1)} %fusion.332), channel_id=1, source_target_pairs={{0,16},{1,17},{2,18},{3,19},{4,20},{5,21},{6,22},{7,23},{8,24},{9,... | collective-permute-start | bytes 903176 | tf_op jit(solution)/shard_map/ppermute | solution.py:20
  300.7 65.4 %collective-permute-start.4 = (bf16[1,196,768]{2,1,0:T(8,128)(2,1)}, bf16[1,196,768]{2,1,0:T(8,128)(2,1)}, u32[]{:S(2)}, u32[]{:S(2)}) collective-permute-start(bf16[1,196,768]{2,1,0:T(8,128)(2,1)} %get-tuple-element.1341), channel_id=1, source_target_pairs={{16,0},{17,1},{18,2},{19,3},{20,4},{21,5},{22,6},{23,7},{24,8},{25... | collective-permute-start | bytes 903176 | tf_op jit(solution)/shard_map/ppermute | solution.py:20
  323.3 22.4 %copy-start.9 = (f32[1,196,768]{2,1,0:T(8,128)}, f32[1,196,768]{2,1,0:T(8,128)S(1)}, u32[]{:S(2)}) copy-start(f32[1,196,768]{2,1,0:T(8,128)S(1)} %get-tuple-element.1516) | copy-start | bytes 1806340 | tf_op jit(solution)/shard_map/cond
  400.7 11.8 %collective-permute-start.5 = (bf16[1,196,768]{2,1,0:T(8,128)(2,1)S(1)}, bf16[1,196,768]{2,1,0:T(8,128)(2,1)S(1)}, u32[]{:S(2)}, u32[]{:S(2)}) collective-permute-start(bf16[1,196,768]{2,1,0:T(8,128)(2,1)S(1)} %get-tuple-element.1343), channel_id=1, source_target_pairs={{16,0},{17,1},{18,2},{19,3},{20,4},{21,5},{22,6},{23,7},{24,8},{25... | collective-permute-start | bytes 903176 | tf_op jit(solution)/shard_map/ppermute | solution.py:20
  453.5 23.4 %copy-start.41 = (bf16[196,768]{0,1:T(8,128)(2,1)S(1)}, bf16[196,768]{0,1:T(8,128)(2,1)}, u32[]{:S(2)}) copy-start(bf16[196,768]{0,1:T(8,128)(2,1)} %get-tuple-element.983) | copy-start | bytes 903172
  481.5 157.9 %reduce-scatter.5.cloned.1.call-start = ((), (), s32[]{:S(2)}) async-start(), calls=%async_computation.4 | async-start | bytes 7520256 | tf_op jit(solution)/shard_map/reduce_scatter | solution.py:389
  492.9 262.1 %reduce-scatter.9.cloned.1.call-start = ((), (), s32[]{:S(2)}) async-start(), calls=%async_computation.8 | async-start | bytes 10027008 | tf_op jit(solution)/shard_map/reduce_scatter | solution.py:396
  509.0 362.2 %reduce-scatter.11.cloned.1.call-start = ((), (), s32[]{:S(2)}) async-start(), calls=%async_computation.10 | async-start | bytes 10027008 | tf_op jit(solution)/shard_map/reduce_scatter | solution.py:398
  525.7 347.4 %copy-start.137 = (s32[3,196]{1,0:T(4,128)S(1)}, s32[3,196]{1,0:T(4,128)}, u32[]{:S(2)}) copy-start(s32[3,196]{1,0:T(4,128)} %param.35) | copy-start | bytes 7060
  525.7 350.7 %copy-start.183 = (u32[32]{0:T(128)S(1)}, u32[32]{0:T(128)}, u32[]{:S(2)}) copy-start(u32[32]{0:T(128)} %constant.1143) | copy-start | bytes 388
  525.7 356.3 %copy-start.13 = (bf16[196,768]{1,0:T(8,128)(2,1)S(1)}, bf16[196,768]{1,0:T(8,128)(2,1)}, u32[]{:S(2)}) copy-start(bf16[196,768]{1,0:T(8,128)(2,1)} %get-tuple-element.1340) | copy-start | bytes 903172
  525.7 509.3 %all-gather.7.cloned.1.call-start = ((), (), s32[]{:S(2)}) async-start(), calls=%async_computation.7 | async-start | bytes 1253376 | tf_op jit(solution)/shard_map/all_gather | solution.py:418
  546.7 491.1 %all-gather.5.cloned.1.call-start = ((), (), s32[]{:S(2)}) async-start(), calls=%async_computation.5 | async-start | bytes 3760128 | tf_op jit(solution)/shard_map/all_gather | solution.py:409
  641.1 402.2 %all-gather.9.cloned.1.call-start = ((), (), s32[]{:S(2)}) async-start(), calls=%async_computation.9 | async-start | bytes 5013504 | tf_op jit(solution)/shard_map/all_gather | solution.py:430
  756.8 314.5 %all-gather.11.cloned.1.call-start = ((), (), s32[]{:S(2)}) async-start(), calls=%async_computation.11 | async-start | bytes 5013504 | tf_op jit(solution)/shard_map/all_gather | solution.py:436
  887.9 143.7 %copy-start.184 = (bf16[196]{0:T(256)(128)(2,1)S(1)}, bf16[196]{0:T(256)(128)(2,1)}, u32[]{:S(2)}) copy-start(bf16[196]{0:T(256)(128)(2,1)} %get-tuple-element.1294) | copy-start | bytes 1180
  889.2 144.6 %copy-start.127 = (bf16[1,196,768]{2,1,0:T(8,128)(2,1)S(1)}, bf16[1,196,768]{2,1,0:T(8,128)(2,1)}, u32[]{:S(2)}) copy-start(bf16[1,196,768]{2,1,0:T(8,128)(2,1)} %copy-done.126) | copy-start | bytes 903172
  (167 other events, 872.6 us)
Sparse Core Ops, SparseCore 0:
  481.6 63.4 reduce-scatter.6
  550.2 89.0 reduce-scatter.4
  644.1 110.8 reduce-scatter.8
  760.1 111.1 reduce-scatter.10
  873.9 38.1 all-gather.6
  914.9 46.4 all-gather.4
  964.2 52.8 all-gather.8
  1019.3 51.9 all-gather.10
where the time goes:
time: 1090 us
  waiting for transfers between devices  369 us (34%)
  matrix products  250 us (23%)
  other arithmetic  145 us (13%)
  blocking collectives  120 us (11%)
  local copies, waits for them, and re-layouts  112 us (10%)
  starting transfers between devices  67 us (6%)
  between operations  19.5 us (2%)
    unnamed x2, blocking collectives  120 us
    reduce_scatter x1, waiting for transfers between devices, shards(): lax.psum_scatter(grad_totals[11], ('dp', 'rep'), scatter_dimension=0, til...  114 us
    reduce_scatter x1, waiting for transfers between devices, shards(): lax.psum_scatter(grad_totals[9], ('dp', 'rep'), scatter_dimension=0, tile...  114 us
    reduce_scatter x1, waiting for transfers between devices, shards(): lax.psum_scatter(grad_totals[2], ('dp', 'rep'), scatter_dimension=0, tile...  92.6 us
    ppermute x6, starting transfers between devices, from_behind(): return lax.ppermute(value, axis, pairs)  66.4 us
    dot_general x5, matrix products, forward(): jnp.dot(normed_two, w_up, preferred_element_type=jnp.float32)  39.6 us
    another operation x40, local copies, waits for them, and re-layouts  36.1 us
    dot_general x3, matrix products, back_input(): jnp.einsum('bro,io->bri', grad_branch_two, w_down, preferred_element_type...  27.7 us
  transfers between devices with their start and end apart: 14, of which 6 were waited for; matrix products, arithmetic and copies ran while one was open for 28% of the time, Pallas kernels for 0%

commit v1 on v0

v1 whole, which is shorter than its diff:
```python
from functools import partial
import math

import jax
import jax.numpy as jnp
from jax import lax
from jax.experimental import pallas as pl
from jax.experimental.pallas import tpu as pltpu
from jax.sharding import PartitionSpec as P

HEAD_DIM = 64
PAIR = 2 * HEAD_DIM
ROW_TILE = 16
COLUMNS = 256

norm_eps = 1e-06
masked_score = -1e30
f32 = jnp.float32
bf16 = jnp.bfloat16

NN = (((1,), (0,)), ((), ()))
NT = (((1,), (1,)), ((), ()))
TN = (((0,), (0,)), ((), ()))

GAIN_ONE, SHIFT_ONE, BIAS_QUERY, BIAS_VALUE, BIAS_OUT, GAIN_TWO, SHIFT_TWO, BIAS_DOWN, BIAS_UP = range(9)


def product(left, right, dims):
    return lax.dot_general(left, right, dims, preferred_element_type=f32)


def spans(size, step):
    return [slice(at, min(at + step, size)) for at in range(0, size, step)]


def column_sum(values):
    return jnp.sum(values, axis=0, keepdims=True)


def centre(values):
    centred = values - jnp.mean(values, axis=-1, keepdims=True)
    scale = lax.rsqrt(jnp.mean(centred * centred, axis=-1, keepdims=True) + norm_eps)
    return centred * scale, scale


class Fetch:
    def __init__(self, first, pairs, sem):
        self.first = first
        self.copies = {
            name: pltpu.make_async_copy(source, target, sem.at[at])
            for at, (name, source, target) in enumerate(pairs)
        }

    def start(self):
        @pl.when(self.first)
        def _():
            for copy in self.copies.values():
                copy.start()

    def wait(self, name):
        copy = self.copies.pop(name, None)
        if copy is not None:

            @pl.when(self.first)
            def _():
                copy.wait()


def row_mask(shape, count):
    return lax.broadcasted_iota(jnp.int32, shape, 0) < count


def gather_matrix(index_ref, count):
    slots = index_ref.shape[-1]
    padded = -(-slots // ROW_TILE) * ROW_TILE
    shape = (padded, slots)
    patch = lax.broadcasted_iota(jnp.int32, shape, 0)
    slot = lax.broadcasted_iota(jnp.int32, shape, 1)
    chosen = jnp.broadcast_to(index_ref[...], shape) == patch
    return jnp.where(chosen & (slot < count), 1.0, 0.0).astype(bf16)


def forward_part(r, fetch, vec, weights, count):
    rows, width = r["u"].shape[-2:]
    hidden = weights["up"].shape[1]
    for span in spans(rows, ROW_TILE):
        normal, _ = centre(r["u"][span, :].astype(f32))
        r["a"][span, :] = (normal * vec(GAIN_ONE) + vec(SHIFT_ONE)).astype(bf16)
    fetch.wait("qkv")
    for span in spans(3 * width, COLUMNS):
        packed = product(r["a"][...], weights["qkv"][:, span], NN)
        if span.start < width:
            packed = packed + vec(BIAS_QUERY, span)
        elif span.start >= 2 * width:
            packed = packed + vec(BIAS_VALUE, slice(span.start - 2 * width, span.stop - 2 * width))
        r["qkv"][:, span] = packed.astype(bf16)
    low = (lax.broadcasted_iota(jnp.int32, (1, PAIR), 1) < HEAD_DIM).astype(bf16)
    lane = lax.broadcasted_iota(jnp.int32, (rows, PAIR), 1) < HEAD_DIM
    for at in range(0, width, PAIR):
        query = r["qkv"][:, at : at + PAIR]
        key = r["qkv"][:, width + at : width + at + PAIR]
        value = r["qkv"][:, 2 * width + at : 2 * width + at + PAIR]
        both = jnp.concatenate([query * low, query * (1 - low)], axis=0)
        scores = product(both, key, NT) * (1.0 / math.sqrt(HEAD_DIM))
        live = lax.broadcasted_iota(jnp.int32, scores.shape, 1) < count
        scores = jnp.where(live, scores, masked_score)
        powers = jnp.exp(scores - jnp.max(scores, axis=-1, keepdims=True))
        chance = powers * (1.0 / jnp.sum(powers, axis=-1, keepdims=True))
        mixed = product(chance.astype(bf16), value, NN)
        r["o"][:, at : at + PAIR] = jnp.where(lane, mixed[:rows], mixed[rows:]).astype(bf16)
    fetch.wait("out")
    for span in spans(width, COLUMNS):
        r["r"][:, span] = r["u"][:, span].astype(f32) + (
            product(r["o"][...], weights["out"][:, span], NN) + vec(BIAS_OUT, span)
        )
    for span in spans(rows, ROW_TILE):
        normal, _ = centre(r["r"][span, :])
        r["c"][span, :] = (normal * vec(GAIN_TWO) + vec(SHIFT_TWO)).astype(bf16)
    fetch.wait("up")
    for span in spans(hidden, COLUMNS):
        z = product(r["c"][...], weights["up"][:, span], NN) + vec(BIAS_UP, span)
        share = 0.5 * (1.0 + lax.erf(z * math.sqrt(0.5)))
        r["m"][:, span] = (z * share).astype(bf16)
        if r.get("slope") is not None:
            r["slope"][:, span] = share + z * (jnp.exp(-0.5 * z * z) * (1.0 / math.sqrt(2 * math.pi)))
    fetch.wait("down")
    outer = r["y"].shape[-2]
    for span in spans(width, COLUMNS):
        y = r["r"][:, span] + (product(r["m"][...], weights["down"][:, span], NN) + vec(BIAS_DOWN, span))
        y = jnp.where(row_mask(y.shape, count), y, 0.0)
        r["y"][:, span] = y.astype(bf16)[:outer]


def norm_back(normal, scale, gain, grad):
    x = grad * gain
    return scale * (
        x - jnp.mean(x, axis=-1, keepdims=True) - normal * jnp.mean(x * normal, axis=-1, keepdims=True)
    )


def backward_part(r, fetch, vec, weights, count, add):
    rows, width = r["u"].shape[-2:]
    hidden = weights["up"].shape[1]
    for span in spans(rows, ROW_TILE):
        live = lax.broadcasted_iota(jnp.int32, (ROW_TILE, width), 0) + span.start < count
        r["gd"][span, :] = jnp.where(live, r["e"][span, :], jnp.zeros((), bf16))
    add(BIAS_DOWN, lambda: column_sum(r["gd"][...].astype(f32)))
    fetch.wait("down")
    for span in spans(hidden, COLUMNS):
        gz = product(r["gd"][...], weights["down"][span, :], NT) * r["slope"][:, span]
        r["gz"][:, span] = gz.astype(bf16)
        add(BIAS_UP, lambda: column_sum(r["gz"][:, span].astype(f32)), span)
    fetch.wait("up")
    for span in spans(width, COLUMNS):
        r["gr"][:, span] = product(r["gz"][...], weights["up"][span, :], NT)
    gain_sum, shift_sum = 0.0, 0.0
    for span in spans(rows, ROW_TILE):
        normal, scale = centre(r["r"][span, :])
        gc = r["gr"][span, :]
        gain_sum, shift_sum = gain_sum + gc * normal, shift_sum + gc
        gr = r["gd"][span, :].astype(f32) + norm_back(normal, scale, vec(GAIN_TWO), gc)
        r["gr"][span, :] = gr
        r["gb"][span, :] = gr.astype(bf16)
    add(GAIN_TWO, lambda: column_sum(gain_sum))
    add(SHIFT_TWO, lambda: column_sum(shift_sum))
    add(BIAS_OUT, lambda: column_sum(r["gb"][...].astype(f32)))
    fetch.wait("out")
    for span in spans(width, COLUMNS):
        r["go"][:, span] = product(r["gb"][...], weights["out"][span, :], NT).astype(bf16)
    low = (lax.broadcasted_iota(jnp.int32, (1, PAIR), 1) < HEAD_DIM).astype(bf16)
    lane = lax.broadcasted_iota(jnp.int32, (rows, PAIR), 1) < HEAD_DIM
    score_scale = 1.0 / math.sqrt(HEAD_DIM)
    live = row_mask((rows, rows), count)
    for at in range(0, width, PAIR):
        query = r["qkv"][:, at : at + PAIR]
        key = r["qkv"][:, width + at : width + at + PAIR]
        value = r["qkv"][:, 2 * width + at : 2 * width + at + PAIR]
        go = r["go"][:, at : at + PAIR]
        scores = product(jnp.concatenate([key * low, key * (1 - low)], axis=0), query, NT) * score_scale
        grads = product(jnp.concatenate([value * low, value * (1 - low)], axis=0), go, NT)
        chances, inner = [], []
        for head in range(2):
            score = jnp.where(live, scores[head * rows : (head + 1) * rows], masked_score)
            powers = jnp.exp(score - jnp.max(score, axis=0, keepdims=True))
            chance = powers * (1.0 / jnp.sum(powers, axis=0, keepdims=True))
            gp = grads[head * rows : (head + 1) * rows]
            gs = chance * (gp - jnp.sum(gp * chance, axis=0, keepdims=True))
            chances.append(chance.astype(bf16))
            inner.append(jnp.where(live, gs, 0.0).astype(bf16))
        gw = product(jnp.concatenate(chances, axis=0), go, NN)
        gk = product(jnp.concatenate(inner, axis=0), query, NN) * score_scale
        gq = [product(gs, key, TN) * score_scale for gs in inner]
        r["gqkv"][:, at : at + PAIR] = jnp.where(lane, gq[0], gq[1]).astype(bf16)
        r["gqkv"][:, width + at : width + at + PAIR] = jnp.where(lane, gk[:rows], gk[rows:]).astype(bf16)
        r["gqkv"][:, 2 * width + at : 2 * width + at + PAIR] = jnp.where(lane, gw[:rows], gw[rows:]).astype(
            bf16
        )
    add(BIAS_QUERY, lambda: column_sum(r["gqkv"][:, :width].astype(f32)))
    add(BIAS_VALUE, lambda: column_sum(r["gqkv"][:, 2 * width :].astype(f32)))
    fetch.wait("qkv")
    for span in spans(width, COLUMNS):
        r["ga"][:, span] = product(r["gqkv"][...], weights["qkv"][span, :], NT)
    gain_sum, shift_sum = 0.0, 0.0
    for span in spans(rows, ROW_TILE):
        normal, scale = centre(r["u"][span, :].astype(f32))
        ga = r["ga"][span, :]
        gain_sum, shift_sum = gain_sum + ga * normal, shift_sum + ga
        gu = r["gr"][span, :] + norm_back(normal, scale, vec(GAIN_ONE), ga)
        r["gu"][span, :] = gu.astype(bf16)
    add(GAIN_ONE, lambda: column_sum(gain_sum))
    add(SHIFT_ONE, lambda: column_sum(shift_sum))


def vector_reader(ref):
    def vec(row, span=None):
        width = ref.shape[1]
        if span is None:
            return ref[row : row + 1, :]
        at = row + span.start // width
        start = span.start % width
        return ref[at : at + 1, start : start + span.stop - span.start]

    return vec


def vector_adder(ref):
    def add(row, values, span=None):
        width = ref.shape[1]
        values = values()
        at, start = row, 0
        if span is not None:
            at, start = row + span.start // width, span.start % width
        ref[at : at + 1, start : start + values.shape[1]] += values

    return add


def pad_rows(target, source):
    inner, rows = source.shape[0], target.shape[0]
    target[:inner, :] = source[...]
    if rows > inner:
        target[inner:, :] = jnp.zeros((rows - inner, target.shape[1]), target.dtype)


WEIGHTS = ("qkv", "out", "up", "down")
ANY = pl.BlockSpec(memory_space=pl.ANY)


def image_block(shape):
    return pl.BlockSpec((pl.Squeezed(),) + tuple(shape), lambda i, *_: (i, 0, 0))


def fixed_block(shape):
    return pl.BlockSpec(tuple(shape), lambda i, *_: (0,) * len(shape))


def weight_scratch(weights):
    return [pltpu.VMEM(weight.shape, weight.dtype) for weight in weights] + [
        pltpu.SemaphoreType.DMA((len(weights),))
    ]


def call(kernel, images, scalars, ins, in_specs, outs, out_specs, scratch, flops, name):
    return pl.pallas_call(
        kernel,
        out_shape=outs,
        grid_spec=pltpu.PrefetchScalarGridSpec(
            num_scalar_prefetch=1,
            grid=(images,),
            in_specs=in_specs,
            out_specs=out_specs,
            scratch_shapes=scratch,
        ),
        compiler_params=pltpu.CompilerParams(
            dimension_semantics=("arbitrary",), vmem_limit_bytes=60 << 20
        ),
        cost_estimate=pl.CostEstimate(flops=flops, bytes_accessed=flops // 300, transcendentals=0),
        name=name,
    )(scalars, *ins)


def first_forward(scalars, index, source, vectors, weights):
    images, slots, width = source.shape
    rows = -(-slots // ROW_TILE) * ROW_TILE
    hidden = weights[2].shape[1]

    def kernel(scalar_ref, index_ref, source_ref, vec_ref, *rest):
        hbm, (u_ref, y_ref), rest = rest[:4], rest[4:6], rest[6:]
        local, sem, rest = rest[:4], rest[4], rest[5:]
        padded, a_ref, qkv_ref, o_ref, r_ref, c_ref, m_ref = rest
        image = pl.program_id(0)
        fetch = Fetch(image == 0, list(zip(WEIGHTS, hbm, local)), sem)
        fetch.start()
        count = scalar_ref[1 + image]
        pad_rows(padded, source_ref)
        chosen = gather_matrix(index_ref, count)
        gathered = product(chosen, padded[...], TN)
        u_ref[:slots, :] = gathered.astype(bf16)
        u_ref[slots:, :] = jnp.zeros((rows - slots, width), bf16)
        refs = dict(u=u_ref, a=a_ref, qkv=qkv_ref, o=o_ref, r=r_ref, c=c_ref, m=m_ref, y=y_ref)
        forward_part(refs, fetch, vector_reader(vec_ref), dict(zip(WEIGHTS, local)), count)

    return call(
        kernel,
        images,
        scalars,
        (index, source, vectors) + weights,
        [image_block((1, slots)), image_block((slots, width)), fixed_block(vectors.shape)] + [ANY] * 4,
        [
            jax.ShapeDtypeStruct((images, rows, width), bf16),
            jax.ShapeDtypeStruct((images, slots, width), bf16),
        ],
        [image_block((rows, width)), image_block((slots, width))],
        weight_scratch(weights)
        + [
            pltpu.VMEM((rows, width), bf16),
            pltpu.VMEM((rows, width), bf16),
            pltpu.VMEM((rows, 3 * width), bf16),
            pltpu.VMEM((rows, width), bf16),
            pltpu.VMEM((rows, width), f32),
            pltpu.VMEM((rows, width), bf16),
            pltpu.VMEM((rows, hidden), bf16),
        ],
        images * 2 * rows * 12 * width * width,
        "first_forward",
    )


def whole_layer(scalars, kept, received, cotangent, vectors, weights):
    images, rows, width = kept.shape
    slots = cotangent.shape[1]
    hidden = weights[2].shape[1]
    saved = [
        ((rows, width), bf16),
        ((rows, width), bf16),
        ((rows, 3 * width), bf16),
        ((rows, width), bf16),
        ((rows, width), f32),
        ((rows, width), bf16),
        ((rows, hidden), bf16),
        ((rows, hidden), f32),
        ((slots, width), bf16),
        ((slots, width), bf16),
    ]

    def kernel(scalar_ref, kept_ref, received_ref, e_ref, vec_ref, *rest):
        hbm, outs, rest = rest[:4], rest[4:14], rest[14:]
        local, sem, rest = rest[:4], rest[4], rest[5:]
        e_pad, gd_ref, gz_ref, gb_ref, gr_ref, go_ref, gqkv_ref, ga_ref, gu_pad = rest
        u_ref, a_ref, qkv_ref, o_ref, r_ref, c_ref, m_ref, slope_ref, y_ref, gu_ref = outs
        image = pl.program_id(0)
        fetch = Fetch(image == 0, list(zip(WEIGHTS, hbm, local)), sem)
        fetch.start()
        count = scalar_ref[1 + image]

        @pl.when(scalar_ref[0] == 0)
        def _():
            u_ref[...] = kept_ref[...]

        @pl.when(scalar_ref[0] != 0)
        def _():
            pad_rows(u_ref, received_ref)

        pad_rows(e_pad, e_ref)
        refs = dict(
            u=u_ref, a=a_ref, qkv=qkv_ref, o=o_ref, r=r_ref, c=c_ref, m=m_ref, slope=slope_ref, y=y_ref,
            e=e_pad, gd=gd_ref, gz=gz_ref, gb=gb_ref, gr=gr_ref, go=go_ref, gqkv=gqkv_ref, ga=ga_ref,
            gu=gu_pad,
        )
        vec = vector_reader(vec_ref)
        near = dict(zip(WEIGHTS, local))
        forward_part(refs, fetch, vec, near, count)
        backward_part(refs, fetch, vec, near, count, lambda row, values, span=None: None)
        gu_ref[...] = gu_pad[:slots, :]

    return call(
        kernel,
        images,
        scalars,
        (kept, received, cotangent, vectors) + weights,
        [
            image_block((rows, width)),
            image_block((slots, width)),
            image_block((slots, width)),
            fixed_block(vectors.shape),
        ]
        + [ANY] * 4,
        [jax.ShapeDtypeStruct((images,) + shape, dtype) for shape, dtype in saved],
        [image_block(shape) for shape, _ in saved],
        weight_scratch(weights)
        + [
            pltpu.VMEM((rows, width), bf16),
            pltpu.VMEM((rows, width), bf16),
            pltpu.VMEM((rows, hidden), bf16),
            pltpu.VMEM((rows, width), bf16),
            pltpu.VMEM((rows, width), f32),
            pltpu.VMEM((rows, width), bf16),
            pltpu.VMEM((rows, 3 * width), bf16),
            pltpu.VMEM((rows, width), f32),
            pltpu.VMEM((rows, width), bf16),
        ],
        images * 4 * rows * 12 * width * width,
        "whole_layer",
    )


def layer_backward(scalars, index, u, qkv, r, slope, cotangent, received, vectors, weights):
    images, rows, width = u.shape
    slots = cotangent.shape[1]
    hidden = weights[2].shape[1]
    made = [
        ((rows, width), bf16),
        ((rows, hidden), bf16),
        ((rows, width), bf16),
        ((rows, 3 * width), bf16),
        ((slots, width), bf16),
    ]
    lines = vectors.shape[0]

    def kernel(scalar_ref, index_ref, u_ref, qkv_ref, r_ref, slope_ref, e_ref, received_ref, vec_ref, *rest):
        hbm, outs, rest = rest[:4], rest[4:10], rest[10:]
        local, sem, rest = rest[:4], rest[4], rest[5:]
        gd_ref, gz_ref, gb_ref, gqkv_ref, grad_ref, sums_ref = outs
        e_pad, gr_ref, go_ref, ga_ref, gu_ref = rest
        image = pl.program_id(0)
        order = ("down", "up", "out", "qkv")
        found = dict(zip(WEIGHTS, zip(hbm, local)))
        fetch = Fetch(image == 0, [(name,) + found[name] for name in order], sem)
        fetch.start()
        count = scalar_ref[1 + image]
        early = scalar_ref[0] == 0

        @pl.when(image == 0)
        def _():
            sums_ref[...] = jnp.zeros(sums_ref.shape, f32)

        @pl.when(early)
        def _():
            pad_rows(e_pad, received_ref)

        @pl.when(jnp.logical_not(early))
        def _():
            pad_rows(e_pad, e_ref)

        refs = dict(
            u=u_ref, qkv=qkv_ref, r=r_ref, slope=slope_ref, e=e_pad, gd=gd_ref, gz=gz_ref, gb=gb_ref,
            gr=gr_ref, go=go_ref, gqkv=gqkv_ref, ga=ga_ref, gu=gu_ref,
        )
        near = dict(zip(WEIGHTS, local))
        backward_part(refs, fetch, vector_reader(vec_ref), near, count, vector_adder(sums_ref))

        @pl.when(early)
        def _():
            chosen = gather_matrix(index_ref, count)
            grad_ref[...] = product(chosen, gu_ref[:slots, :], NN)[:slots, :].astype(bf16)

        @pl.when(jnp.logical_not(early))
        def _():
            grad_ref[...] = gu_ref[:slots, :]

    return call(
        kernel,
        images,
        scalars,
        (index, u, qkv, r, slope, cotangent, received, vectors) + weights,
        [
            image_block((1, slots)),
            image_block((rows, width)),
            image_block((rows, 3 * width)),
            image_block((rows, width)),
            image_block((rows, hidden)),
            image_block((slots, width)),
            image_block((slots, width)),
            fixed_block(vectors.shape),
        ]
        + [ANY] * 4,
        [jax.ShapeDtypeStruct((images,) + shape, dtype) for shape, dtype in made]
        + [jax.ShapeDtypeStruct((lines, width), f32)],
        [image_block(shape) for shape, _ in made] + [fixed_block((lines, width))],
        weight_scratch(weights)
        + [
            pltpu.VMEM((rows, width), bf16),
            pltpu.VMEM((rows, width), f32),
            pltpu.VMEM((rows, width), bf16),
            pltpu.VMEM((rows, width), f32),
            pltpu.VMEM((rows, width), bf16),
        ],
        images * 2 * rows * 12 * width * width,
        "layer_backward",
    )


def weight_gradient(side, sources, name):
    depth = sources[0][0].shape[0]
    width = min(min(left.shape[1], right.shape[1]) for left, right in sources)
    starts = [0]
    for left, right in sources:
        starts.append(starts[-1] + max(left.shape[1], right.shape[1]) // width)
    blocks = starts[-1]
    half = blocks // 2

    def chosen(i, scalar_ref):
        bit = scalar_ref[0]
        return jnp.where(i < half, (1 - bit) * half + i, bit * half + i - half)

    def kernel(scalar_ref, *refs):
        send_ref, keep_ref = refs[-2:]
        step = pl.program_id(0)
        block = chosen(step, scalar_ref)
        for at in range(len(sources)):
            left_ref, right_ref = refs[2 * at : 2 * at + 2]

            @pl.when((block >= starts[at]) & (block < starts[at + 1]) & (step < half))
            def _():
                for span in spans(width, COLUMNS):
                    send_ref[:, span] = product(left_ref[...], right_ref[:, span], TN).astype(bf16)

            @pl.when((block >= starts[at]) & (block < starts[at + 1]) & (step >= half))
            def _():
                for span in spans(width, COLUMNS):
                    keep_ref[:, span] = product(left_ref[...], right_ref[:, span], TN)

    def column_block(array, first, last):
        if array.shape[1] == width:
            return pl.BlockSpec((depth, width), lambda i, s: (0, 0))
        return pl.BlockSpec(
            (depth, width), lambda i, s: (0, jnp.clip(chosen(i, s), first, last - 1) - first)
        )

    out = (half, width, width)
    square = (pl.Squeezed(), width, width)
    return call(
        kernel,
        blocks,
        side,
        [array for source in sources for array in source],
        [
            column_block(array, starts[at], starts[at + 1])
            for at, source in enumerate(sources)
            for array in source
        ],
        [jax.ShapeDtypeStruct(out, bf16), jax.ShapeDtypeStruct(out, f32)],
        [
            pl.BlockSpec(square, lambda i, s: (jnp.minimum(i, half - 1), 0, 0)),
            pl.BlockSpec(square, lambda i, s: (jnp.maximum(i - half, 0), 0, 0)),
        ],
        [],
        2 * depth * width * width * blocks,
        name,
    )


def swapped(value, axis, stride):
    length = lax.axis_size(axis)
    return lax.ppermute(value, axis, [(i, i ^ stride) for i in range(length)])


def bit_of(axis, stride):
    return (lax.axis_index(axis) // stride) % 2


def halved(pair, bit):
    height = pair.shape[0] // 2
    send = lax.dynamic_slice_in_dim(pair, (1 - bit) * height, height, axis=0).astype(bf16)
    keep = lax.dynamic_slice_in_dim(pair, bit * height, height, axis=0)
    return send, keep


def joined(mine, other, bit):
    first = bit == 0
    return jnp.concatenate([jnp.where(first, mine, other), jnp.where(first, other, mine)], axis=0)


def strides_of(size):
    return [1 << at for at in range(size.bit_length() - 1)]


def reduce_blocks(send, keep, total):
    width = send.shape[-1]
    send, keep = send.reshape(-1, width), keep.reshape(-1, width)
    value = keep + swapped(send, "rep", 1).astype(f32)
    strides = strides_of(lax.axis_size("dp"))
    for stride in strides:
        send, keep = halved(value, bit_of("dp", stride))
        value = keep + swapped(send, "dp", stride).astype(f32)
    value = (value / total).astype(bf16)
    for stride in reversed(strides):
        value = joined(value, swapped(value, "dp", stride), bit_of("dp", stride))
    return value, swapped(value, "rep", 1)


def reduce_vectors(value):
    value = value + swapped(value, "rep", 1)
    for stride in strides_of(lax.axis_size("dp")):
        value = value + swapped(value, "dp", stride)
    return value


def shards(
    boundary,
    keep_index,
    keep_count,
    gain_one,
    shift_one,
    w_qkv,
    bias_query,
    bias_value,
    w_out,
    bias_out,
    gain_two,
    shift_two,
    w_up,
    bias_up,
    w_down,
    bias_down,
):
    images, slots = keep_index.shape
    width = boundary.shape[-1]
    weights = (w_qkv[0], w_out[0], w_up[0], w_down[0])
    hidden = weights[2].shape[1]
    small = (gain_one, shift_one, bias_query, bias_value, bias_out, gain_two, shift_two, bias_down)
    used = len(small) + hidden // width
    vectors = jnp.concatenate(
        [jnp.concatenate(small, axis=0), bias_up.reshape(-1, width), jnp.zeros((-used % 8, width), bf16)], axis=0
    ).astype(f32)
    section = lax.axis_index("section").astype(jnp.int32)
    scalars = jnp.concatenate([section[None], keep_count])
    index = keep_index[:, None, :]
    rows_in = boundary[0]

    kept, output = first_forward(scalars, index, rows_in, vectors, weights)
    received = lax.ppermute(output, "section", [(0, 1)])
    u, a, qkv, o, r, c, m, slope, output, grad_first = whole_layer(
        scalars, kept, received, rows_in, vectors, weights
    )
    returned = lax.ppermute(grad_first, "section", [(1, 0)])
    gd, gz, gb, gqkv, grad_rows, sums = layer_backward(
        scalars, index, u, qkv, r, slope, rows_in, returned, vectors, weights
    )

    def flat(array):
        return array.reshape(-1, array.shape[-1])

    total = images * lax.axis_size(("dp", "rep"))
    rep = lax.axis_index("rep")
    side = rep.astype(jnp.int32)[None]
    grads = (
        weight_gradient(side, [(flat(m), flat(gd))], "grad_down"),
        weight_gradient(side, [(flat(c), flat(gz))], "grad_up"),
        weight_gradient(side, [(flat(a), flat(gqkv)), (flat(o), flat(gb))], "grad_attention"),
    )
    down, up, attention = [
        joined(mine, other, rep).astype(f32).reshape(-1, width, width)
        for mine, other in (reduce_blocks(send, keep, total) for send, keep in grads)
    ]
    sums = reduce_vectors(sums) / total

    def across(blocks):
        return jnp.transpose(blocks, (1, 0, 2)).reshape(width, -1)

    return (
        output[None],
        grad_rows[None],
        sums[GAIN_ONE][None],
        sums[SHIFT_ONE][None],
        across(attention[:3])[None],
        sums[BIAS_QUERY][None],
        sums[BIAS_VALUE][None],
        attention[3][None],
        sums[BIAS_OUT][None],
        sums[GAIN_TWO][None],
        sums[SHIFT_TWO][None],
        across(up)[None],
        sums[BIAS_UP : BIAS_UP + hidden // width].reshape(1, -1),
        down.reshape(1, -1, width),
        sums[BIAS_DOWN][None],
    )


def solution(mesh):
    per_image = ("dp", "rep")
    matrix, line = P("section", None, None), P("section", None)
    rows = P("section", per_image, None, None)
    kinds = (line, line, matrix, line, line, matrix, line, line, line, matrix, line, matrix, line)
    return jax.shard_map(
        shards,
        mesh=mesh,
        in_specs=(rows, P(per_image, None), P(per_image)) + kinds,
        out_specs=(rows, rows) + kinds,
        check_vma=False,
    )
```

time: 1090 us -> 514 us (0.47)
  matrix products: 250 us -> 0 us
  waiting for transfers between devices: 369 us -> 214 us
  Pallas kernels: 0 us -> 139 us
  blocking collectives: 120 us -> 0 us
  other arithmetic: 145 us -> 52.3 us
  local copies, waits for them, and re-layouts: 112 us -> 56.8 us
  starting transfers between devices: 67 us -> 41.3 us
  between operations: 19.5 us -> 1.43 us
    reduce_scatter x4 -> x0, waiting for transfers between devices: 340 us -> none  [the longest x1 114 us: shards(): lax.psum_scatter(grad_totals[11], ('dp', 'rep'), scatter_dimension=0, til...]
    dot_general x65 -> x0, matrix products: 236 us -> none  [the longest x5 39.6 us: forward(): jnp.dot(normed_two, w_up, preferred_element_type=jnp.float32)]
    ppermute x6 -> x30, waiting for transfers between devices: 8.37 us -> 214 us  [the longest x28 172 us: swapped(): return lax.ppermute(value, axis, [(i, i ^ stride) for i in range(length)])]
    pallas_call x0 -> x6, Pallas kernels: none -> 139 us  [call(): pl.pallas_call(kernel, out_shape=outs, grid_spec=pltpu.PrefetchScalarGrid...]
    unnamed x2 -> x0, blocking collectives: 120 us -> none
    convert_element_type x77 -> x6, other arithmetic: 47.7 us -> 6.07 us  [the longest x2 5.22 us: shards(): joined(mine, other, rep).astype(f32).reshape(-1, width, width)]
    reduce_sum x49 -> x0, other arithmetic: 32.3 us -> none  [the longest x16 7.7 us: layer_norm(): variance = jnp.mean(centred * centred, axis=-1, keepdims=True)]
    broadcast_in_dim x7 -> x0, other arithmetic: 25.3 us -> none  [the longest x5 23.3 us: shards(): grad[None]]
  transfers between devices with their start and end apart: 14 -> 30, of which waited for: 6 -> 15; matrix products, arithmetic and copies ran while one was open for 28% -> 18% of each run, Pallas kernels for 0% -> 3%
where the time goes in v1:
time: 514 us; the launch traced here: 505 us
  waiting for transfers between devices  214 us (42%)
  Pallas kernels  139 us (27%)
  local copies, waits for them, and re-layouts  56.8 us (11%)
  other arithmetic  52.3 us (10%)
  starting transfers between devices  41.3 us (8%)
    ppermute x28, waiting for transfers between devices, swapped(): return lax.ppermute(value, axis, [(i, i ^ stride) for i in range(length)])  172 us
    pallas_call x6, Pallas kernels, call(): pl.pallas_call(kernel, out_shape=outs, grid_spec=pltpu.PrefetchScalarGrid...  139 us
    ppermute x28, starting transfers between devices, swapped(): return lax.ppermute(value, axis, [(i, i ^ stride) for i in range(length)])  35.1 us
    another operation x2, local copies, waits for them, and re-layouts, shards(): across(up)[None]  25.7 us
    ppermute x1, waiting for transfers between devices, shards(): returned = lax.ppermute(grad_first, 'section', [(1, 0)])  22.1 us
    ppermute x1, waiting for transfers between devices, shards(): received = lax.ppermute(output, 'section', [(0, 1)])  19.9 us
    unnamed x55, local copies, waits for them, and re-layouts  15.1 us
    select_n x11, other arithmetic, joined(): jnp.where(first, mine, other)  11.2 us
  transfers between devices with their start and end apart: 30, of which 15 were waited for; matrix products, arithmetic and copies ran while one was open for 18% of the time, Pallas kernels for 3%

profile of v1, /device:TPU:0, one launch (start us, length us, event | category | flops | bytes accessed | tf_op | source)
XLA Modules:
  0.0 505.0 jit_solution(687273229011855006)
XLA Ops:
  5.4 25.6 %first_forward.1 = (bf16[3,208,768]{2,1,0:T(8,128)(2,1)}, bf16[3,196,768]{2,1,0:T(8,128)(2,1)}) custom-call(s32[4]{0:T(128)} %pad_add_fusion.scalar_ref, s32[3,1,196]{2,1,0:T(1,128)} %broadcast_in_dim.19.index_ref, bf16[3,196,768]{2,1,0:T(8,128)(2,1)} %bitcast.67, f32[16,768]{1,0:T(8,128)} %convert_element_type.93.vec_ref, bf16[768,2304]{1,0:T(8,128)(2,1)} %bitcast.58, ...), custom_call_target="tpu_custom_call" | custom-call | flops 8833204224 | bytes 29444014 | tf_op jit(solution)/shard_map/first_forward/pallas_call | solution.py:264
  31.0 4.9 collective-permute-start
  36.0 19.9 %collective-permute-done.received_ref = bf16[3,196,768]{2,1,0:T(8,128)(2,1)S(1)} collective-permute-done((bf16[3,196,768]{2,1,0:T(8,128)(2,1)}, bf16[3,196,768]{2,1,0:T(8,128)(2,1)S(1)}, u32[]{:S(2)}, u32[]{:S(2)}) %collective-permute-start) | collective-permute-done | bytes 903200 | tf_op jit(solution)/shard_map/ppermute | solution.py:632
  56.8 50.4 %whole_layer.1 = (bf16[3,208,768]{2,1,0:T(8,128)(2,1)}, bf16[3,208,768]{2,1,0:T(8,128)(2,1)}, bf16[3,208,2304]{2,1,0:T(8,128)(2,1)}, bf16[3,208,768]{2,1,0:T(8,1...) custom-call(s32[4]{0:T(128)} %pad_add_fusion.scalar_ref, ...), custom_call_target="tpu_custom_call" | custom-call | flops 17666408448 | bytes 58888028 | tf_op jit(solution)/shard_map/whole_layer/pallas_call | solution.py:264
  108.5 22.1 %collective-permute-done.1.received_ref = bf16[3,196,768]{2,1,0:T(8,128)(2,1)S(1)} collective-permute-done((bf16[3,196,768]{2,1,0:T(8,128)(2,1)}, bf16[3,196,768]{2,1,0:T(8,128)(2,1)S(1)}, u32[]{:S(2)}, u32[]{:S(2)}) %collective-permute-start.1) | collective-permute-done | bytes 903200 | tf_op jit(solution)/shard_map/ppermute | solution.py:636
  131.6 37.1 %layer_backward.1 = (bf16[3,208,768]{2,1,0:T(8,128)(2,1)}, bf16[3,208,3072]{2,1,0:T(8,128)(2,1)}, bf16[3,208,768]{2,1,0:T(8,128)(2,1)}, bf16[3,208,2304]{2,1,0:T...) custom-call(s32[4]{0:T(128)} %pad_add_fusion.scalar_ref, s32[3,1,196]{2,1,0:T(1,128)} %broadcast_in_dim.19.index_ref, ...), custom_call_target="tpu_custom_call" | custom-call | flops 8833204224 | bytes 29444014 | tf_op jit(solution)/shard_map/layer_backward/pallas_call | solution.py:264
  168.7 9.1 %grad_attention.1 = (bf16[2,768,768]{2,1,0:T(8,128)(2,1)}, f32[2,768,768]{2,1,0:T(8,128)}) custom-call(s32[1]{0:T(128)} %bitcast.8.scalar_ref, bf16[624,768]{1,0:T(8,128)(2,1)} %bitcast.74, bf16[624,2304]{1,0:T(8,128)(2,1)} %bitcast.72, bf16[624,768]{1,0:T(8,128)(2,1)} %bitcast.75, bf16[624,768]{1,0:T(8,128)(2,1)} %bitcast.77), custom_call_target="tpu_custom_call" | custom-call | flops 2944401408 | bytes 9814671 | tf_op jit(solution)/shard_map/grad_attention/pallas_call | solution.py:264
  177.7 8.4 %grad_up.1 = (bf16[2,768,768]{2,1,0:T(8,128)(2,1)}, f32[2,768,768]{2,1,0:T(8,128)}) custom-call(s32[1]{0:T(128)} %bitcast.8.scalar_ref, bf16[624,768]{1,0:T(8,128)(2,1)} %bitcast.73, bf16[624,3072]{1,0:T(8,128)(2,1)} %bitcast.71), custom_call_target="tpu_custom_call" | custom-call | flops 2944401408 | bytes 9814671 | tf_op jit(solution)/shard_map/grad_up/pallas_call | solution.py:264
  186.6 8.5 %grad_down.1 = (bf16[2,768,768]{2,1,0:T(8,128)(2,1)}, f32[2,768,768]{2,1,0:T(8,128)}) custom-call(s32[1]{0:T(128)} %bitcast.8.scalar_ref, bf16[624,3072]{1,0:T(8,128)(2,1)} %bitcast.70, bf16[624,768]{1,0:T(8,128)(2,1)} %bitcast.76), custom_call_target="tpu_custom_call" | custom-call | flops 2944401408 | bytes 9814671 | tf_op jit(solution)/shard_map/grad_down/pallas_call | solution.py:264
  195.3 3.7 bitcast_add_fusion.2
  209.8 18.3 %collective-permute-done.7 = bf16[768,768]{1,0:T(8,128)(2,1)} collective-permute-done((bf16[768,768]{1,0:T(8,128)(2,1)S(1)}, bf16[768,768]{1,0:T(8,128)(2,1)}, u32[]{:S(2)}, u32[]{:S(2)}) %collective-permute-start.7) | collective-permute-done | bytes 1179680 | tf_op jit(solution)/shard_map/ppermute | solution.py:555
  232.1 21.3 %collective-permute-done.15 = bf16[768,768]{1,0:T(8,128)(2,1)} collective-permute-done((bf16[768,768]{1,0:T(8,128)(2,1)}, bf16[768,768]{1,0:T(8,128)(2,1)}, u32[]{:S(2)}, u32[]{:S(2)}) %collective-permute-start.15) | collective-permute-done | bytes 1179680 | tf_op jit(solution)/shard_map/ppermute | solution.py:555
  256.7 21.4 %collective-permute-done.23 = bf16[768,768]{1,0:T(8,128)(2,1)S(1)} collective-permute-done((bf16[768,768]{1,0:T(8,128)(2,1)S(1)}, bf16[768,768]{1,0:T(8,128)(2,1)S(1)}, u32[]{:S(2)}, u32[]{:S(2)}) %collective-permute-start.23) | collective-permute-done | bytes 1179680 | tf_op jit(solution)/shard_map/ppermute | solution.py:555
  281.8 20.1 %collective-permute-done.9 = bf16[192,768]{1,0:T(8,128)(2,1)S(1)} collective-permute-done((bf16[192,768]{1,0:T(8,128)(2,1)S(1)}, bf16[192,768]{1,0:T(8,128)(2,1)S(1)}, u32[]{:S(2)}, u32[]{:S(2)}) %collective-permute-start.9) | collective-permute-done | bytes 294944 | tf_op jit(solution)/shard_map/ppermute | solution.py:555
  305.2 9.5 %collective-permute-done.17 = bf16[192,768]{1,0:T(8,128)(2,1)S(1)} collective-permute-done((bf16[192,768]{1,0:T(8,128)(2,1)S(1)}, bf16[192,768]{1,0:T(8,128)(2,1)S(1)}, u32[]{:S(2)}, u32[]{:S(2)}) %collective-permute-start.17) | collective-permute-done | bytes 294944 | tf_op jit(solution)/shard_map/ppermute | solution.py:555
  314.8 6.2 %collective-permute-done.10 = bf16[192,768]{1,0:T(8,128)(2,1)S(1)} collective-permute-done((bf16[192,768]{1,0:T(8,128)(2,1)S(1)}, bf16[192,768]{1,0:T(8,128)(2,1)S(1)}, u32[]{:S(2)}, u32[]{:S(2)}) %collective-permute-start.10) | collective-permute-done | bytes 294944 | tf_op jit(solution)/shard_map/ppermute | solution.py:555
  321.8 11.9 %collective-permute-done.24 = bf16[384,768]{1,0:T(8,128)(2,1)S(1)} collective-permute-done((bf16[384,768]{1,0:T(8,128)(2,1)S(1)}, bf16[384,768]{1,0:T(8,128)(2,1)S(1)}, u32[]{:S(2)}, u32[]{:S(2)}) %collective-permute-start.24) | collective-permute-done | bytes 589856 | tf_op jit(solution)/shard_map/ppermute | solution.py:555
  333.9 3.8 collective-permute-start.25
  340.4 12.3 %collective-permute-done.11 = bf16[384,768]{1,0:T(8,128)(2,1)S(1)} collective-permute-done((bf16[384,768]{1,0:T(8,128)(2,1)S(1)}, bf16[384,768]{1,0:T(8,128)(2,1)S(1)}, u32[]{:S(2)}, u32[]{:S(2)}) %collective-permute-start.11) | collective-permute-done | bytes 589856 | tf_op jit(solution)/shard_map/ppermute | solution.py:555
  355.6 3.9 collective-permute-start.26
  361.8 19.4 %collective-permute-done.3 = f32[16,768]{1,0:T(8,128)} collective-permute-done((f32[16,768]{1,0:T(8,128)}, f32[16,768]{1,0:T(8,128)}, u32[]{:S(2)}, u32[]{:S(2)}) %collective-permute-start.3) | collective-permute-done | bytes 49184 | tf_op jit(solution)/shard_map/ppermute | solution.py:555
  392.8 4.3 collective-permute-start.5
  397.1 3.3 collective-permute-done.27
  402.4 11.0 %collective-permute-done.20 = bf16[768,768]{1,0:T(8,128)(2,1)} collective-permute-done((bf16[768,768]{1,0:T(8,128)(2,1)}, bf16[768,768]{1,0:T(8,128)(2,1)}, u32[]{:S(2)}, u32[]{:S(2)}) %collective-permute-start.20) | collective-permute-done | bytes 1179680 | tf_op jit(solution)/shard_map/ppermute | solution.py:555
  418.4 16.1 %collective-permute-done.28 = bf16[768,768]{1,0:T(8,128)(2,1)S(1)} collective-permute-done((bf16[768,768]{1,0:T(8,128)(2,1)S(1)}, bf16[768,768]{1,0:T(8,128)(2,1)S(1)}, u32[]{:S(2)}, u32[]{:S(2)}) %collective-permute-start.28) | collective-permute-done | bytes 1179680 | tf_op jit(solution)/shard_map/ppermute | solution.py:555
  441.5 3.4 slice.54
  444.9 8.0 %copy.35 = f32[768,3,768]{0,2,1:T(8,128)} copy(f32[768,3,768]{2,0,1:T(8,128)} %bitcast.44) | data formatting | bytes 14155776 | tf_op jit(solution)/shard_map/transpose | solution.py:659
  453.0 8.3 %copy.37 = f32[1,768,2304]{2,1,0:T(8,128)} copy(f32[1,768,2304]{1,2,0:T(8,128)} %bitcast.45) | data formatting | bytes 14155776
  464.4 4.6 convert_bitcast_fusion
  469.0 13.4 %copy.36 = f32[768,4,768]{2,1,0:T(4,128)} copy(f32[768,4,768]{2,0,1:T(8,128)} %convert_bitcast_fusion) | data formatting | bytes 18874368 | tf_op jit(solution)/shard_map/broadcast_in_dim;reshape | solution.py:673
  482.4 12.3 %reshape.130 = f32[1,768,3072]{2,1,0:T(8,128)} reshape(f32[768,4,768]{2,1,0:T(4,128)} %copy.36) | data formatting | bytes 18874368 | tf_op jit(solution)/shard_map/broadcast_in_dim;reshape | solution.py:673
  500.3 4.5 maximum_convert_fusion.1
  (154 shorter events, 76.6 us)
Async XLA Ops:
  31.0 24.8 %collective-permute-start = (bf16[3,196,768]{2,1,0:T(8,128)(2,1)}, bf16[3,196,768]{2,1,0:T(8,128)(2,1)S(1)}, u32[]{:S(2)}, u32[]{:S(2)}) collective-permute-start(bf16[3,196,768]{2,1,0:T(8,128)(2,1)} %get-tuple-element.40), channel_id=1, source_target_pairs={{0,16},{1,17},{2,18},{3,19},{4,20},{5,21},{6,22},{7,23},{8,24},{9,... | collective-permute-start | bytes 2709512 | tf_op jit(solution)/shard_map/ppermute | solution.py:632
  107.2 23.4 %collective-permute-start.1 = (bf16[3,196,768]{2,1,0:T(8,128)(2,1)}, bf16[3,196,768]{2,1,0:T(8,128)(2,1)S(1)}, u32[]{:S(2)}, u32[]{:S(2)}) collective-permute-start(bf16[3,196,768]{2,1,0:T(8,128)(2,1)} %get-tuple-element.46), channel_id=1, source_target_pairs={{16,0},{17,1},{18,2},{19,3},{20,4},{21,5},{22,6},{23,7},{24,8},{25... | collective-permute-start | bytes 2709512 | tf_op jit(solution)/shard_map/ppermute | solution.py:636
  177.7 17.6 %collective-permute-start.6 = (bf16[1536,768]{1,0:T(8,128)(2,1)}, bf16[1536,768]{1,0:T(8,128)(2,1)}, u32[]{:S(2)}, u32[]{:S(2)}) collective-permute-start(bf16[1536,768]{1,0:T(8,128)(2,1)} %bitcast.63), channel_id=1, source_target_pairs={{0,1},{1,0},{2,3},{3,2},{4,5},{5,4},{6,7},{7,6},{8,9},{9,8},{10,11... | collective-permute-start | bytes 7077896 | tf_op jit(solution)/shard_map/ppermute | solution.py:555
  186.2 14.6 %collective-permute-start.14 = (bf16[1536,768]{1,0:T(8,128)(2,1)}, bf16[1536,768]{1,0:T(8,128)(2,1)}, u32[]{:S(2)}, u32[]{:S(2)}) collective-permute-start(bf16[1536,768]{1,0:T(8,128)(2,1)} %bitcast.62), channel_id=1, source_target_pairs={{0,1},{1,0},{2,3},{3,2},{4,5},{5,4},{6,7},{7,6},{8,9},{9,8},{10,11... | collective-permute-start | bytes 7077896 | tf_op jit(solution)/shard_map/ppermute | solution.py:555
  195.2 11.2 %collective-permute-start.22 = (bf16[1536,768]{1,0:T(8,128)(2,1)}, bf16[1536,768]{1,0:T(8,128)(2,1)S(1)}, u32[]{:S(2)}, u32[]{:S(2)}) collective-permute-start(bf16[1536,768]{1,0:T(8,128)(2,1)} %bitcast.61), channel_id=1, source_target_pairs={{0,1},{1,0},{2,3},{3,2},{4,5},{5,4},{6,7},{7,6},{8,9},{9,8},{10,11... | collective-permute-start | bytes 7077896 | tf_op jit(solution)/shard_map/ppermute | solution.py:555
  199.2 28.9 %collective-permute-start.7 = (bf16[768,768]{1,0:T(8,128)(2,1)S(1)}, bf16[768,768]{1,0:T(8,128)(2,1)}, u32[]{:S(2)}, u32[]{:S(2)}) collective-permute-start(bf16[768,768]{1,0:T(8,128)(2,1)S(1)} %dynamic-slice_convert_fusion.2), channel_id=1, source_target_pairs={{0,2},{2,0},{4,6},{6,4},{8,10},{10,8},{12,14},{14,12},{1,3},{3,1},... | collective-permute-start | bytes 3538952 | tf_op jit(solution)/shard_map/ppermute | solution.py:555
  204.9 48.5 %collective-permute-start.15 = (bf16[768,768]{1,0:T(8,128)(2,1)}, bf16[768,768]{1,0:T(8,128)(2,1)}, u32[]{:S(2)}, u32[]{:S(2)}) collective-permute-start(bf16[768,768]{1,0:T(8,128)(2,1)} %dynamic-slice_convert_fusion.1), channel_id=1, source_target_pairs={{0,2},{2,0},{4,6},{6,4},{8,10},{10,8},{12,14},{14,12},{1,3},{3,1},... | collective-permute-start | bytes 3538952 | tf_op jit(solution)/shard_map/ppermute | solution.py:555
  209.2 68.9 %collective-permute-start.23 = (bf16[768,768]{1,0:T(8,128)(2,1)S(1)}, bf16[768,768]{1,0:T(8,128)(2,1)S(1)}, u32[]{:S(2)}, u32[]{:S(2)}) collective-permute-start(bf16[768,768]{1,0:T(8,128)(2,1)S(1)} %dynamic-slice_convert_fusion), channel_id=1, source_target_pairs={{0,2},{2,0},{4,6},{6,4},{8,10},{10,8},{12,14},{14,12},{1,3},{3,1},... | collective-permute-start | bytes 3538952 | tf_op jit(solution)/shard_map/ppermute | solution.py:555
  209.8 43.6 %copy-start.3 = (f32[1536,768]{1,0:T(8,128)S(1)}, f32[1536,768]{1,0:T(8,128)}, u32[]{:S(2)}) copy-start(f32[1536,768]{1,0:T(8,128)} %copy-done.2) | copy-start | bytes 14155780
  230.5 47.7 %copy-start.5 = (f32[1536,768]{1,0:T(8,128)S(1)}, f32[1536,768]{1,0:T(8,128)}, u32[]{:S(2)}) copy-start(f32[1536,768]{1,0:T(8,128)} %copy-done.4) | copy-start | bytes 14155780
  230.5 47.9 %collective-permute-start.8 = (bf16[384,768]{1,0:T(8,128)(2,1)S(1)}, bf16[384,768]{1,0:T(8,128)(2,1)S(1)}, u32[]{:S(2)}, u32[]{:S(2)}) collective-permute-start(bf16[384,768]{1,0:T(8,128)(2,1)S(1)} %dynamic-slice_convert_fusion.5), channel_id=1, source_target_pairs={{0,4},{2,6},{4,0},{6,2},{8,12},{10,14},{12,8},{14,10},{1,5},{3,7},... | collective-permute-start | bytes 1769480 | tf_op jit(solution)/shard_map/ppermute | solution.py:555
  255.1 26.1 %collective-permute-start.16 = (bf16[384,768]{1,0:T(8,128)(2,1)S(1)}, bf16[384,768]{1,0:T(8,128)(2,1)S(1)}, u32[]{:S(2)}, u32[]{:S(2)}) collective-permute-start(bf16[384,768]{1,0:T(8,128)(2,1)S(1)} %dynamic-slice_convert_fusion.4), channel_id=1, source_target_pairs={{0,4},{2,6},{4,0},{6,2},{8,12},{10,14},{12,8},{14,10},{1,5},{3,7},... | collective-permute-start | bytes 1769480 | tf_op jit(solution)/shard_map/ppermute | solution.py:555
  278.6 23.3 %collective-permute-start.9 = (bf16[192,768]{1,0:T(8,128)(2,1)S(1)}, bf16[192,768]{1,0:T(8,128)(2,1)S(1)}, u32[]{:S(2)}, u32[]{:S(2)}) collective-permute-start(bf16[192,768]{1,0:T(8,128)(2,1)S(1)} %dynamic-slice_convert_fusion.8), channel_id=1, source_target_pairs={{0,8},{2,10},{4,12},{6,14},{8,0},{10,2},{12,4},{14,6},{1,9},{3,11}... | collective-permute-start | bytes 884744 | tf_op jit(solution)/shard_map/ppermute | solution.py:555
  281.4 33.3 %collective-permute-start.17 = (bf16[192,768]{1,0:T(8,128)(2,1)S(1)}, bf16[192,768]{1,0:T(8,128)(2,1)S(1)}, u32[]{:S(2)}, u32[]{:S(2)}) collective-permute-start(bf16[192,768]{1,0:T(8,128)(2,1)S(1)} %dynamic-slice_convert_fusion.7), channel_id=1, source_target_pairs={{0,8},{2,10},{4,12},{6,14},{8,0},{10,2},{12,4},{14,6},{1,9},{3,11}... | collective-permute-start | bytes 884744 | tf_op jit(solution)/shard_map/ppermute | solution.py:555
  302.0 19.0 %collective-permute-start.10 = (bf16[192,768]{1,0:T(8,128)(2,1)S(1)}, bf16[192,768]{1,0:T(8,128)(2,1)S(1)}, u32[]{:S(2)}, u32[]{:S(2)}) collective-permute-start(bf16[192,768]{1,0:T(8,128)(2,1)S(1)} %multiply_convert_fusion.2), channel_id=1, source_target_pairs={{0,8},{2,10},{4,12},{6,14},{8,0},{10,2},{12,4},{14,6},{1,9},{3,11}... | collective-permute-start | bytes 884744 | tf_op jit(solution)/shard_map/ppermute | solution.py:555
  302.2 31.6 %collective-permute-start.24 = (bf16[384,768]{1,0:T(8,128)(2,1)S(1)}, bf16[384,768]{1,0:T(8,128)(2,1)S(1)}, u32[]{:S(2)}, u32[]{:S(2)}) collective-permute-start(bf16[384,768]{1,0:T(8,128)(2,1)S(1)} %dynamic-slice_convert_fusion.3), channel_id=1, source_target_pairs={{0,4},{2,6},{4,0},{6,2},{8,12},{10,14},{12,8},{14,10},{1,5},{3,7},... | collective-permute-start | bytes 1769480 | tf_op jit(solution)/shard_map/ppermute | solution.py:555
  314.7 23.0 %collective-permute-start.18 = (bf16[192,768]{1,0:T(8,128)(2,1)S(1)}, bf16[192,768]{1,0:T(8,128)(2,1)S(1)}, u32[]{:S(2)}, u32[]{:S(2)}) collective-permute-start(bf16[192,768]{1,0:T(8,128)(2,1)S(1)} %multiply_convert_fusion.1), channel_id=1, source_target_pairs={{0,8},{2,10},{4,12},{6,14},{8,0},{10,2},{12,4},{14,6},{1,9},{3,11}... | collective-permute-start | bytes 884744 | tf_op jit(solution)/shard_map/ppermute | solution.py:555
  321.1 31.6 %collective-permute-start.11 = (bf16[384,768]{1,0:T(8,128)(2,1)S(1)}, bf16[384,768]{1,0:T(8,128)(2,1)S(1)}, u32[]{:S(2)}, u32[]{:S(2)}) collective-permute-start(bf16[384,768]{1,0:T(8,128)(2,1)S(1)} %pad_maximum_fusion.7), channel_id=1, source_target_pairs={{0,4},{2,6},{4,0},{6,2},{8,12},{10,14},{12,8},{14,10},{1,5},{3,7},... | collective-permute-start | bytes 1769480 | tf_op jit(solution)/shard_map/ppermute | solution.py:555
  333.9 21.6 %collective-permute-start.25 = (bf16[192,768]{1,0:T(8,128)(2,1)S(1)}, bf16[192,768]{1,0:T(8,128)(2,1)S(1)}, u32[]{:S(2)}, u32[]{:S(2)}) collective-permute-start(bf16[192,768]{1,0:T(8,128)(2,1)S(1)} %dynamic-slice_convert_fusion.6), channel_id=1, source_target_pairs={{0,8},{2,10},{4,12},{6,14},{8,0},{10,2},{12,4},{14,6},{1,9},{3,11}... | collective-permute-start | bytes 884744 | tf_op jit(solution)/shard_map/ppermute | solution.py:555
  337.8 45.0 %collective-permute-start.19 = (bf16[384,768]{1,0:T(8,128)(2,1)S(1)}, bf16[384,768]{1,0:T(8,128)(2,1)S(1)}, u32[]{:S(2)}, u32[]{:S(2)}) collective-permute-start(bf16[384,768]{1,0:T(8,128)(2,1)S(1)} %pad_maximum_fusion.8), channel_id=1, source_target_pairs={{0,4},{2,6},{4,0},{6,2},{8,12},{10,14},{12,8},{14,10},{1,5},{3,7},... | collective-permute-start | bytes 1769480 | tf_op jit(solution)/shard_map/ppermute | solution.py:555
  354.0 34.5 %collective-permute-start.12 = (bf16[768,768]{1,0:T(8,128)(2,1)}, bf16[768,768]{1,0:T(8,128)(2,1)}, u32[]{:S(2)}, u32[]{:S(2)}) collective-permute-start(bf16[768,768]{1,0:T(8,128)(2,1)} %pad_maximum_fusion.4), channel_id=1, source_target_pairs={{0,2},{2,0},{4,6},{6,4},{8,10},{10,8},{12,14},{14,12},{1,3},{3,1},... | collective-permute-start | bytes 3538952 | tf_op jit(solution)/shard_map/ppermute | solution.py:555
  355.6 27.1 %collective-permute-start.26 = (bf16[192,768]{1,0:T(8,128)(2,1)S(1)}, bf16[192,768]{1,0:T(8,128)(2,1)S(1)}, u32[]{:S(2)}, u32[]{:S(2)}) collective-permute-start(bf16[192,768]{1,0:T(8,128)(2,1)S(1)} %multiply_convert_fusion), channel_id=1, source_target_pairs={{0,8},{2,10},{4,12},{6,14},{8,0},{10,2},{12,4},{14,6},{1,9},{3,11}... | collective-permute-start | bytes 884744 | tf_op jit(solution)/shard_map/ppermute | solution.py:555
  359.5 1.2 collective-permute-start.2
  361.4 19.9 %collective-permute-start.3 = (f32[16,768]{1,0:T(8,128)}, f32[16,768]{1,0:T(8,128)}, u32[]{:S(2)}, u32[]{:S(2)}) collective-permute-start(f32[16,768]{1,0:T(8,128)} %add.106), channel_id=1, source_target_pairs={{0,2},{2,0},{4,6},{6,4},{8,10},{10,8},{12,14},{14,12},{1,3},{3,1},... | collective-permute-start | bytes 147464 | tf_op jit(solution)/shard_map/ppermute | solution.py:555
  382.7 9.3 %collective-permute-start.4 = (f32[16,768]{1,0:T(8,128)}, f32[16,768]{1,0:T(8,128)}, u32[]{:S(2)}, u32[]{:S(2)}) collective-permute-start(f32[16,768]{1,0:T(8,128)} %add.107), channel_id=1, source_target_pairs={{0,4},{2,6},{4,0},{6,2},{8,12},{10,14},{12,8},{14,10},{1,5},{3,7},... | collective-permute-start | bytes 147464 | tf_op jit(solution)/shard_map/ppermute | solution.py:555
  384.1 29.2 %collective-permute-start.20 = (bf16[768,768]{1,0:T(8,128)(2,1)}, bf16[768,768]{1,0:T(8,128)(2,1)}, u32[]{:S(2)}, u32[]{:S(2)}) collective-permute-start(bf16[768,768]{1,0:T(8,128)(2,1)} %pad_maximum_fusion.5), channel_id=1, source_target_pairs={{0,2},{2,0},{4,6},{6,4},{8,10},{10,8},{12,14},{14,12},{1,3},{3,1},... | collective-permute-start | bytes 3538952 | tf_op jit(solution)/shard_map/ppermute | solution.py:555
  386.5 13.9 %collective-permute-start.27 = (bf16[384,768]{1,0:T(8,128)(2,1)}, bf16[384,768]{1,0:T(8,128)(2,1)}, u32[]{:S(2)}, u32[]{:S(2)}) collective-permute-start(bf16[384,768]{1,0:T(8,128)(2,1)} %pad_maximum_fusion.9), channel_id=1, source_target_pairs={{0,4},{2,6},{4,0},{6,2},{8,12},{10,14},{12,8},{14,10},{1,5},{3,7},... | collective-permute-start | bytes 1769480 | tf_op jit(solution)/shard_map/ppermute | solution.py:555
  392.0 45.3 %collective-permute-start.13 = (bf16[1536,768]{1,0:T(8,128)(2,1)}, bf16[1536,768]{1,0:T(8,128)(2,1)}, u32[]{:S(2)}, u32[]{:S(2)}) collective-permute-start(bf16[1536,768]{1,0:T(8,128)(2,1)} %pad_maximum_fusion.1), channel_id=1, source_target_pairs={{0,1},{1,0},{2,3},{3,2},{4,5},{5,4},{6,7},{7,6},{8,9},{9,8},{10,11... | collective-permute-start | bytes 7077896 | tf_op jit(solution)/shard_map/ppermute | solution.py:555
  392.8 24.3 %collective-permute-start.5 = (f32[16,768]{1,0:T(8,128)S(1)}, f32[16,768]{1,0:T(8,128)S(1)}, u32[]{:S(2)}, u32[]{:S(2)}) collective-permute-start(f32[16,768]{1,0:T(8,128)S(1)} %add.108), channel_id=1, source_target_pairs={{0,8},{2,10},{4,12},{6,14},{8,0},{10,2},{12,4},{14,6},{1,9},{3,11}... | collective-permute-start | bytes 147464 | tf_op jit(solution)/shard_map/ppermute | solution.py:555
  401.8 32.8 %collective-permute-start.28 = (bf16[768,768]{1,0:T(8,128)(2,1)S(1)}, bf16[768,768]{1,0:T(8,128)(2,1)S(1)}, u32[]{:S(2)}, u32[]{:S(2)}) collective-permute-start(bf16[768,768]{1,0:T(8,128)(2,1)S(1)} %pad_maximum_fusion.6), channel_id=1, source_target_pairs={{0,2},{2,0},{4,6},{6,4},{8,10},{10,8},{12,14},{14,12},{1,3},{3,1},... | collective-permute-start | bytes 3538952 | tf_op jit(solution)/shard_map/ppermute | solution.py:555
  417.2 44.1 %collective-permute-start.21 = (bf16[1536,768]{1,0:T(8,128)(2,1)}, bf16[1536,768]{1,0:T(8,128)(2,1)}, u32[]{:S(2)}, u32[]{:S(2)}) collective-permute-start(bf16[1536,768]{1,0:T(8,128)(2,1)} %pad_maximum_fusion.2), channel_id=1, source_target_pairs={{0,1},{1,0},{2,3},{3,2},{4,5},{5,4},{6,7},{7,6},{8,9},{9,8},{10,11... | collective-permute-start | bytes 7077896 | tf_op jit(solution)/shard_map/ppermute | solution.py:555
  437.3 60.4 %collective-permute-start.29 = (bf16[1536,768]{1,0:T(8,128)(2,1)}, bf16[1536,768]{1,0:T(8,128)(2,1)}, u32[]{:S(2)}, u32[]{:S(2)}) collective-permute-start(bf16[1536,768]{1,0:T(8,128)(2,1)} %pad_maximum_fusion.3), channel_id=1, source_target_pairs={{0,1},{1,0},{2,3},{3,2},{4,5},{5,4},{6,7},{7,6},{8,9},{9,8},{10,11... | collective-permute-start | bytes 7077896 | tf_op jit(solution)/shard_map/ppermute | solution.py:555
  (24 other events, 94.7 us)

commit v2 on v1

v2 whole, which is shorter than its diff:
```python
import functools
from functools import partial
import math

import jax
import jax.numpy as jnp
from jax import lax
from jax.experimental import pallas as pl
from jax.experimental.pallas import tpu as pltpu
from jax.sharding import PartitionSpec as P

HEAD_DIM = 64
PAIR = 2 * HEAD_DIM
ROW_TILE = 16
COLUMNS = 256

norm_eps = 1e-06
masked_score = -1e30
f32 = jnp.float32
bf16 = jnp.bfloat16

NN = (((1,), (0,)), ((), ()))
NT = (((1,), (1,)), ((), ()))
TN = (((0,), (0,)), ((), ()))

VECTORS = range(9)
GAIN_ONE, SHIFT_ONE, BIAS_QUERY, BIAS_VALUE, BIAS_OUT, GAIN_TWO, SHIFT_TWO, BIAS_DOWN, BIAS_UP = VECTORS
SECTION, DP, REP = "section", "dp", "rep"
U, A, QKV, O, R, C, M, SLOPE, GD, GZ, GB, GR, GO, GQKV, GA, GU, E, Y, GRAD = range(19)
WEIGHTS = range(19, 23)
W_QKV, W_OUT, W_UP, W_DOWN = WEIGHTS
DOWN, UP, QUERY_VALUE, KEY_OUT, SUMS, OUT = range(100, 106)
ORDER = "FAGFdAFUdAuQdqKudqkuqdkusdkquskqukqdksdqusqkuk"
COST = 10**11
ANY = pl.BlockSpec(memory_space=pl.ANY)


def product(left, right, dims):
    return lax.dot_general(left, right, dims, preferred_element_type=f32)


def spans(size, step):
    return [slice(at, min(at + step, size)) for at in range(0, size, step)]


def column_sum(values):
    return jnp.sum(values, axis=0, keepdims=True)


def centre(values):
    centred = values - jnp.mean(values, axis=-1, keepdims=True)
    scale = lax.rsqrt(jnp.mean(centred * centred, axis=-1, keepdims=True) + norm_eps)
    return centred * scale, scale


class Copies:
    def __init__(self, sem, pairs):
        self.made = {
            name: pltpu.make_async_copy(source, target, sem.at[at])
            for at, (name, (source, target)) in enumerate(pairs.items())
        }

    def start(self, *names):
        for name in names or tuple(self.made):
            if name in self.made:
                self.made[name].start()

    def wait(self, *names):
        for name in names or tuple(self.made):
            if name in self.made:
                self.made.pop(name).wait()


def first_section():
    return lax.axis_index(SECTION) == 0


def row_mask(shape, count):
    return lax.broadcasted_iota(jnp.int32, shape, 0) < count


def gather_matrix(slots_of, count):
    slots = slots_of.shape[1]
    shape = (-(-slots // ROW_TILE) * ROW_TILE, slots)
    patch = lax.broadcasted_iota(jnp.int32, shape, 0)
    slot = lax.broadcasted_iota(jnp.int32, shape, 1)
    chosen = jnp.broadcast_to(slots_of, shape) == patch
    return jnp.where(chosen & (slot < count), 1.0, 0.0).astype(bf16)


def forward_part(r, wait, done, vec, weights, count):
    rows, width = r[U].shape[-2:]
    hidden = weights[W_UP].shape[1]
    for span in spans(rows, ROW_TILE):
        normal, _ = centre(r[U][span, :].astype(f32))
        r[A][span, :] = (normal * vec(GAIN_ONE) + vec(SHIFT_ONE)).astype(bf16)
    done(U, A)
    wait(W_QKV)
    for span in spans(3 * width, COLUMNS):
        packed = product(r[A][...], weights[W_QKV][:, span], NN)
        if span.start < width:
            packed = packed + vec(BIAS_QUERY, span)
        elif span.start >= 2 * width:
            packed = packed + vec(BIAS_VALUE, slice(span.start - 2 * width, span.stop - 2 * width))
        r[QKV][:, span] = packed.astype(bf16)
    done(QKV)
    low = (lax.broadcasted_iota(jnp.int32, (1, PAIR), 1) < HEAD_DIM).astype(bf16)
    lane = lax.broadcasted_iota(jnp.int32, (rows, PAIR), 1) < HEAD_DIM
    for at in range(0, width, PAIR):
        query = r[QKV][:, at : at + PAIR]
        key = r[QKV][:, width + at : width + at + PAIR]
        value = r[QKV][:, 2 * width + at : 2 * width + at + PAIR]
        both = jnp.concatenate([query * low, query * (1 - low)], axis=0)
        scores = product(both, key, NT) * (1.0 / math.sqrt(HEAD_DIM))
        live = lax.broadcasted_iota(jnp.int32, scores.shape, 1) < count
        scores = jnp.where(live, scores, masked_score)
        powers = jnp.exp(scores - jnp.max(scores, axis=-1, keepdims=True))
        chance = powers * (1.0 / jnp.sum(powers, axis=-1, keepdims=True))
        mixed = product(chance.astype(bf16), value, NN)
        r[O][:, at : at + PAIR] = jnp.where(lane, mixed[:rows], mixed[rows:]).astype(bf16)
    done(O)
    wait(W_OUT)
    for span in spans(width, COLUMNS):
        r[R][:, span] = r[U][:, span].astype(f32) + (
            product(r[O][...], weights[W_OUT][:, span], NN) + vec(BIAS_OUT, span)
        )
    for span in spans(rows, ROW_TILE):
        normal, _ = centre(r[R][span, :])
        r[C][span, :] = (normal * vec(GAIN_TWO) + vec(SHIFT_TWO)).astype(bf16)
    done(R, C)
    wait(W_UP)
    for span in spans(hidden, COLUMNS):
        z = product(r[C][...], weights[W_UP][:, span], NN) + vec(BIAS_UP, span)
        share = 0.5 * (1.0 + lax.erf(z * math.sqrt(0.5)))
        r[M][:, span] = (z * share).astype(bf16)
        r[SLOPE][:, span] = share + z * (jnp.exp(-0.5 * z * z) * (1.0 / math.sqrt(2 * math.pi)))
    done(M, SLOPE)


def output_part(r, vec, weights, count):
    rows, width = r[R].shape
    outer = r[Y].shape[0]
    for span in spans(width, COLUMNS):
        y = r[R][:, span] + (product(r[M][...], weights[W_DOWN][:, span], NN) + vec(BIAS_DOWN, span))
        r[Y][:, span] = jnp.where(row_mask(y.shape, count), y, 0.0).astype(bf16)[:outer]


def norm_back(normal, scale, gain, grad):
    x = grad * gain
    return scale * (
        x - jnp.mean(x, axis=-1, keepdims=True) - normal * jnp.mean(x * normal, axis=-1, keepdims=True)
    )


def feed_forward_back(r, wait, done, vec, weights, count, add):
    rows, width = r[R].shape
    hidden = weights[W_UP].shape[1]
    for span in spans(rows, ROW_TILE):
        live = lax.broadcasted_iota(jnp.int32, (ROW_TILE, width), 0) + span.start < count
        r[GD][span, :] = jnp.where(live, r[E][span, :], jnp.zeros((), bf16))
    add(BIAS_DOWN, lambda: column_sum(r[GD][...].astype(f32)))
    wait(W_DOWN, SLOPE)
    for span in spans(hidden, COLUMNS):
        gz = product(r[GD][...], weights[W_DOWN][span, :], NT) * r[SLOPE][:, span]
        r[GZ][:, span] = gz.astype(bf16)
        add(BIAS_UP, lambda: column_sum(r[GZ][:, span].astype(f32)), span)
    done(GZ)
    wait(W_UP, R)
    for span in spans(width, COLUMNS):
        r[GR][:, span] = product(r[GZ][...], weights[W_UP][span, :], NT)
    gain_sum, shift_sum = 0.0, 0.0
    for span in spans(rows, ROW_TILE):
        normal, scale = centre(r[R][span, :])
        gc = r[GR][span, :]
        gain_sum, shift_sum = gain_sum + gc * normal, shift_sum + gc
        gr = r[GD][span, :].astype(f32) + norm_back(normal, scale, vec(GAIN_TWO), gc)
        r[GR][span, :] = gr
        r[GB][span, :] = gr.astype(bf16)
    done(GB, GR)
    add(GAIN_TWO, lambda: column_sum(gain_sum))
    add(SHIFT_TWO, lambda: column_sum(shift_sum))
    add(BIAS_OUT, lambda: column_sum(r[GB][...].astype(f32)))


def attention_back(r, wait, done, vec, weights, count, add):
    rows, width = r[U].shape
    wait(GB, W_OUT)
    for span in spans(width, COLUMNS):
        r[GO][:, span] = product(r[GB][...], weights[W_OUT][span, :], NT).astype(bf16)
    wait(QKV)
    low = (lax.broadcasted_iota(jnp.int32, (1, PAIR), 1) < HEAD_DIM).astype(bf16)
    lane = lax.broadcasted_iota(jnp.int32, (rows, PAIR), 1) < HEAD_DIM
    score_scale = 1.0 / math.sqrt(HEAD_DIM)
    live = row_mask((rows, rows), count)
    for at in range(0, width, PAIR):
        query = r[QKV][:, at : at + PAIR]
        key = r[QKV][:, width + at : width + at + PAIR]
        value = r[QKV][:, 2 * width + at : 2 * width + at + PAIR]
        go = r[GO][:, at : at + PAIR]
        scores = product(jnp.concatenate([key * low, key * (1 - low)], axis=0), query, NT) * score_scale
        grads = product(jnp.concatenate([value * low, value * (1 - low)], axis=0), go, NT)
        chances, inner = [], []
        for head in range(2):
            score = jnp.where(live, scores[head * rows : (head + 1) * rows], masked_score)
            powers = jnp.exp(score - jnp.max(score, axis=0, keepdims=True))
            chance = powers * (1.0 / jnp.sum(powers, axis=0, keepdims=True))
            gp = grads[head * rows : (head + 1) * rows]
            gs = chance * (gp - jnp.sum(gp * chance, axis=0, keepdims=True))
            chances.append(chance.astype(bf16))
            inner.append(jnp.where(live, gs, 0.0).astype(bf16))
        gw = product(jnp.concatenate(chances, axis=0), go, NN)
        gk = product(jnp.concatenate(inner, axis=0), query, NN) * score_scale
        gq = [product(gs, key, TN) * score_scale for gs in inner]
        r[GQKV][:, at : at + PAIR] = jnp.where(lane, gq[0], gq[1]).astype(bf16)
        r[GQKV][:, width + at : width + at + PAIR] = jnp.where(lane, gk[:rows], gk[rows:]).astype(bf16)
        r[GQKV][:, 2 * width + at : 2 * width + at + PAIR] = jnp.where(lane, gw[:rows], gw[rows:]).astype(
            bf16
        )
    done(GQKV)
    add(BIAS_QUERY, lambda: column_sum(r[GQKV][:, :width].astype(f32)))
    add(BIAS_VALUE, lambda: column_sum(r[GQKV][:, 2 * width :].astype(f32)))
    wait(W_QKV, U, GR)
    for span in spans(width, COLUMNS):
        r[GA][:, span] = product(r[GQKV][...], weights[W_QKV][span, :], NT)
    gain_sum, shift_sum = 0.0, 0.0
    for span in spans(rows, ROW_TILE):
        normal, scale = centre(r[U][span, :].astype(f32))
        ga = r[GA][span, :]
        gain_sum, shift_sum = gain_sum + ga * normal, shift_sum + ga
        gu = r[GR][span, :] + norm_back(normal, scale, vec(GAIN_ONE), ga)
        r[GU][span, :] = gu.astype(bf16)
    add(GAIN_ONE, lambda: column_sum(gain_sum))
    add(SHIFT_ONE, lambda: column_sum(shift_sum))


def vector_reader(refs):
    named = dict(zip(VECTORS, refs))

    def vec(name, span=None):
        ref = named[name]
        return (ref[...] if span is None else ref[:, span]).astype(f32)

    return vec


def vector_adder(ref):
    def add(name, values, span=None):
        values = values()
        start = 0 if span is None else span.start
        row, start = VECTORS.index(name) + start // ref.shape[1], start % ref.shape[1]
        ref[row : row + 1, start : start + values.shape[1]] += values

    return add


def pad_rows(target, source):
    inner, rows = source.shape[0], target.shape[0]
    target[:inner, :] = source[...]
    if rows > inner:
        target[inner:, :] = jnp.zeros((rows - inner, target.shape[1]), target.dtype)


def padded_rows(slots):
    return -(-slots // ROW_TILE) * ROW_TILE


def image_block(shape, image):
    return pl.BlockSpec((pl.Squeezed(),) + tuple(shape), lambda *_: (image, 0, 0))


def fixed_block(shape):
    return pl.BlockSpec(tuple(shape), lambda *_: (0,) * len(shape))


def weight_scratch(weights):
    return [pltpu.VMEM(weight.shape, weight.dtype) for weight in weights] + [
        pltpu.SemaphoreType.DMA((len(weights),))
    ]


def fetch_weights(sem, hbm, local, order=WEIGHTS):
    found = dict(zip(WEIGHTS, zip(hbm, local)))
    return Copies(sem, {name: found[name] for name in order}), dict(zip(WEIGHTS, local))


def call(kernel, steps, scalars, ins, in_specs, outs, out_specs, scratch, name, aliases=None):
    return pl.pallas_call(
        kernel,
        out_shape=outs,
        grid_spec=pltpu.PrefetchScalarGridSpec(
            num_scalar_prefetch=1,
            grid=(steps,),
            in_specs=in_specs,
            out_specs=out_specs,
            scratch_shapes=scratch,
        ),
        compiler_params=pltpu.CompilerParams(
            dimension_semantics=("arbitrary",), vmem_limit_bytes=60 << 20
        ),
        input_output_aliases=aliases or {},
        cost_estimate=pl.CostEstimate(flops=COST, bytes_accessed=COST, transcendentals=0),
        name=name,
    )(scalars, *ins)


def split(refs, *sizes):
    out, at = [], 0
    for size in sizes:
        out.append(refs[at] if size is None else refs[at : at + size])
        at += 1 if size is None else size
    assert at == len(refs)
    return out


def nothing(*_):
    return None


SAVED = (U, A, QKV, O, R, C, M, SLOPE)
MADE = (GZ, GB, GQKV, GRAD)


def image_shapes(slots, rows, width, hidden):
    narrow, wide = (rows, width), (rows, hidden)
    return {
        U: (narrow, bf16),
        A: (narrow, bf16),
        QKV: ((rows, 3 * width), bf16),
        O: (narrow, bf16),
        R: (narrow, f32),
        C: (narrow, bf16),
        M: (wide, bf16),
        SLOPE: (wide, f32),
        GD: (narrow, bf16),
        GZ: (wide, bf16),
        GB: (narrow, bf16),
        GR: (narrow, f32),
        GO: (narrow, bf16),
        GQKV: ((rows, 3 * width), bf16),
        GA: (narrow, f32),
        GU: (narrow, bf16),
        E: (narrow, bf16),
        Y: ((slots, width), bf16),
        GRAD: ((slots, width), bf16),
    }


def first_forward(image, carry, count, index, source, vectors, weights):
    images, slots, width = source.shape
    rows, hidden = padded_rows(slots), weights[2].shape[1]
    shapes = image_shapes(slots, rows, width, hidden)
    work = SAVED + (Y,)
    old = () if carry is None else tuple(carry)
    at = 1 + 2 + len(vectors) + 4

    def kernel(count_ref, index_ref, source_ref, *rest):
        vecs, hbm, _, places, y_ref, local, sem, scratch, padded, out_sem = split(
            rest, len(vectors), 4, len(old), len(work), None, 4, None, len(work), None, None
        )

        @pl.when(first_section())
        def _():
            fetch, near = fetch_weights(sem, hbm, local)
            fetch.start()
            kept = count_ref[image]
            refs = dict(zip(work, scratch))
            store = Copies(out_sem, {name: (refs[name], place.at[image]) for name, place in zip(work, places)})
            pad_rows(padded, source_ref)
            chosen = gather_matrix(index_ref[image : image + 1, :], kept)
            refs[U][:slots, :] = product(chosen, padded[...], TN).astype(bf16)
            refs[U][slots:, :] = jnp.zeros((rows - slots, width), bf16)
            vec = vector_reader(vecs)
            forward_part(refs, fetch.wait, store.start, vec, near, kept)
            fetch.wait(W_DOWN)
            output_part(refs, vec, near, kept)
            store.start(Y)
            y_ref[...] = refs[Y][...]
            store.wait()

    *carry, output = call(
        kernel,
        1,
        count,
        (index, source) + vectors + weights + old,
        [fixed_block(index.shape), image_block((slots, width), image)]
        + [fixed_block(vector.shape) for vector in vectors]
        + [ANY] * (4 + len(old)),
        [jax.ShapeDtypeStruct((images,) + shapes[name][0], shapes[name][1]) for name in work]
        + [jax.ShapeDtypeStruct((1, slots, width), bf16)],
        [ANY] * len(work) + [image_block((slots, width), 0)],
        weight_scratch(weights)
        + [pltpu.VMEM(*shapes[name]) for name in work]
        + [pltpu.VMEM((rows, width), bf16), pltpu.SemaphoreType.DMA((len(work),))],
        f"first_forward_{image}",
        {at + k: k for k in range(len(old))},
    )
    return carry, output


def middle(image, saved, made, sums, count, received, cotangent, vectors, weights):
    images, slots, width = cotangent.shape
    rows, hidden = padded_rows(slots), weights[2].shape[1]
    shapes = image_shapes(slots, rows, width, hidden)
    carry = SAVED + MADE
    lines = -(-(len(vectors) - 1 + hidden // width) // 8) * 8
    work = (E, GD, GR, GO, GA, GU) + carry
    old = tuple(saved) + (() if made is None else tuple(made) + (sums,))
    at = 1 + 2 + len(vectors) + 4

    def kernel(count_ref, received_ref, e_ref, *rest):
        vecs, hbm, previous, places, sums_ref, grad_ref, local, sem, scratch, out_sem = split(
            rest, len(vectors), 4, len(old), len(carry), None, None, 4, None, len(work), None
        )
        sums_ref[...] = jnp.zeros(sums_ref.shape, f32) if made is None else previous[-1][...]

        @pl.when(jnp.logical_not(first_section()))
        def _():
            fetch, near = fetch_weights(sem, hbm, local)
            fetch.start()
            live = count_ref[image]
            refs = dict(zip(work, scratch))
            store = Copies(
                out_sem, {name: (refs[name], place.at[image]) for name, place in zip(carry, places)}
            )
            pad_rows(refs[U], received_ref)
            pad_rows(refs[E], e_ref)
            vec, add = vector_reader(vecs), vector_adder(sums_ref)
            forward_part(refs, fetch.wait, store.start, vec, near, live)
            fetch.wait(W_DOWN)
            feed_forward_back(refs, nothing, store.start, vec, near, live, add)
            attention_back(refs, nothing, store.start, vec, near, live, add)
            refs[GRAD][...] = refs[GU][:slots, :]
            store.start(GRAD)
            grad_ref[...] = refs[GU][:slots, :]
            store.wait()

    results = call(
        kernel,
        1,
        count,
        (received, cotangent) + vectors + weights + old,
        [image_block((slots, width), 0), image_block((slots, width), image)]
        + [fixed_block(vector.shape) for vector in vectors]
        + [ANY] * (4 + len(old) - (made is not None))
        + ([] if made is None else [fixed_block(sums.shape)]),
        [jax.ShapeDtypeStruct((images,) + shapes[name][0], shapes[name][1]) for name in carry]
        + [jax.ShapeDtypeStruct((lines, width), f32), jax.ShapeDtypeStruct((1, slots, width), bf16)],
        [ANY] * len(carry) + [fixed_block((lines, width)), image_block((slots, width), 0)],
        weight_scratch(weights)
        + [pltpu.VMEM(*shapes[name]) for name in work]
        + [pltpu.SemaphoreType.DMA((len(carry),))],
        f"middle_{image}",
        {at + k: k for k in range(len(old))},
    )
    return results[: len(SAVED)], results[len(SAVED) : -2], results[-2], results[-1]


def late_feed_forward(image, saved, made, output, sums, count, received, vectors, weights):
    images, rows, hidden = saved[SAVED.index(M)].shape
    slots, width = received.shape[1:]
    shapes = image_shapes(slots, rows, width, hidden)
    loads = (SLOPE, R, M)
    stores = (GZ, GB, Y)
    work = (SLOPE, R, M, E, GD, GZ, GB, Y)
    near_names = (W_DOWN, W_UP)
    old = [made[MADE.index(GZ)], made[MADE.index(GB)], output, sums]
    at = 1 + 1 + len(vectors) + len(loads) + len(near_names)

    def kernel(count_ref, received_ref, *rest):
        vecs, sources, hbm, previous, places, sums_ref, gr_ref, local, scratch, sem = split(
            rest, len(vectors), len(loads), 2, len(old), len(stores), None, None, 2, len(work), None
        )
        live = count_ref[image]
        refs = dict(zip(work, scratch)) | {GR: gr_ref}
        near = dict(zip(near_names, local))
        far = dict(zip(near_names, hbm))
        source = {name: ref.at[image] for name, ref in zip(loads, sources)}
        place = {name: ref.at[image] for name, ref in zip(stores, places)}
        vec = vector_reader(vecs)
        sums_ref[...] = previous[-1][...]
        early = first_section()

        @pl.when(early)
        def _():
            fetch = Copies(
                sem,
                {
                    W_DOWN: (far[W_DOWN], near[W_DOWN]),
                    SLOPE: (source[SLOPE], refs[SLOPE]),
                    W_UP: (far[W_UP], near[W_UP]),
                    R: (source[R], refs[R]),
                },
            )
            fetch.start()
            store = Copies(sem.at[pl.ds(4, 2)], {name: (refs[name], place[name]) for name in (GZ, GB)})
            pad_rows(refs[E], received_ref)
            feed_forward_back(refs, fetch.wait, store.start, vec, near, live, vector_adder(sums_ref))
            store.wait()

        @pl.when(jnp.logical_not(early))
        def _():
            fetch = Copies(
                sem,
                {
                    M: (source[M], refs[M]),
                    W_DOWN: (far[W_DOWN], near[W_DOWN]),
                    R: (source[R], refs[R]),
                },
            )
            fetch.start()
            fetch.wait()
            output_part(refs, vec, near, live)
            store = Copies(sem.at[pl.ds(4, 1)], {Y: (refs[Y], place[Y])})
            store.start()
            store.wait()

    gz, gb, output, sums, gr = call(
        kernel,
        1,
        count,
        (received,)
        + vectors
        + tuple(saved[SAVED.index(name)] for name in loads)
        + tuple(weights[WEIGHTS.index(name)] for name in near_names)
        + tuple(old),
        [image_block((slots, width), 0)]
        + [fixed_block(vector.shape) for vector in vectors]
        + [ANY] * (len(loads) + len(near_names) + len(old) - 1)
        + [fixed_block(sums.shape)],
        [
            jax.ShapeDtypeStruct((images,) + shapes[GZ][0], bf16),
            jax.ShapeDtypeStruct((images,) + shapes[GB][0], bf16),
            jax.ShapeDtypeStruct((images,) + shapes[Y][0], bf16),
            jax.ShapeDtypeStruct(sums.shape, f32),
            jax.ShapeDtypeStruct((1,) + shapes[GR][0], f32),
        ],
        [ANY] * 3 + [fixed_block(sums.shape), image_block(shapes[GR][0], 0)],
        [pltpu.VMEM(weights[WEIGHTS.index(name)].shape, bf16) for name in near_names]
        + [pltpu.VMEM(*shapes[name]) for name in work]
        + [pltpu.SemaphoreType.DMA((7,))],
        f"late_feed_forward_{image}",
        {at + k: k for k in range(len(old))},
    )
    return [gz, gb] + list(made[2:]), output, sums, gr


def late_attention(image, saved, made, sums, gr, count, index, vectors, weights):
    images, slots, width = made[MADE.index(GRAD)].shape
    rows, hidden = saved[SAVED.index(M)].shape[1:]
    shapes = image_shapes(slots, rows, width, hidden)
    work = (GB, QKV, U, GO, GQKV, GA, GU, GRAD)
    near_names = (W_OUT, W_QKV)
    old = [made[MADE.index(GQKV)], made[MADE.index(GRAD)], sums]
    sources = (made[MADE.index(GB)], saved[SAVED.index(QKV)], saved[SAVED.index(U)])
    at = 1 + 2 + len(vectors) + len(sources) + len(near_names)

    def kernel(count_ref, index_ref, gr_ref, *rest):
        vecs, loads, hbm, previous, gqkv_ref, grad_ref, sums_ref, local, scratch, sem = split(
            rest, len(vectors), len(sources), 2, len(old), None, None, None, 2, len(work), None
        )
        live = count_ref[image]
        sums_ref[...] = previous[-1][...]
        refs = dict(zip(work, scratch)) | {GR: gr_ref}
        near = dict(zip(near_names, local))

        @pl.when(first_section())
        def _():
            fetch = Copies(
                sem,
                {
                    GB: (loads[0].at[image], refs[GB]),
                    W_OUT: (hbm[0], near[W_OUT]),
                    QKV: (loads[1].at[image], refs[QKV]),
                    W_QKV: (hbm[1], near[W_QKV]),
                    U: (loads[2].at[image], refs[U]),
                },
            )
            fetch.start()
            store = Copies(
                sem.at[pl.ds(5, 2)],
                {GQKV: (refs[GQKV], gqkv_ref.at[image]), GRAD: (refs[GRAD], grad_ref.at[image])},
            )
            attention_back(refs, fetch.wait, store.start, vector_reader(vecs), near, live, vector_adder(sums_ref))
            chosen = gather_matrix(index_ref[image : image + 1, :], live)
            refs[GRAD][...] = product(chosen, refs[GU][:slots, :], NN)[:slots, :].astype(bf16)
            store.start(GRAD)
            store.wait()

    gqkv, grad, sums = call(
        kernel,
        1,
        count,
        (index, gr)
        + vectors
        + sources
        + tuple(weights[WEIGHTS.index(name)] for name in near_names)
        + tuple(old),
        [fixed_block(index.shape), image_block((rows, width), 0)]
        + [fixed_block(vector.shape) for vector in vectors]
        + [ANY] * (len(sources) + len(near_names) + len(old) - 1)
        + [fixed_block(sums.shape)],
        [
            jax.ShapeDtypeStruct((images,) + shapes[GQKV][0], bf16),
            jax.ShapeDtypeStruct((images,) + shapes[GRAD][0], bf16),
            jax.ShapeDtypeStruct(sums.shape, f32),
        ],
        [ANY] * 2 + [fixed_block(sums.shape)],
        [pltpu.VMEM(weights[WEIGHTS.index(name)].shape, bf16) for name in near_names]
        + [pltpu.VMEM(*shapes[name]) for name in work]
        + [pltpu.SemaphoreType.DMA((7,))],
        f"late_attention_{image}",
        {at + k: k for k in range(len(old))},
    )
    return list(made[:2]) + [gqkv, grad], sums


def pick(table, at):
    value = table[0]
    for k in range(1, len(table)):
        value = jnp.where(at == k, table[k], value)
    return value


def weight_gradient(side, arrays, blocks, name):
    depth = arrays[0].shape[0]
    width = min(array.shape[1] for array in arrays)
    half = len(blocks) // 2

    def chosen(i, scalar_ref):
        bit = scalar_ref[0]
        return jnp.where(i < half, (1 - bit) * half + i, bit * half + i - half)

    def kernel(scalar_ref, *refs):
        send_ref, keep_ref = refs[-2:]
        step = pl.program_id(0)
        block = chosen(step, scalar_ref)
        for left, right in dict.fromkeys((left, right) for left, right, _ in blocks):
            here = functools.reduce(
                jnp.logical_or, [block == k for k, entry in enumerate(blocks) if entry[:2] == (left, right)]
            )

            @pl.when(here & (step < half))
            def _():
                send_ref[...] = product(refs[left][...], refs[right][...], TN).astype(bf16)

            @pl.when(here & (step >= half))
            def _():
                keep_ref[...] = product(refs[left][...], refs[right][...], TN)

    def columns(at):
        table = [column if right == at else 0 for _, right, column in blocks]
        return pl.BlockSpec((depth, width), lambda i, s: (0, pick(table, chosen(i, s))))

    return call(
        kernel,
        2 * half,
        side,
        arrays,
        [columns(at) for at in range(len(arrays))],
        [jax.ShapeDtypeStruct((half * width, width), bf16), jax.ShapeDtypeStruct((half * width, width), f32)],
        [
            pl.BlockSpec((width, width), lambda i, s: (jnp.minimum(i, half - 1), 0)),
            pl.BlockSpec((width, width), lambda i, s: (jnp.maximum(i - half, 0), 0)),
        ],
        [],
        name,
    )


def down_gradient(side, count, m, cotangent, received):
    images, slots, width = cotangent.shape
    rows, hidden = m.shape[1:]
    blocks = hidden // width
    half = blocks // 2
    scalars = jnp.concatenate([side, count])

    def chosen(i, scalar_ref):
        bit = scalar_ref[0]
        return jnp.where(i < half, (1 - bit) * half + i, bit * half + i - half)

    def kernel(scalar_ref, m_ref, e_ref, *rest):
        arrived, (send_ref, keep_ref, gd_ref) = rest[:images], rest[images:]
        step = pl.program_id(0)
        early = first_section()

        @pl.when(step == 0)
        def _():
            for image in range(images):
                live = row_mask((slots, width), scalar_ref[1 + image])
                top = slice(image * rows, image * rows + slots)
                gd_ref[top, :] = jnp.where(live, jnp.where(early, arrived[image][...], e_ref[image]), jnp.zeros((), bf16))
                gd_ref[top.stop : (image + 1) * rows, :] = jnp.zeros((rows - slots, width), bf16)

        left = m_ref[...].reshape(images * rows, width)

        @pl.when(step < half)
        def _():
            send_ref[...] = product(left, gd_ref[...], TN).astype(bf16)

        @pl.when(step >= half)
        def _():
            keep_ref[...] = product(left, gd_ref[...], TN)

    return call(
        kernel,
        blocks,
        scalars,
        (m, cotangent) + tuple(received),
        [
            pl.BlockSpec((images, rows, width), lambda i, s: (0, 0, chosen(i, s))),
            fixed_block(cotangent.shape),
        ]
        + [image_block((slots, width), 0)] * images,
        [jax.ShapeDtypeStruct((half * width, width), bf16), jax.ShapeDtypeStruct((half * width, width), f32)],
        [
            pl.BlockSpec((width, width), lambda i, s: (jnp.minimum(i, half - 1), 0)),
            pl.BlockSpec((width, width), lambda i, s: (jnp.maximum(i - half, 0), 0)),
        ],
        [pltpu.VMEM((images * rows, width), bf16)],
        "grad_down",
    )


def assembled(side, mine, other, places, shapes, name, before=None):
    width = mine.shape[1]
    half = mine.shape[0] // width
    before = before or {}

    def chosen(i, scalar_ref):
        bit = scalar_ref[0]
        return jnp.where(i < half, bit * half + i, (1 - bit) * half + i - half)

    def kernel(scalar_ref, mine_ref, other_ref, *refs):
        outs = refs[len(before) :]
        step = pl.program_id(0)
        block = chosen(step, scalar_ref)
        for at, out_ref in enumerate(outs):
            here = functools.reduce(
                jnp.logical_or, [block == k for k, entry in enumerate(places) if entry[0] == at]
            )

            @pl.when(here & (step < half))
            def _():
                out_ref[...] = mine_ref[...].astype(f32)

            @pl.when(here & (step >= half))
            def _():
                out_ref[...] = other_ref[...].astype(f32)

    def place(at):
        last = [entry for entry in places if entry[0] == at][0]
        entries = [entry if entry[0] == at else last for entry in places]

        def index(i, s):
            block = chosen(i, s)
            return (pick([entry[1] for entry in entries], block), pick([entry[2] for entry in entries], block))

        return index

    return call(
        kernel,
        2 * half,
        side,
        (mine, other) + tuple(before.values()),
        [
            pl.BlockSpec((width, width), lambda i, s: (jnp.minimum(i, half - 1), 0)),
            pl.BlockSpec((width, width), lambda i, s: (jnp.maximum(i - half, 0), 0)),
        ]
        + [ANY] * len(before),
        [jax.ShapeDtypeStruct(shape, f32) for shape in shapes],
        [pl.BlockSpec((width, width), place(at)) for at in range(len(shapes))],
        [],
        name,
        {3 + k: at for k, at in enumerate(before)},
    )


def swapped(value, axis, stride):
    length = lax.axis_size(axis)
    return lax.ppermute(value, axis, [(i, i ^ stride) for i in range(length)])


def bit_of(axis, stride):
    return (lax.axis_index(axis) // stride) % 2


def plain_call(kernel, ins, outs, scratch, name):
    return pl.pallas_call(
        kernel,
        out_shape=outs,
        in_specs=[ANY] * len(ins),
        out_specs=[pl.BlockSpec(memory_space=pltpu.VMEM)] * len(outs),
        scratch_shapes=scratch,
        compiler_params=pltpu.CompilerParams(vmem_limit_bytes=60 << 20),
        cost_estimate=pl.CostEstimate(flops=COST, bytes_accessed=COST, transcendentals=0),
        name=name,
    )(*ins)


def halved(keep, coming, stride):
    height, width = keep.shape[0] // 2, keep.shape[1]
    if height % ROW_TILE:
        bit = bit_of(DP, stride)
        pair = keep + coming.astype(f32)
        send = lax.dynamic_slice_in_dim(pair, (1 - bit) * height, height, axis=0).astype(bf16)
        return send, lax.dynamic_slice_in_dim(pair, bit * height, height, axis=0)

    def kernel(keep_ref, coming_ref, send_ref, stay_ref, kept, came, sem):
        bit = bit_of(DP, stride)
        copies = []
        for at, half in enumerate((1 - bit, bit)):
            rows = pl.ds(pl.multiple_of(half * height, ROW_TILE), height)
            copies.append(pltpu.make_async_copy(keep_ref.at[rows, :], kept.at[at], sem.at[2 * at]))
            copies.append(pltpu.make_async_copy(coming_ref.at[rows, :], came.at[at], sem.at[2 * at + 1]))
        for copy in copies:
            copy.start()
        for copy in copies[:2]:
            copy.wait()
        send_ref[...] = (kept[0] + came[0].astype(f32)).astype(bf16)
        for copy in copies[2:]:
            copy.wait()
        stay_ref[...] = kept[1] + came[1].astype(f32)

    shape = (height, width)
    return plain_call(
        kernel,
        (keep, coming),
        [jax.ShapeDtypeStruct(shape, bf16), jax.ShapeDtypeStruct(shape, f32)],
        [
            pltpu.VMEM((2,) + shape, f32),
            pltpu.VMEM((2,) + shape, bf16),
            pltpu.SemaphoreType.DMA((4,)),
        ],
        f"halved_{stride}",
    )


def summed(keep, coming, total):
    if keep.shape[0] % ROW_TILE:
        return ((keep + coming.astype(f32)) / total).astype(bf16)

    def kernel(keep_ref, coming_ref, out_ref, kept, came, sem):
        copies = [
            pltpu.make_async_copy(keep_ref, kept, sem.at[0]),
            pltpu.make_async_copy(coming_ref, came, sem.at[1]),
        ]
        for copy in copies:
            copy.start()
        for copy in copies:
            copy.wait()
        out_ref[...] = ((kept[...] + came[...].astype(f32)) / total).astype(bf16)

    return plain_call(
        kernel,
        (keep, coming),
        [jax.ShapeDtypeStruct(keep.shape, bf16)],
        [pltpu.VMEM(keep.shape, f32), pltpu.VMEM(keep.shape, bf16), pltpu.SemaphoreType.DMA((2,))],
        "summed",
    )[0]


def joined(mine, other, stride):
    height, width = mine.shape
    if height % ROW_TILE:
        first = bit_of(DP, stride) == 0
        return jnp.concatenate([jnp.where(first, mine, other), jnp.where(first, other, mine)], axis=0)

    def kernel(mine_ref, other_ref, out_ref, sem):
        bit = bit_of(DP, stride)
        copies = []
        for at, (half, source) in enumerate(((bit, mine_ref), (1 - bit, other_ref))):
            rows = pl.ds(pl.multiple_of(half * height, ROW_TILE), height)
            copies.append(pltpu.make_async_copy(source, out_ref.at[rows, :], sem.at[at]))
        for copy in copies:
            copy.start()
        for copy in copies:
            copy.wait()

    return plain_call(
        kernel,
        (mine, other),
        [jax.ShapeDtypeStruct((2 * height, width), bf16)],
        [pltpu.SemaphoreType.DMA((2,))],
        f"joined_{stride}",
    )[0]


def strides_of(size):
    return [1 << at for at in range(size.bit_length() - 1)]


class Line:
    def __init__(self):
        self.last = None

    def gate(self, value):
        if self.last is None:
            return value
        return lax.optimization_barrier((value, self.last))[0]

    def passed(self, value):
        self.last = value


class Exchange:
    def __init__(self, line, send, keep, strides, total):
        self.line, self.keep, self.strides, self.total = line, keep, strides, total
        self.at, self.value, self.result = 0, None, None
        self.coming = swapped(send, REP, 1)

    def advance(self):
        coming = self.line.gate(self.coming)
        count = len(self.strides)
        if self.at < count:
            stride = self.strides[self.at]
            send, self.keep = halved(self.keep, coming, stride)
            self.coming = swapped(send, DP, stride)
            self.line.passed(send)
        elif self.at == count:
            self.value = summed(self.keep, coming, self.total)
            self.coming = swapped(self.value, DP, self.strides[-1])
            self.line.passed(self.value)
        elif self.at <= 2 * count:
            stride = self.strides[2 * count - self.at]
            self.value = joined(self.value, coming, stride)
            if self.at < 2 * count:
                self.coming = swapped(self.value, DP, self.strides[2 * count - 1 - self.at])
            else:
                self.coming = swapped(self.value, REP, 1)
            self.line.passed(self.value)
        else:
            self.result = (self.value, coming)
            self.line.passed(coming)
        self.at += 1


class Total:
    def __init__(self, line, value, strides, total):
        self.line, self.value, self.total = line, value, total
        self.partners = [(REP, 1)] + [(DP, stride) for stride in strides]
        self.at, self.result = 0, None
        self.coming = swapped(value, *self.partners[0])

    def advance(self):
        self.value = self.value + self.line.gate(self.coming)
        self.at += 1
        if self.at < len(self.partners):
            self.coming = swapped(self.value, *self.partners[self.at])
        else:
            self.result = self.value / self.total
        self.line.passed(self.value)


def shards(
    boundary,
    keep_index,
    keep_count,
    gain_one,
    shift_one,
    w_qkv,
    bias_query,
    bias_value,
    w_out,
    bias_out,
    gain_two,
    shift_two,
    w_up,
    bias_up,
    w_down,
    bias_down,
):
    images = keep_index.shape[0]
    width = boundary.shape[-1]
    weights = (w_qkv[0], w_out[0], w_up[0], w_down[0])
    hidden = weights[2].shape[1]
    vectors = (gain_one, shift_one, bias_query, bias_value, bias_out, gain_two, shift_two, bias_down, bias_up)
    rows_in = boundary[0]

    line = Line()
    carry, received = None, []
    for image in range(images):
        carry, first_output = first_forward(image, carry, keep_count, keep_index, rows_in, vectors, weights)
        received.append(lax.ppermute(first_output, SECTION, [(0, 1)]))
    saved, output = carry[:-1], carry[-1]
    made, sums, returned = None, None, []
    for image in range(images):
        saved, made, sums, grad_first = middle(
            image, saved, made, sums, keep_count, received[image], rows_in, vectors, weights
        )
        returned.append(lax.ppermute(grad_first, SECTION, [(1, 0)]))
    line.passed(grad_first)

    def flat(name):
        array = saved[SAVED.index(name)] if name in SAVED else made[MADE.index(name)]
        return array.reshape(-1, array.shape[-1])

    total = images * lax.axis_size((DP, REP))
    side = lax.axis_index(REP).astype(jnp.int32)[None]
    near_first = strides_of(lax.axis_size(DP))
    far_first = near_first[1::-1] + near_first[2:]
    square, many = (width, width), hidden // width
    forwards, attentions = list(range(images)), list(range(images))
    residual = [None] * images
    exchanges, outs = {}, {}

    def begin(name, pair, strides):
        line.passed(pair[0])
        exchanges[name] = Exchange(line, *pair, strides, total)

    def feed_forward():
        nonlocal made, output, sums
        image = forwards.pop(0)
        made, output, sums, residual[image] = late_feed_forward(
            image, saved, made, output, sums, line.gate(keep_count), returned[image], vectors, weights
        )
        line.passed(residual[image])

    def attention():
        nonlocal made, sums
        image = attentions.pop(0)
        made, sums = late_attention(
            image, saved, made, sums, residual[image], line.gate(keep_count), keep_index, vectors, weights
        )
        line.passed(sums)

    def grad_down():
        pair = down_gradient(line.gate(side), keep_count, saved[SAVED.index(M)], rows_in, returned)
        begin(DOWN, pair, near_first)

    def grad_up():
        blocks = [(0, 1, column) for column in range(many)]
        begin(UP, weight_gradient(line.gate(side), (flat(C), flat(GZ)), blocks, "grad_up"), near_first)

    def grad_query_value():
        exchanges[SUMS] = Total(line, sums, near_first, total)
        pair = weight_gradient(line.gate(side), (flat(A), flat(GQKV)), [(0, 1, 0), (0, 1, 2)], "grad_query_value")
        begin(QUERY_VALUE, pair, far_first)

    def grad_key_out():
        arrays = (flat(A), flat(GQKV), flat(O), flat(GB))
        pair = weight_gradient(line.gate(side), arrays, [(0, 1, 1), (2, 3, 0)], "grad_key_out")
        begin(KEY_OUT, pair, near_first)

    def end(name):
        places, shapes = {
            DOWN: ([(0, k, 0) for k in range(many)], [(hidden, width)]),
            UP: ([(0, 0, k) for k in range(many)], [(width, hidden)]),
            QUERY_VALUE: ([(0, 0, 0), (0, 0, 2)], [(width, 3 * width)]),
            KEY_OUT: ([(0, 0, 1), (1, 0, 0)], [(width, 3 * width), square]),
        }[name]
        part = name in (QUERY_VALUE, KEY_OUT)
        before = {0: outs[QKV]} if part and QKV in outs else {}
        mine, other = exchanges[name].result
        whole = assembled(line.gate(side), mine, other, places, shapes, f"whole_{name}", before)
        line.passed(whole[0])
        outs[QKV if part else name] = whole[0]
        outs.update({OUT: piece for piece in whole[1:]})

    steps = dict(zip("FAGUQK", (feed_forward, attention, grad_down, grad_up, grad_query_value, grad_key_out)))
    transfers = dict(zip("duqks", (DOWN, UP, QUERY_VALUE, KEY_OUT, SUMS)))
    stages = 2 * len(near_first) + 2
    plain = "FA" * images + "GUQK" + "duqk" * stages + "s" * (stages // 2)
    for step in ORDER if (images, stages) == (3, 8) else plain:
        if step in steps:
            steps[step]()
            continue
        name = transfers[step]
        exchanges[name].advance()
        if exchanges[name].result is not None and name != SUMS:
            end(name)
    assert all(exchange.result is not None for exchange in exchanges.values())
    sums = exchanges[SUMS].result
    small = [sums[at : at + 1] for at in VECTORS[:-1]]
    return (
        output[None],
        made[MADE.index(GRAD)][None],
        small[GAIN_ONE],
        small[SHIFT_ONE],
        outs[QKV][None],
        small[BIAS_QUERY],
        small[BIAS_VALUE],
        outs[OUT][None],
        small[BIAS_OUT],
        small[GAIN_TWO],
        small[SHIFT_TWO],
        outs[UP][None],
        sums[BIAS_UP : BIAS_UP + many].reshape(1, -1),
        outs[DOWN][None],
        small[BIAS_DOWN],
    )


def solution(mesh):
    per_image = (DP, REP)
    matrix, line = P(SECTION, None, None), P(SECTION, None)
    rows = P(SECTION, per_image, None, None)
    kinds = (line, line, matrix, line, line, matrix, line, line, line, matrix, line, matrix, line)
    return jax.shard_map(
        shards,
        mesh=mesh,
        in_specs=(rows, P(per_image, None), P(per_image)) + kinds,
        out_specs=(rows, rows) + kinds,
        check_vma=False,
    )
```

time: 514 us -> 387 us (0.75)
  waiting for transfers between devices: 214 us -> 75.7 us
  Pallas kernels: 139 us -> 242 us
  local copies, waits for them, and re-layouts: 56.8 us -> 7.08 us
  other arithmetic: 52.3 us -> 5.73 us
  starting transfers between devices: 41.3 us -> 47.5 us
    ppermute x28 -> x36, waiting for transfers between devices: 172 us -> 61.8 us  [swapped(): return lax.ppermute(value, axis, [(i, i ^ stride) for i in range(length)])]
    pallas_call x0 -> x28, Pallas kernels: none -> 69.5 us  [plain_call(): pl.pallas_call(kernel, out_shape=outs, in_specs=[ANY] * len(ins), out_spe...]
    pallas_call x6 -> x20, Pallas kernels: 139 us -> 173 us  [call(): pl.pallas_call(kernel, out_shape=outs, grid_spec=pltpu.PrefetchScalarGrid...]
    ppermute x2 -> x6, waiting for transfers between devices: 42.1 us -> 13.9 us  [the longest x3 13.9 us: shards(): returned.append(lax.ppermute(grad_first, SECTION, [(1, 0)]))]
    another operation x2 -> x0, local copies, waits for them, and re-layouts: 25.7 us -> none  [shards(): across(up)[None]]
    concatenate x12 -> x1, other arithmetic: 12.2 us -> 0.59 us  [down_gradient(): scalars = jnp.concatenate([side, count])]
    select_n x11 -> x0, other arithmetic: 11.2 us -> none  [joined(): jnp.where(first, mine, other)]
    add x12 -> x3, other arithmetic: 14.5 us -> 4.31 us  [advance(): self.value = self.value + self.line.gate(self.coming)]
  transfers between devices with their start and end apart: 30 -> 42, of which waited for: 15 -> 15; matrix products, arithmetic and copies ran while one was open for 18% -> 2% of each run, Pallas kernels for 3% -> 55%
where the time goes in v2:
time: 387 us; the launch traced here: 380 us
  Pallas kernels  242 us (63%)
  waiting for transfers between devices  75.7 us (20%)
  starting transfers between devices  47.5 us (12%)
  local copies, waits for them, and re-layouts  7.08 us (2%)
  other arithmetic  5.73 us (1%)
    pallas_call x20, Pallas kernels, call(): pl.pallas_call(kernel, out_shape=outs, grid_spec=pltpu.PrefetchScalarGrid...  173 us
    pallas_call x28, Pallas kernels, plain_call(): pl.pallas_call(kernel, out_shape=outs, in_specs=[ANY] * len(ins), out_spe...  69.5 us
    ppermute x36, waiting for transfers between devices, swapped(): return lax.ppermute(value, axis, [(i, i ^ stride) for i in range(length)])  61.8 us
    ppermute x36, starting transfers between devices, swapped(): return lax.ppermute(value, axis, [(i, i ^ stride) for i in range(length)])  31.9 us
    ppermute x3, waiting for transfers between devices, shards(): returned.append(lax.ppermute(grad_first, SECTION, [(1, 0)]))  13.9 us
    ppermute x3, starting transfers between devices, shards(): returned.append(lax.ppermute(grad_first, SECTION, [(1, 0)]))  9.63 us
  transfers between devices with their start and end apart: 42, of which 15 were waited for; matrix products, arithmetic and copies ran while one was open for 2% of the time, Pallas kernels for 55%

profile of v2, /device:TPU:0, one launch (start us, length us, event | category | flops | bytes accessed | tf_op | source)
XLA Modules:
  0.0 380.1 jit_solution(15413801249359181477)
XLA Ops:
  0.6 12.7 %first_forward_0.1 = (bf16[3,208,768]{2,1,0:T(8,128)(2,1)}, bf16[3,208,768]{2,1,0:T(8,128)(2,1)}, bf16[3,208,2304]{2,1,0:T(8,128)(2,1)}, bf16[3,208,768]{2,1,0:T...) custom-call(s32[3]{0:T(128)} %count_ref.17, ...), custom_call_target="tpu_custom_call" | custom-call | flops 99999997952 | bytes 99999997952 | tf_op jit(solution)/shard_map/first_forward_0/pallas_call | solution.py:287
  15.3 12.8 %first_forward_1.1 = (bf16[3,208,768]{2,1,0:T(8,128)(2,1)}, bf16[3,208,768]{2,1,0:T(8,128)(2,1)}, bf16[3,208,2304]{2,1,0:T(8,128)(2,1)}, bf16[3,208,768]{2,1,0:T...) custom-call(s32[3]{0:T(128)} %count_ref.17, ...), custom_call_target="tpu_custom_call", output_to_operand_aliasing={{0}: (16, {}), {1}: (17, {}), {2}: (18, {}), {3}: (19, {}),... | custom-call | flops 99999997952 | bytes 99999997952 | tf_op jit(solution)/shard_map/first_forward_1/pallas_call | solution.py:287
  30.2 12.9 %first_forward_2.1 = (bf16[3,208,768]{2,1,0:T(8,128)(2,1)}, bf16[3,208,768]{2,1,0:T(8,128)(2,1)}, bf16[3,208,2304]{2,1,0:T(8,128)(2,1)}, bf16[3,208,768]{2,1,0:T...) custom-call(s32[3]{0:T(128)} %count_ref.17, ...), custom_call_target="tpu_custom_call", output_to_operand_aliasing={{0}: (16, {}), {1}: (17, {}), {2}: (18, {}), {3}: (19, {}),... | custom-call | flops 99999997952 | bytes 99999997952 | tf_op jit(solution)/shard_map/first_forward_2/pallas_call | solution.py:287
  49.6 7.2 %middle_1.1 = (bf16[3,208,768]{2,1,0:T(8,128)(2,1)}, bf16[3,208,768]{2,1,0:T(8,128)(2,1)}, bf16[3,208,2304]{2,1,0:T(8,128)(2,1)}, bf16[3,208,768]{2,1,0:T(8,128)...) custom-call(s32[3]{0:T(128)} %count_ref.17, ...), custom_call_target="tpu_custom_call", output_to_operand_aliasing={{0}: (16, {}), {1}: (17, {}), {2}: (18, {}), {3}: (19, {}),... | custom-call | flops 99999997952 | bytes 99999997952 | tf_op jit(solution)/shard_map/middle_1/pallas_call | solution.py:287
  56.8 8.5 %middle_2.1 = (bf16[3,208,768]{2,1,0:T(8,128)(2,1)}, bf16[3,208,768]{2,1,0:T(8,128)(2,1)}, bf16[3,208,2304]{2,1,0:T(8,128)(2,1)}, bf16[3,208,768]{2,1,0:T(8,128)...) custom-call(s32[3]{0:T(128)} %count_ref.17, ...), custom_call_target="tpu_custom_call", output_to_operand_aliasing={{0}: (16, {}), {1}: (17, {}), {2}: (18, {}), {3}: (19, {}),... | custom-call | flops 99999997952 | bytes 99999997952 | tf_op jit(solution)/shard_map/middle_2/pallas_call | solution.py:287
  65.3 7.0 %collective-permute-start.5 = (bf16[1,196,768]{2,1,0:T(8,128)(2,1)}, bf16[1,196,768]{2,1,0:T(8,128)(2,1)}, u32[]{:S(2)}, u32[]{:S(2)}) collective-permute-start(bf16[1,196,768]{2,1,0:T(8,128)(2,1)} %get-tuple-element.250), channel_id=1, source_target_pairs={{16,0},{17,1},{18,2},{19,3},{20,4},{21,5},{22,6},{23,7},{24,8},{25... | collective-permute-start | bytes 903176 | tf_op jit(solution)/shard_map/ppermute | solution.py:990
  73.7 10.6 %late_feed_forward_0.1 = (bf16[3,208,3072]{2,1,0:T(8,128)(2,1)}, bf16[3,208,768]{2,1,0:T(8,128)(2,1)}, bf16[3,196,768]{2,1,0:T(8,128)(2,1)}, f32[16,768]{1,0:T(8,128)}, f32[1,208,768]{2,1,0:T(8,128)}) custom-call(s32[3]{0:T(128)} %count_ref.17, ...), custom_call_target="tpu_custom_call", output_to_operand_aliasing={{0}: (16, {}), {1}: (17, {}), {2}: (18, {}), {3}: (19, {})} | custom-call | flops 99999997952 | bytes 99999997952 | tf_op jit(solution)/shard_map/late_feed_forward_0/pallas_call | solution.py:287
  84.3 10.4 %late_attention_0.1 = (bf16[3,208,2304]{2,1,0:T(8,128)(2,1)}, bf16[3,196,768]{2,1,0:T(8,128)(2,1)}, f32[16,768]{1,0:T(8,128)}) custom-call(s32[3]{0:T(128)} %count_ref.17, s32[3,196]{1,0:T(4,128)} %index_ref.11, f32[1,208,768]{2,1,0:T(8,128)} %get-tuple-element.260.gr_ref, ...), custom_call_target="tpu_custom_call", output_to_operand_aliasing={{0}: (17, {}), {1}: (18, {}), {2}: (19, {})} | custom-call | flops 99999997952 | bytes 99999997952 | tf_op jit(solution)/shard_map/late_attention_0/pallas_call | solution.py:287
  95.4 7.8 %collective-permute-done.5.rest_2_.received_ref = bf16[1,196,768]{2,1,0:T(8,128)(2,1)} collective-permute-done((bf16[1,196,768]{2,1,0:T(8,128)(2,1)}, bf16[1,196,768]{2,1,0:T(8,128)(2,1)}, u32[]{:S(2)}, u32[]{:S(2)}) %collective-permute-start.5) | collective-permute-done | bytes 301088 | tf_op jit(solution)/shard_map/ppermute | solution.py:990
  103.1 6.2 %collective-permute-done.4.rest_1_.received_ref = bf16[1,196,768]{2,1,0:T(8,128)(2,1)} collective-permute-done((bf16[1,196,768]{2,1,0:T(8,128)(2,1)}, bf16[1,196,768]{2,1,0:T(8,128)(2,1)}, u32[]{:S(2)}, u32[]{:S(2)}) %collective-permute-start.4) | collective-permute-done | bytes 301088 | tf_op jit(solution)/shard_map/ppermute | solution.py:990
  109.3 9.7 %grad_down.1 = (bf16[1536,768]{1,0:T(8,128)(2,1)}, f32[1536,768]{1,0:T(8,128)}) custom-call(s32[4]{0:T(128)} %pad_add_fusion.scalar_ref, bf16[3,208,3072]{2,1,0:T(8,128)(2,1)} %get-tuple-element.255.rest_11_.m_ref, bf16[3,196,768]{2,1,0:T(8,128)(2,1)} %bitcast.65, bf16[1,196,768]{2,1,0:T(8,128)(2,1)} %collective-permute-done.3.received_ref.rest_0_, ...), custom_call_target="tpu_custom_call" | custom-call | flops 99999997952 | bytes 99999997952 | tf_op jit(solution)/shard_map/grad_down/pallas_call | solution.py:287
  118.9 10.8 %late_feed_forward_1.1 = (bf16[3,208,3072]{2,1,0:T(8,128)(2,1)}, bf16[3,208,768]{2,1,0:T(8,128)(2,1)}, bf16[3,196,768]{2,1,0:T(8,128)(2,1)}, f32[16,768]{1,0:T(8,128)}, f32[1,208,768]{2,1,0:T(8,128)}) custom-call(s32[3]{0:T(128)} %count_ref.17, ...), custom_call_target="tpu_custom_call", output_to_operand_aliasing={{0}: (16, {}), {1}: (17, {}), {2}: (18, {}), {3}: (19, {})} | custom-call | flops 99999997952 | bytes 99999997952 | tf_op jit(solution)/shard_map/late_feed_forward_1/pallas_call | solution.py:287
  131.1 4.9 %halved_1.4 = (bf16[768,768]{1,0:T(8,128)(2,1)}, f32[768,768]{1,0:T(8,128)}) custom-call(f32[1536,768]{1,0:T(8,128)} %get-tuple-element.271.keep_ref, bf16[1536,768]{1,0:T(8,128)(2,1)} %copy-done.2), custom_call_target="tpu_custom_call" | custom-call | flops 99999997952 | bytes 99999997952 | tf_op jit(solution)/shard_map/halved_1/pallas_call | solution.py:788
  138.5 10.4 %late_attention_1.1 = (bf16[3,208,2304]{2,1,0:T(8,128)(2,1)}, bf16[3,196,768]{2,1,0:T(8,128)(2,1)}, f32[16,768]{1,0:T(8,128)}) custom-call(s32[3]{0:T(128)} %count_ref.17, s32[3,196]{1,0:T(4,128)} %index_ref.11, f32[1,208,768]{2,1,0:T(8,128)} %get-tuple-element.276.gr_ref, ...), custom_call_target="tpu_custom_call", output_to_operand_aliasing={{0}: (17, {}), {1}: (18, {}), {2}: (19, {})} | custom-call | flops 99999997952 | bytes 99999997952 | tf_op jit(solution)/shard_map/late_attention_1/pallas_call | solution.py:287
  148.8 10.9 %late_feed_forward_2.1 = (bf16[3,208,3072]{2,1,0:T(8,128)(2,1)}, bf16[3,208,768]{2,1,0:T(8,128)(2,1)}, bf16[3,196,768]{2,1,0:T(8,128)(2,1)}, f32[16,768]{1,0:T(8,128)}, f32[1,208,768]{2,1,0:T(8,128)}) custom-call(s32[3]{0:T(128)} %count_ref.17, ...), custom_call_target="tpu_custom_call", output_to_operand_aliasing={{0}: (16, {}), {1}: (17, {}), {2}: (18, {}), {3}: (19, {})} | custom-call | flops 99999997952 | bytes 99999997952 | tf_op jit(solution)/shard_map/late_feed_forward_2/pallas_call | solution.py:287
  159.7 8.4 %grad_up.1 = (bf16[1536,768]{1,0:T(8,128)(2,1)}, f32[1536,768]{1,0:T(8,128)}) custom-call(s32[1]{0:T(128)} %bitcast.scalar_ref, bf16[624,768]{1,0:T(8,128)(2,1)} %bitcast.77, bf16[624,3072]{1,0:T(8,128)(2,1)} %bitcast.69), custom_call_target="tpu_custom_call" | custom-call | flops 99999997952 | bytes 99999997952 | tf_op jit(solution)/shard_map/grad_up/pallas_call | solution.py:287
  168.4 3.2 halved_2.4
  173.2 10.4 %late_attention_2.1 = (bf16[3,208,2304]{2,1,0:T(8,128)(2,1)}, bf16[3,196,768]{2,1,0:T(8,128)(2,1)}, f32[16,768]{1,0:T(8,128)}) custom-call(s32[3]{0:T(128)} %count_ref.17, s32[3,196]{1,0:T(4,128)} %index_ref.11, f32[1,208,768]{2,1,0:T(8,128)} %get-tuple-element.290.gr_ref, ...), custom_call_target="tpu_custom_call", output_to_operand_aliasing={{0}: (17, {}), {1}: (18, {}), {2}: (19, {})} | custom-call | flops 99999997952 | bytes 99999997952 | tf_op jit(solution)/shard_map/late_attention_2/pallas_call | solution.py:287
  183.7 4.9 %halved_1.5 = (bf16[768,768]{1,0:T(8,128)(2,1)}, f32[768,768]{1,0:T(8,128)}) custom-call(f32[1536,768]{1,0:T(8,128)} %get-tuple-element.304.keep_ref, bf16[1536,768]{1,0:T(8,128)(2,1)} %collective-permute-done.9.coming_ref), custom_call_target="tpu_custom_call" | custom-call | flops 99999997952 | bytes 99999997952 | tf_op jit(solution)/shard_map/halved_1/pallas_call | solution.py:788
  189.2 5.9 %grad_query_value.1 = (bf16[768,768]{1,0:T(8,128)(2,1)}, f32[768,768]{1,0:T(8,128)}) custom-call(s32[1]{0:T(128)} %bitcast.scalar_ref, bf16[624,768]{1,0:T(8,128)(2,1)} %bitcast.74, bf16[624,2304]{1,0:T(8,128)(2,1)} %bitcast.70), custom_call_target="tpu_custom_call" | custom-call | flops 99999997952 | bytes 99999997952 | tf_op jit(solution)/shard_map/grad_query_value/pallas_call | solution.py:287
  205.0 6.2 %grad_key_out.1 = (bf16[768,768]{1,0:T(8,128)(2,1)}, f32[768,768]{1,0:T(8,128)}) custom-call(s32[1]{0:T(128)} %bitcast.scalar_ref, bf16[624,768]{1,0:T(8,128)(2,1)} %bitcast.75, bf16[624,2304]{1,0:T(8,128)(2,1)} %bitcast.71, bf16[624,768]{1,0:T(8,128)(2,1)} %bitcast.76, bf16[624,768]{1,0:T(8,128)(2,1)} %bitcast.73), custom_call_target="tpu_custom_call" | custom-call | flops 99999997952 | bytes 99999997952 | tf_op jit(solution)/shard_map/grad_key_out/pallas_call | solution.py:287
  211.2 6.1 %collective-permute-done.10.coming_ref = bf16[768,768]{1,0:T(8,128)(2,1)} collective-permute-done((bf16[768,768]{1,0:T(8,128)(2,1)}, bf16[768,768]{1,0:T(8,128)(2,1)}, u32[]{:S(2)}, u32[]{:S(2)}) %collective-permute-start.10) | collective-permute-done | bytes 1179680 | tf_op jit(solution)/shard_map/ppermute | solution.py:780
  217.3 3.2 halved_2.6
  225.7 7.6 %collective-permute-done.15.coming_ref = bf16[384,768]{1,0:T(8,128)(2,1)} collective-permute-done((bf16[384,768]{1,0:T(8,128)(2,1)}, bf16[384,768]{1,0:T(8,128)(2,1)}, u32[]{:S(2)}, u32[]{:S(2)}) %collective-permute-start.15) | collective-permute-done | bytes 589856 | tf_op jit(solution)/shard_map/ppermute | solution.py:780
  241.0 4.4 %collective-permute-done.13.coming_ref = bf16[384,768]{1,0:T(8,128)(2,1)} collective-permute-done((bf16[384,768]{1,0:T(8,128)(2,1)}, bf16[384,768]{1,0:T(8,128)(2,1)}, u32[]{:S(2)}, u32[]{:S(2)}) %collective-permute-start.13) | collective-permute-done | bytes 589856 | tf_op jit(solution)/shard_map/ppermute | solution.py:780
  259.2 6.9 %collective-permute-done.17.coming_ref = bf16[192,768]{1,0:T(8,128)(2,1)} collective-permute-done((bf16[192,768]{1,0:T(8,128)(2,1)}, bf16[192,768]{1,0:T(8,128)(2,1)}, u32[]{:S(2)}, u32[]{:S(2)}) %collective-permute-start.17) | collective-permute-done | bytes 294944 | tf_op jit(solution)/shard_map/ppermute | solution.py:780
  271.1 15.7 %collective-permute-done.25.other_ref = bf16[384,768]{1,0:T(8,128)(2,1)} collective-permute-done((bf16[384,768]{1,0:T(8,128)(2,1)}, bf16[384,768]{1,0:T(8,128)(2,1)}, u32[]{:S(2)}, u32[]{:S(2)}) %collective-permute-start.25) | collective-permute-done | bytes 589856 | tf_op jit(solution)/shard_map/ppermute | solution.py:780
  310.4 12.5 %collective-permute-done.29.other_ref = bf16[384,768]{1,0:T(8,128)(2,1)} collective-permute-done((bf16[384,768]{1,0:T(8,128)(2,1)}, bf16[384,768]{1,0:T(8,128)(2,1)}, u32[]{:S(2)}, u32[]{:S(2)}) %collective-permute-start.29) | collective-permute-done | bytes 589856 | tf_op jit(solution)/shard_map/ppermute | solution.py:780
  344.2 6.9 %whole_100.1 = f32[3072,768]{1,0:T(8,128)} custom-call(s32[1]{0:T(128)} %bitcast.scalar_ref, bf16[1536,768]{1,0:T(8,128)(2,1)} %joined_1.5.mine_ref, bf16[1536,768]{1,0:T(8,128)(2,1)} %copy-done.1), custom_call_target="tpu_custom_call" | custom-call | flops 99999997952 | bytes 99999997952 | tf_op jit(solution)/shard_map/whole_100/pallas_call | solution.py:287
  360.7 4.0 %whole_102.1.refs_0_ = f32[768,2304]{1,0:T(8,128)} custom-call(s32[1]{0:T(128)} %bitcast.scalar_ref, bf16[768,768]{1,0:T(8,128)(2,1)} %joined_2.7.mine_ref, bf16[768,768]{1,0:T(8,128)(2,1)} %copy-done.3), custom_call_target="tpu_custom_call" | custom-call | flops 99999997952 | bytes 99999997952 | tf_op jit(solution)/shard_map/whole_102/pallas_call | solution.py:287
  367.5 6.9 %whole_101.1 = f32[768,3072]{1,0:T(8,128)} custom-call(s32[1]{0:T(128)} %bitcast.scalar_ref, bf16[1536,768]{1,0:T(8,128)(2,1)} %joined_1.6.mine_ref, bf16[1536,768]{1,0:T(8,128)(2,1)} %collective-permute-done.41.other_ref), custom_call_target="tpu_custom_call" | custom-call | flops 99999997952 | bytes 99999997952 | tf_op jit(solution)/shard_map/whole_101/pallas_call | solution.py:287
  375.4 4.2 %whole_103.1 = (f32[768,2304]{1,0:T(8,128)}, f32[768,768]{1,0:T(8,128)}) custom-call(s32[1]{0:T(128)} %bitcast.scalar_ref, bf16[768,768]{1,0:T(8,128)(2,1)} %joined_1.7.mine_ref, bf16[768,768]{1,0:T(8,128)(2,1)} %copy-done.5, f32[768,2304]{1,0:T(8,128)} %whole_102.1.refs_0_), custom_call_target="tpu_custom_call", output_to_operand_aliasing={{0}: (3, {})} | custom-call | flops 99999997952 | bytes 99999997952 | tf_op jit(solution)/shard_map/whole_103/pallas_call | solution.py:287
  (122 shorter events, 118.5 us)
Async XLA Ops:
  13.3 31.8 %collective-permute-start.2 = (bf16[1,196,768]{2,1,0:T(8,128)(2,1)}, bf16[1,196,768]{2,1,0:T(8,128)(2,1)}, u32[]{:S(2)}, u32[]{:S(2)}) collective-permute-start(bf16[1,196,768]{2,1,0:T(8,128)(2,1)} %get-tuple-element.215), channel_id=1, source_target_pairs={{0,16},{1,17},{2,18},{3,19},{4,20},{5,21},{6,22},{7,23},{8,24},{9,... | collective-permute-start | bytes 903176 | tf_op jit(solution)/shard_map/ppermute | solution.py:983
  28.2 21.4 %collective-permute-start.1 = (bf16[1,196,768]{2,1,0:T(8,128)(2,1)}, bf16[1,196,768]{2,1,0:T(8,128)(2,1)}, u32[]{:S(2)}, u32[]{:S(2)}) collective-permute-start(bf16[1,196,768]{2,1,0:T(8,128)(2,1)} %get-tuple-element.214), channel_id=1, source_target_pairs={{0,16},{1,17},{2,18},{3,19},{4,20},{5,21},{6,22},{7,23},{8,24},{9,... | collective-permute-start | bytes 903176 | tf_op jit(solution)/shard_map/ppermute | solution.py:983
  43.1 13.7 %collective-permute-start = (bf16[1,196,768]{2,1,0:T(8,128)(2,1)}, bf16[1,196,768]{2,1,0:T(8,128)(2,1)}, u32[]{:S(2)}, u32[]{:S(2)}) collective-permute-start(bf16[1,196,768]{2,1,0:T(8,128)(2,1)} %get-tuple-element.213), channel_id=1, source_target_pairs={{0,16},{1,17},{2,18},{3,19},{4,20},{5,21},{6,22},{7,23},{8,24},{9,... | collective-permute-start | bytes 903176 | tf_op jit(solution)/shard_map/ppermute | solution.py:983
  48.3 25.4 %collective-permute-start.3 = (bf16[1,196,768]{2,1,0:T(8,128)(2,1)}, bf16[1,196,768]{2,1,0:T(8,128)(2,1)}, u32[]{:S(2)}, u32[]{:S(2)}) collective-permute-start(bf16[1,196,768]{2,1,0:T(8,128)(2,1)} %get-tuple-element.252), channel_id=1, source_target_pairs={{16,0},{17,1},{18,2},{19,3},{20,4},{21,5},{22,6},{23,7},{24,8},{25... | collective-permute-start | bytes 903176 | tf_op jit(solution)/shard_map/ppermute | solution.py:990
  65.3 37.8 %collective-permute-start.5 = (bf16[1,196,768]{2,1,0:T(8,128)(2,1)}, bf16[1,196,768]{2,1,0:T(8,128)(2,1)}, u32[]{:S(2)}, u32[]{:S(2)}) collective-permute-start(bf16[1,196,768]{2,1,0:T(8,128)(2,1)} %get-tuple-element.250), channel_id=1, source_target_pairs={{16,0},{17,1},{18,2},{19,3},{20,4},{21,5},{22,6},{23,7},{24,8},{25... | collective-permute-start | bytes 903176 | tf_op jit(solution)/shard_map/ppermute | solution.py:990
  72.4 36.9 %collective-permute-start.4 = (bf16[1,196,768]{2,1,0:T(8,128)(2,1)}, bf16[1,196,768]{2,1,0:T(8,128)(2,1)}, u32[]{:S(2)}, u32[]{:S(2)}) collective-permute-start(bf16[1,196,768]{2,1,0:T(8,128)(2,1)} %get-tuple-element.270), channel_id=1, source_target_pairs={{16,0},{17,1},{18,2},{19,3},{20,4},{21,5},{22,6},{23,7},{24,8},{25... | collective-permute-start | bytes 903176 | tf_op jit(solution)/shard_map/ppermute | solution.py:990
  136.1 32.3 %collective-permute-start.7 = (bf16[768,768]{1,0:T(8,128)(2,1)}, bf16[768,768]{1,0:T(8,128)(2,1)}, u32[]{:S(2)}, u32[]{:S(2)}) collective-permute-start(bf16[768,768]{1,0:T(8,128)(2,1)} %get-tuple-element.278), channel_id=1, source_target_pairs={{0,2},{2,0},{4,6},{6,4},{8,10},{10,8},{12,14},{14,12},{1,3},{3,1},... | collective-permute-start | bytes 3538952 | tf_op jit(solution)/shard_map/ppermute | solution.py:780
  168.1 15.5 %collective-permute-start.9 = (bf16[1536,768]{1,0:T(8,128)(2,1)}, bf16[1536,768]{1,0:T(8,128)(2,1)}, u32[]{:S(2)}, u32[]{:S(2)}) collective-permute-start(bf16[1536,768]{1,0:T(8,128)(2,1)} %get-tuple-element.294), channel_id=1, source_target_pairs={{0,1},{1,0},{2,3},{3,2},{4,5},{5,4},{6,7},{7,6},{8,9},{9,8},{10,11... | collective-permute-start | bytes 7077896 | tf_op jit(solution)/shard_map/ppermute | solution.py:780
  171.6 23.7 %collective-permute-start.12 = (bf16[384,768]{1,0:T(8,128)(2,1)}, bf16[384,768]{1,0:T(8,128)(2,1)}, u32[]{:S(2)}, u32[]{:S(2)}) collective-permute-start(bf16[384,768]{1,0:T(8,128)(2,1)} %get-tuple-element.296), channel_id=1, source_target_pairs={{0,4},{2,6},{4,0},{6,2},{8,12},{10,14},{12,8},{14,10},{1,5},{3,7},... | collective-permute-start | bytes 1769480 | tf_op jit(solution)/shard_map/ppermute | solution.py:780
  183.6 84.5 %collective-permute-start.8 = (f32[16,768]{1,0:T(8,128)}, f32[16,768]{1,0:T(8,128)}, u32[]{:S(2)}, u32[]{:S(2)}) collective-permute-start(f32[16,768]{1,0:T(8,128)} %get-tuple-element.303), channel_id=1, source_target_pairs={{0,1},{1,0},{2,3},{3,2},{4,5},{5,4},{6,7},{7,6},{8,9},{9,8},{10,11... | collective-permute-start | bytes 147464 | tf_op jit(solution)/shard_map/ppermute | solution.py:780
  188.6 28.7 %collective-permute-start.10 = (bf16[768,768]{1,0:T(8,128)(2,1)}, bf16[768,768]{1,0:T(8,128)(2,1)}, u32[]{:S(2)}, u32[]{:S(2)}) collective-permute-start(bf16[768,768]{1,0:T(8,128)(2,1)} %get-tuple-element.307), channel_id=1, source_target_pairs={{0,2},{2,0},{4,6},{6,4},{8,10},{10,8},{12,14},{14,12},{1,3},{3,1},... | collective-permute-start | bytes 3538952 | tf_op jit(solution)/shard_map/ppermute | solution.py:780
  197.6 23.4 %collective-permute-start.16 = (bf16[192,768]{1,0:T(8,128)(2,1)}, bf16[192,768]{1,0:T(8,128)(2,1)}, u32[]{:S(2)}, u32[]{:S(2)}) collective-permute-start(bf16[192,768]{1,0:T(8,128)(2,1)} %get-tuple-element.315), channel_id=1, source_target_pairs={{0,8},{2,10},{4,12},{6,14},{8,0},{10,2},{12,4},{14,6},{1,9},{3,11}... | collective-permute-start | bytes 884744 | tf_op jit(solution)/shard_map/ppermute | solution.py:780
  204.5 28.7 %collective-permute-start.15 = (bf16[384,768]{1,0:T(8,128)(2,1)}, bf16[384,768]{1,0:T(8,128)(2,1)}, u32[]{:S(2)}, u32[]{:S(2)}) collective-permute-start(bf16[384,768]{1,0:T(8,128)(2,1)} %get-tuple-element.317), channel_id=1, source_target_pairs={{0,4},{2,6},{4,0},{6,2},{8,12},{10,14},{12,8},{14,10},{1,5},{3,7},... | collective-permute-start | bytes 1769480 | tf_op jit(solution)/shard_map/ppermute | solution.py:780
  211.2 26.0 %collective-permute-start.14 = (bf16[768,768]{1,0:T(8,128)(2,1)}, bf16[768,768]{1,0:T(8,128)(2,1)}, u32[]{:S(2)}, u32[]{:S(2)}) collective-permute-start(bf16[768,768]{1,0:T(8,128)(2,1)} %get-tuple-element.320), channel_id=1, source_target_pairs={{0,1},{1,0},{2,3},{3,2},{4,5},{5,4},{6,7},{7,6},{8,9},{9,8},{10,11... | collective-permute-start | bytes 3538952 | tf_op jit(solution)/shard_map/ppermute | solution.py:780
  220.5 24.8 %collective-permute-start.13 = (bf16[384,768]{1,0:T(8,128)(2,1)}, bf16[384,768]{1,0:T(8,128)(2,1)}, u32[]{:S(2)}, u32[]{:S(2)}) collective-permute-start(bf16[384,768]{1,0:T(8,128)(2,1)} %get-tuple-element.323), channel_id=1, source_target_pairs={{0,4},{2,6},{4,0},{6,2},{8,12},{10,14},{12,8},{14,10},{1,5},{3,7},... | collective-permute-start | bytes 1769480 | tf_op jit(solution)/shard_map/ppermute | solution.py:780
  223.0 29.7 %collective-permute-start.19 = (bf16[192,768]{1,0:T(8,128)(2,1)}, bf16[192,768]{1,0:T(8,128)(2,1)}, u32[]{:S(2)}, u32[]{:S(2)}) collective-permute-start(bf16[192,768]{1,0:T(8,128)(2,1)} %summed.4.mine_ref), channel_id=1, source_target_pairs={{0,8},{2,10},{4,12},{6,14},{8,0},{10,2},{12,4},{14,6},{1,9},{3,11}... | collective-permute-start | bytes 884744 | tf_op jit(solution)/shard_map/ppermute | solution.py:780
  240.4 15.9 %collective-permute-start.18 = (bf16[384,768]{1,0:T(8,128)(2,1)}, bf16[384,768]{1,0:T(8,128)(2,1)}, u32[]{:S(2)}, u32[]{:S(2)}) collective-permute-start(bf16[384,768]{1,0:T(8,128)(2,1)} %get-tuple-element.331), channel_id=1, source_target_pairs={{0,2},{2,0},{4,6},{6,4},{8,10},{10,8},{12,14},{14,12},{1,3},{3,1},... | collective-permute-start | bytes 1769480 | tf_op jit(solution)/shard_map/ppermute | solution.py:780
  247.7 18.4 %collective-permute-start.17 = (bf16[192,768]{1,0:T(8,128)(2,1)}, bf16[192,768]{1,0:T(8,128)(2,1)}, u32[]{:S(2)}, u32[]{:S(2)}) collective-permute-start(bf16[192,768]{1,0:T(8,128)(2,1)} %get-tuple-element.334), channel_id=1, source_target_pairs={{0,8},{2,10},{4,12},{6,14},{8,0},{10,2},{12,4},{14,6},{1,9},{3,11}... | collective-permute-start | bytes 884744 | tf_op jit(solution)/shard_map/ppermute | solution.py:780
  249.8 43.6 %collective-permute-start.23 = (bf16[96,768]{1,0:T(8,128)(2,1)}, bf16[96,768]{1,0:T(8,128)(2,1)}, u32[]{:S(2)}, u32[]{:S(2)}) collective-permute-start(bf16[96,768]{1,0:T(8,128)(2,1)} %get-tuple-element.338), channel_id=1, source_target_pairs={{0,8},{2,10},{4,12},{6,14},{8,0},{10,2},{12,4},{14,6},{1,9},{3,11}... | collective-permute-start | bytes 442376 | tf_op jit(solution)/shard_map/ppermute | solution.py:780
  254.7 32.2 %collective-permute-start.25 = (bf16[384,768]{1,0:T(8,128)(2,1)}, bf16[384,768]{1,0:T(8,128)(2,1)}, u32[]{:S(2)}, u32[]{:S(2)}) collective-permute-start(bf16[384,768]{1,0:T(8,128)(2,1)} %joined_4.4.mine_ref), channel_id=1, source_target_pairs={{0,4},{2,6},{4,0},{6,2},{8,12},{10,14},{12,8},{14,10},{1,5},{3,7},... | collective-permute-start | bytes 1769480 | tf_op jit(solution)/shard_map/ppermute | solution.py:780
  258.7 32.6 %collective-permute-start.24 = (bf16[192,768]{1,0:T(8,128)(2,1)}, bf16[192,768]{1,0:T(8,128)(2,1)}, u32[]{:S(2)}, u32[]{:S(2)}) collective-permute-start(bf16[192,768]{1,0:T(8,128)(2,1)} %get-tuple-element.341), channel_id=1, source_target_pairs={{0,4},{2,6},{4,0},{6,2},{8,12},{10,14},{12,8},{14,10},{1,5},{3,7},... | collective-permute-start | bytes 884744 | tf_op jit(solution)/shard_map/ppermute | solution.py:780
  268.0 30.0 %collective-permute-start.22 = (bf16[192,768]{1,0:T(8,128)(2,1)}, bf16[192,768]{1,0:T(8,128)(2,1)}, u32[]{:S(2)}, u32[]{:S(2)}) collective-permute-start(bf16[192,768]{1,0:T(8,128)(2,1)} %summed.5.mine_ref), channel_id=1, source_target_pairs={{0,8},{2,10},{4,12},{6,14},{8,0},{10,2},{12,4},{14,6},{1,9},{3,11}... | collective-permute-start | bytes 884744 | tf_op jit(solution)/shard_map/ppermute | solution.py:780
  269.6 30.5 %collective-permute-start.21 = (f32[16,768]{1,0:T(8,128)}, f32[16,768]{1,0:T(8,128)}, u32[]{:S(2)}, u32[]{:S(2)}) collective-permute-start(f32[16,768]{1,0:T(8,128)} %add.12), channel_id=1, source_target_pairs={{0,2},{2,0},{4,6},{6,4},{8,10},{10,8},{12,14},{14,12},{1,3},{3,1},... | collective-permute-start | bytes 147464 | tf_op jit(solution)/shard_map/ppermute | solution.py:780
  289.1 43.5 %collective-permute-start.32 = (bf16[768,768]{1,0:T(8,128)(2,1)}, bf16[768,768]{1,0:T(8,128)(2,1)}, u32[]{:S(2)}, u32[]{:S(2)}) collective-permute-start(bf16[768,768]{1,0:T(8,128)(2,1)} %joined_2.4.mine_ref), channel_id=1, source_target_pairs={{0,2},{2,0},{4,6},{6,4},{8,10},{10,8},{12,14},{14,12},{1,3},{3,1},... | collective-permute-start | bytes 3538952 | tf_op jit(solution)/shard_map/ppermute | solution.py:780
  299.9 23.0 %collective-permute-start.29 = (bf16[384,768]{1,0:T(8,128)(2,1)}, bf16[384,768]{1,0:T(8,128)(2,1)}, u32[]{:S(2)}, u32[]{:S(2)}) collective-permute-start(bf16[384,768]{1,0:T(8,128)(2,1)} %joined_4.5.mine_ref), channel_id=1, source_target_pairs={{0,4},{2,6},{4,0},{6,2},{8,12},{10,14},{12,8},{14,10},{1,5},{3,7},... | collective-permute-start | bytes 1769480 | tf_op jit(solution)/shard_map/ppermute | solution.py:780
  301.5 39.8 %collective-permute-start.26 = (f32[16,768]{1,0:T(8,128)}, f32[16,768]{1,0:T(8,128)}, u32[]{:S(2)}, u32[]{:S(2)}) collective-permute-start(f32[16,768]{1,0:T(8,128)} %add.13), channel_id=1, source_target_pairs={{0,4},{2,6},{4,0},{6,2},{8,12},{10,14},{12,8},{14,10},{1,5},{3,7},... | collective-permute-start | bytes 147464 | tf_op jit(solution)/shard_map/ppermute | solution.py:780
  305.9 20.9 %collective-permute-start.28 = (bf16[96,768]{1,0:T(8,128)(2,1)}, bf16[96,768]{1,0:T(8,128)(2,1)}, u32[]{:S(2)}, u32[]{:S(2)}) collective-permute-start(bf16[96,768]{1,0:T(8,128)(2,1)} %summed.7.mine_ref), channel_id=1, source_target_pairs={{0,8},{2,10},{4,12},{6,14},{8,0},{10,2},{12,4},{14,6},{1,9},{3,11}... | collective-permute-start | bytes 442376 | tf_op jit(solution)/shard_map/ppermute | solution.py:780
  308.8 19.8 %collective-permute-start.33 = (bf16[192,768]{1,0:T(8,128)(2,1)}, bf16[192,768]{1,0:T(8,128)(2,1)}, u32[]{:S(2)}, u32[]{:S(2)}) collective-permute-start(bf16[192,768]{1,0:T(8,128)(2,1)} %joined_4.6.mine_ref), channel_id=1, source_target_pairs={{0,2},{2,0},{4,6},{6,4},{8,10},{10,8},{12,14},{14,12},{1,3},{3,1},... | collective-permute-start | bytes 884744 | tf_op jit(solution)/shard_map/ppermute | solution.py:780
  325.2 29.3 %collective-permute-start.35 = (bf16[768,768]{1,0:T(8,128)(2,1)}, bf16[768,768]{1,0:T(8,128)(2,1)}, u32[]{:S(2)}, u32[]{:S(2)}) collective-permute-start(bf16[768,768]{1,0:T(8,128)(2,1)} %joined_2.5.mine_ref), channel_id=1, source_target_pairs={{0,2},{2,0},{4,6},{6,4},{8,10},{10,8},{12,14},{14,12},{1,3},{3,1},... | collective-permute-start | bytes 3538952 | tf_op jit(solution)/shard_map/ppermute | solution.py:780
  330.6 20.5 %collective-permute-start.36 = (bf16[384,768]{1,0:T(8,128)(2,1)}, bf16[384,768]{1,0:T(8,128)(2,1)}, u32[]{:S(2)}, u32[]{:S(2)}) collective-permute-start(bf16[384,768]{1,0:T(8,128)(2,1)} %joined_1.4.mine_ref), channel_id=1, source_target_pairs={{0,4},{2,6},{4,0},{6,2},{8,12},{10,14},{12,8},{14,10},{1,5},{3,7},... | collective-permute-start | bytes 1769480 | tf_op jit(solution)/shard_map/ppermute | solution.py:780
  340.8 24.4 %collective-permute-start.38 = (bf16[384,768]{1,0:T(8,128)(2,1)}, bf16[384,768]{1,0:T(8,128)(2,1)}, u32[]{:S(2)}, u32[]{:S(2)}) collective-permute-start(bf16[384,768]{1,0:T(8,128)(2,1)} %joined_2.6.mine_ref), channel_id=1, source_target_pairs={{0,2},{2,0},{4,6},{6,4},{8,10},{10,8},{12,14},{14,12},{1,3},{3,1},... | collective-permute-start | bytes 1769480 | tf_op jit(solution)/shard_map/ppermute | solution.py:780
  342.8 14.9 %collective-permute-start.34 = (f32[16,768]{1,0:T(8,128)}, f32[16,768]{1,0:T(8,128)}, u32[]{:S(2)}, u32[]{:S(2)}) collective-permute-start(f32[16,768]{1,0:T(8,128)} %add.14), channel_id=1, source_target_pairs={{0,8},{2,10},{4,12},{6,14},{8,0},{10,2},{12,4},{14,6},{1,9},{3,11}... | collective-permute-start | bytes 147464 | tf_op jit(solution)/shard_map/ppermute | solution.py:780
  (17 other events, 110.3 us)

commit v3 on v2

--- a/solution.py
+++ b/solution.py
@@ -30,7 +30,7 @@
 WEIGHTS = range(19, 23)
 W_QKV, W_OUT, W_UP, W_DOWN = WEIGHTS
 DOWN, UP, QUERY_VALUE, KEY_OUT, SUMS, OUT = range(100, 106)
-ORDER = "FAGFdAFUdAuQdqKudqkuqdkusdkquskqukqdksdqusqkuk"
+ORDER = "FAGFUduAQduqdKukdqukqdskuqdkqskuqkdsdquqkusk"
 COST = 10**11
 ANY = pl.BlockSpec(memory_space=pl.ANY)
 
@@ -283,7 +283,7 @@
     return Copies(sem, {name: found[name] for name in order}), dict(zip(WEIGHTS, local))
 
 
-def call(kernel, steps, scalars, ins, in_specs, outs, out_specs, scratch, name, aliases=None):
+def call(kernel, steps, scalars, ins, in_specs, outs, out_specs, scratch, name, aliases=None, room=60):
     return pl.pallas_call(
         kernel,
         out_shape=outs,
@@ -295,7 +295,7 @@
             scratch_shapes=scratch,
         ),
         compiler_params=pltpu.CompilerParams(
-            dimension_semantics=("arbitrary",), vmem_limit_bytes=60 << 20
+            dimension_semantics=("arbitrary",), vmem_limit_bytes=room << 20
         ),
         input_output_aliases=aliases or {},
         cost_estimate=pl.CostEstimate(flops=COST, bytes_accessed=COST, transcendentals=0),
@@ -397,49 +397,134 @@
     return carry, output
 
 
-def middle(image, saved, made, sums, count, received, cotangent, vectors, weights):
-    images, slots, width = cotangent.shape
+def tick(first, image, late, saved, made, output, sums, scalars, index, received, source, vectors, weights):
+    images, slots, width = source.shape
     rows, hidden = padded_rows(slots), weights[2].shape[1]
     shapes = image_shapes(slots, rows, width, hidden)
-    carry = SAVED + MADE
+    carry = SAVED + MADE + (Y,)
     lines = -(-(len(vectors) - 1 + hidden // width) // 8) * 8
     work = (E, GD, GR, GO, GA, GU) + carry
-    old = tuple(saved) + (() if made is None else tuple(made) + (sums,))
-    at = 1 + 2 + len(vectors) + 4
-
-    def kernel(count_ref, received_ref, e_ref, *rest):
-        vecs, hbm, previous, places, sums_ref, grad_ref, local, sem, scratch, out_sem = split(
+    old = tuple(saved) + (() if made is None else tuple(made)) + (output,) + (() if made is None else (sums,))
+    slots_of = [k for k, name in enumerate(carry) if made is not None or name not in MADE]
+    slots_of += [] if made is None else [len(carry)]
+    at = 1 + 3 + len(vectors) + 4
+    other = first if first is not None else late if late is not None else image
+
+    def kernel(scalar_ref, index_ref, received_ref, source_ref, *rest):
+        vecs, hbm, previous, places, sums_ref, send_ref, local, sem, scratch, out_sem = split(
             rest, len(vectors), 4, len(old), len(carry), None, None, 4, None, len(work), None
         )
         sums_ref[...] = jnp.zeros(sums_ref.shape, f32) if made is None else previous[-1][...]
-
-        @pl.when(jnp.logical_not(first_section()))
+        early = first_section()
+        later = jnp.logical_not(early)
+        here = jnp.where(early, other, image)
+        live = scalar_ref[here]
+        refs = dict(zip(work, scratch))
+        place = {name: ref.at[here] for name, ref in zip(carry, places)}
+        store = Copies(out_sem, {name: (refs[name], place[name]) for name in carry})
+        vec, add = vector_reader(vecs), vector_adder(sums_ref)
+
+        def gathered():
+            pad_rows(refs[E], source_ref)
+            chosen = gather_matrix(index_ref[first : first + 1, :], live)
+            refs[U][:slots, :] = product(chosen, refs[E][...], TN).astype(bf16)
+            refs[U][slots:, :] = jnp.zeros((rows - slots, width), bf16)
+
+        def forward(fetch, near):
+            forward_part(refs, fetch.wait, store.start, vec, near, live)
+            fetch.wait(W_DOWN)
+
+        def backward(near):
+            feed_forward_back(refs, nothing, store.start, vec, near, live, add)
+            attention_back(refs, nothing, store.start, vec, near, live, add)
+
+        def sent():
+            refs[GRAD][...] = refs[GU][:slots, :]
+            store.start(GRAD)
+            send_ref[...] = refs[GU][:slots, :]
+
+        if first is not None:
+            fetch, near = fetch_weights(sem, hbm, local)
+            fetch.start()
+
+            @pl.when(early)
+            def _():
+                gathered()
+
+            @pl.when(later)
+            def _():
+                pad_rows(refs[U], received_ref)
+
+            forward(fetch, near)
+
+            @pl.when(early)
+            def _():
+                output_part(refs, vec, near, live)
+                store.start(Y)
+                send_ref[...] = refs[Y][...]
+                Copies(out_sem, {name: (refs[name], place[name]) for name in carry}).wait(*SAVED, Y)
+
+            @pl.when(later)
+            def _():
+                pad_rows(refs[E], source_ref)
+                backward(near)
+                sent()
+                Copies(out_sem, {name: (refs[name], place[name]) for name in carry}).wait(*SAVED, *MADE)
+
+            return
+
+        @pl.when(later)
         def _():
             fetch, near = fetch_weights(sem, hbm, local)
             fetch.start()
-            live = count_ref[image]
-            refs = dict(zip(work, scratch))
-            store = Copies(
-                out_sem, {name: (refs[name], place.at[image]) for name, place in zip(carry, places)}
-            )
             pad_rows(refs[U], received_ref)
-            pad_rows(refs[E], e_ref)
-            vec, add = vector_reader(vecs), vector_adder(sums_ref)
-            forward_part(refs, fetch.wait, store.start, vec, near, live)
-            fetch.wait(W_DOWN)
-            feed_forward_back(refs, nothing, store.start, vec, near, live, add)
-            attention_back(refs, nothing, store.start, vec, near, live, add)
-            refs[GRAD][...] = refs[GU][:slots, :]
+            pad_rows(refs[E], source_ref)
+            forward(fetch, near)
+            if late is None:
+                backward(near)
+                sent()
+                store.wait(*SAVED, *MADE)
+
+        if late is None:
+            return
+
+        @pl.when(early)
+        def _():
+            fetch, _ = fetch_weights(sem, hbm, local, (W_DOWN, W_UP, W_OUT, W_QKV))
+            load = Copies(out_sem, {name: (place[name], refs[name]) for name in (SLOPE, R, QKV, U)})
+            fetch.start()
+            load.start()
+            pad_rows(refs[E], received_ref)
+            fetch.wait()
+            load.wait()
+
+        backward(dict(zip(WEIGHTS, local)))
+
+        @pl.when(early)
+        def _():
+            chosen = gather_matrix(index_ref[late : late + 1, :], live)
+            refs[GRAD][...] = product(chosen, refs[GU][:slots, :], NN)[:slots, :].astype(bf16)
             store.start(GRAD)
-            grad_ref[...] = refs[GU][:slots, :]
-            store.wait()
+
+        @pl.when(later)
+        def _():
+            sent()
+            Copies(out_sem, {name: (refs[name], place[name]) for name in SAVED}).wait()
+
+        store.wait(*MADE)
 
     results = call(
         kernel,
         1,
-        count,
-        (received, cotangent) + vectors + weights + old,
-        [image_block((slots, width), 0), image_block((slots, width), image)]
+        scalars,
+        (index, received, source) + vectors + weights + old,
+        [
+            fixed_block(index.shape),
+            image_block((slots, width), 0),
+            pl.BlockSpec(
+                (pl.Squeezed(), slots, width), lambda i, s: (jnp.where(s[images] == 0, other, image), 0, 0)
+            ),
+        ]
         + [fixed_block(vector.shape) for vector in vectors]
         + [ANY] * (4 + len(old) - (made is not None))
         + ([] if made is None else [fixed_block(sums.shape)]),
@@ -449,13 +534,14 @@
         weight_scratch(weights)
         + [pltpu.VMEM(*shapes[name]) for name in work]
         + [pltpu.SemaphoreType.DMA((len(carry),))],
-        f"middle_{image}",
-        {at + k: k for k in range(len(old))},
+        f"tick_{image}",
+        {at + k: slot for k, slot in enumerate(slots_of)},
     )
-    return results[: len(SAVED)], results[len(SAVED) : -2], results[-2], results[-1]
-
-
-def late_feed_forward(image, saved, made, output, sums, count, received, vectors, weights):
+    saved, made = results[: len(SAVED)], results[len(SAVED) : len(SAVED) + len(MADE)]
+    return saved, made, results[-3], results[-2], results[-1]
+
+
+def late_feed_forward(image, outputs, saved, made, output, sums, count, received, vectors, weights):
     images, rows, hidden = saved[SAVED.index(M)].shape
     slots, width = received.shape[1:]
     shapes = image_shapes(slots, rows, width, hidden)
@@ -485,6 +571,7 @@
             fetch = Copies(
                 sem,
                 {
+                    E: (received_ref.at[0], refs[Y]),
                     W_DOWN: (far[W_DOWN], near[W_DOWN]),
                     SLOPE: (source[SLOPE], refs[SLOPE]),
                     W_UP: (far[W_UP], near[W_UP]),
@@ -492,27 +579,28 @@
                 },
             )
             fetch.start()
-            store = Copies(sem.at[pl.ds(4, 2)], {name: (refs[name], place[name]) for name in (GZ, GB)})
-            pad_rows(refs[E], received_ref)
+            store = Copies(sem.at[pl.ds(5, 2)], {name: (refs[name], place[name]) for name in (GZ, GB)})
+            fetch.wait(E)
+            pad_rows(refs[E], refs[Y])
             feed_forward_back(refs, fetch.wait, store.start, vec, near, live, vector_adder(sums_ref))
             store.wait()
 
         @pl.when(jnp.logical_not(early))
         def _():
-            fetch = Copies(
-                sem,
-                {
-                    M: (source[M], refs[M]),
-                    W_DOWN: (far[W_DOWN], near[W_DOWN]),
-                    R: (source[R], refs[R]),
-                },
-            )
+            fetch = Copies(sem, {W_DOWN: (far[W_DOWN], near[W_DOWN])})
             fetch.start()
-            fetch.wait()
-            output_part(refs, vec, near, live)
-            store = Copies(sem.at[pl.ds(4, 1)], {Y: (refs[Y], place[Y])})
-            store.start()
-            store.wait()
+            for which in outputs:
+                load = Copies(
+                    sem.at[pl.ds(1, 2)],
+                    {name: (sources[loads.index(name)].at[which], refs[name]) for name in (R, M)},
+                )
+                load.start()
+                fetch.wait()
+                load.wait()
+                output_part(refs, vec, near, count_ref[which])
+                store = Copies(sem.at[pl.ds(4, 1)], {Y: (refs[Y], places[stores.index(Y)].at[which])})
+                store.start()
+                store.wait()
 
     gz, gb, output, sums, gr = call(
         kernel,
@@ -523,7 +611,7 @@
         + tuple(saved[SAVED.index(name)] for name in loads)
         + tuple(weights[WEIGHTS.index(name)] for name in near_names)
         + tuple(old),
-        [image_block((slots, width), 0)]
+        [ANY]
         + [fixed_block(vector.shape) for vector in vectors]
         + [ANY] * (len(loads) + len(near_names) + len(old) - 1)
         + [fixed_block(sums.shape)],
@@ -645,7 +733,7 @@
 
             @pl.when(here & (step >= half))
             def _():
-                keep_ref[...] = product(refs[left][...], refs[right][...], TN)
+                keep_ref[...] = product(refs[left][...], refs[right][...], TN).astype(bf16)
 
     def columns(at):
         table = [column if right == at else 0 for _, right, column in blocks]
@@ -657,13 +745,14 @@
         side,
         arrays,
         [columns(at) for at in range(len(arrays))],
-        [jax.ShapeDtypeStruct((half * width, width), bf16), jax.ShapeDtypeStruct((half * width, width), f32)],
+        [jax.ShapeDtypeStruct((half * width, width), bf16)] * 2,
         [
             pl.BlockSpec((width, width), lambda i, s: (jnp.minimum(i, half - 1), 0)),
             pl.BlockSpec((width, width), lambda i, s: (jnp.maximum(i - half, 0), 0)),
         ],
         [],
         name,
+        room=60,
     )
 
 
@@ -699,7 +788,7 @@
 
         @pl.when(step >= half)
         def _():
-            keep_ref[...] = product(left, gd_ref[...], TN)
+            keep_ref[...] = product(left, gd_ref[...], TN).astype(bf16)
 
     return call(
         kernel,
@@ -711,77 +800,15 @@
             fixed_block(cotangent.shape),
         ]
         + [image_block((slots, width), 0)] * images,
-        [jax.ShapeDtypeStruct((half * width, width), bf16), jax.ShapeDtypeStruct((half * width, width), f32)],
+        [jax.ShapeDtypeStruct((half * width, width), bf16)] * 2,
         [
             pl.BlockSpec((width, width), lambda i, s: (jnp.minimum(i, half - 1), 0)),
             pl.BlockSpec((width, width), lambda i, s: (jnp.maximum(i - half, 0), 0)),
         ],
         [pltpu.VMEM((images * rows, width), bf16)],
         "grad_down",
+        room=60,
     )
-
-
-def assembled(side, mine, other, places, shapes, name, before=None):
-    width = mine.shape[1]
-    half = mine.shape[0] // width
-    before = before or {}
-
-    def chosen(i, scalar_ref):
-        bit = scalar_ref[0]
-        return jnp.where(i < half, bit * half + i, (1 - bit) * half + i - half)
-
-    def kernel(scalar_ref, mine_ref, other_ref, *refs):
-        outs = refs[len(before) :]
-        step = pl.program_id(0)
-        block = chosen(step, scalar_ref)
-        for at, out_ref in enumerate(outs):
-            here = functools.reduce(
-                jnp.logical_or, [block == k for k, entry in enumerate(places) if entry[0] == at]
-            )
-
-            @pl.when(here & (step < half))
-            def _():
-                out_ref[...] = mine_ref[...].astype(f32)
-
-            @pl.when(here & (step >= half))
-            def _():
-                out_ref[...] = other_ref[...].astype(f32)
-
-    def place(at):
-        last = [entry for entry in places if entry[0] == at][0]
-        entries = [entry if entry[0] == at else last for entry in places]
-
-        def index(i, s):
-            block = chosen(i, s)
-            return (pick([entry[1] for entry in entries], block), pick([entry[2] for entry in entries], block))
-
-        return index
-
-    return call(
-        kernel,
-        2 * half,
-        side,
-        (mine, other) + tuple(before.values()),
-        [
-            pl.BlockSpec((width, width), lambda i, s: (jnp.minimum(i, half - 1), 0)),
-            pl.BlockSpec((width, width), lambda i, s: (jnp.maximum(i - half, 0), 0)),
-        ]
-        + [ANY] * len(before),
-        [jax.ShapeDtypeStruct(shape, f32) for shape in shapes],
-        [pl.BlockSpec((width, width), place(at)) for at in range(len(shapes))],
-        [],
-        name,
-        {3 + k: at for k, at in enumerate(before)},
-    )
-
-
-def swapped(value, axis, stride):
-    length = lax.axis_size(axis)
-    return lax.ppermute(value, axis, [(i, i ^ stride) for i in range(length)])
-
-
-def bit_of(axis, stride):
-    return (lax.axis_index(axis) // stride) % 2
 
 
 def plain_call(kernel, ins, outs, scratch, name):
@@ -791,18 +818,71 @@
         in_specs=[ANY] * len(ins),
         out_specs=[pl.BlockSpec(memory_space=pltpu.VMEM)] * len(outs),
         scratch_shapes=scratch,
-        compiler_params=pltpu.CompilerParams(vmem_limit_bytes=60 << 20),
+        compiler_params=pltpu.CompilerParams(vmem_limit_bytes=16 << 20),
         cost_estimate=pl.CostEstimate(flops=COST, bytes_accessed=COST, transcendentals=0),
         name=name,
     )(*ins)
+
+
+def assembled(own, stride, pieces, places, shapes, before):
+    shape = pieces[0].shape
+
+    def kernel(*refs):
+        sources, _, outs, (raw, wide, sem) = split(refs, 2, len(before), len(shapes), 3)
+        core = lax.axis_index(REP) if own else 1 - lax.axis_index(REP)
+        near = bit_of(DP, stride)
+        loads = [pltpu.make_async_copy(source, raw.at[k], sem.at[k]) for k, source in enumerate(sources)]
+        for load in loads:
+            load.start()
+
+        def stores(k, act):
+            block = 2 * core + (near if k == 0 else 1 - near)
+            for at, (which, row, column) in enumerate(places):
+                rows, columns = pl.ds(row * shape[0], shape[0]), pl.ds(column * shape[1], shape[1])
+
+                @pl.when(block == at)
+                def _():
+                    act(pltpu.make_async_copy(wide.at[k], outs[which].at[rows, columns], sem.at[2 + k]))
+
+        for k in range(2):
+            loads[k].wait()
+            wide[k] = raw[k].astype(f32)
+            stores(k, lambda copy: copy.start())
+        for k in range(2):
+            stores(k, lambda copy: copy.wait())
+
+    return pl.pallas_call(
+        kernel,
+        out_shape=[jax.ShapeDtypeStruct(whole, f32) for whole in shapes],
+        in_specs=[ANY] * (2 + len(before)),
+        out_specs=[ANY] * len(shapes),
+        scratch_shapes=[
+            pltpu.VMEM((2,) + shape, bf16),
+            pltpu.VMEM((2,) + shape, f32),
+            pltpu.SemaphoreType.DMA((4,)),
+        ],
+        input_output_aliases={2 + k: k for k in range(len(before))},
+        compiler_params=pltpu.CompilerParams(vmem_limit_bytes=16 << 20),
+        cost_estimate=pl.CostEstimate(flops=COST, bytes_accessed=COST, transcendentals=0),
+        name="assembled",
+    )(*pieces, *before)
+
+
+def swapped(value, axis, stride):
+    length = lax.axis_size(axis)
+    return lax.ppermute(value, axis, [(i, i ^ stride) for i in range(length)])
+
+
+def bit_of(axis, stride):
+    return (lax.axis_index(axis) // stride) % 2
 
 
 def halved(keep, coming, stride):
     height, width = keep.shape[0] // 2, keep.shape[1]
     if height % ROW_TILE:
         bit = bit_of(DP, stride)
-        pair = keep + coming.astype(f32)
-        send = lax.dynamic_slice_in_dim(pair, (1 - bit) * height, height, axis=0).astype(bf16)
+        pair = (keep.astype(f32) + coming.astype(f32)).astype(bf16)
+        send = lax.dynamic_slice_in_dim(pair, (1 - bit) * height, height, axis=0)
         return send, lax.dynamic_slice_in_dim(pair, bit * height, height, axis=0)
 
     def kernel(keep_ref, coming_ref, send_ref, stay_ref, kept, came, sem):
@@ -816,18 +896,18 @@
             copy.start()
         for copy in copies[:2]:
             copy.wait()
-        send_ref[...] = (kept[0] + came[0].astype(f32)).astype(bf16)
+        send_ref[...] = (kept[0].astype(f32) + came[0].astype(f32)).astype(bf16)
         for copy in copies[2:]:
             copy.wait()
-        stay_ref[...] = kept[1] + came[1].astype(f32)
+        stay_ref[...] = (kept[1].astype(f32) + came[1].astype(f32)).astype(bf16)
 
     shape = (height, width)
     return plain_call(
         kernel,
         (keep, coming),
-        [jax.ShapeDtypeStruct(shape, bf16), jax.ShapeDtypeStruct(shape, f32)],
+        [jax.ShapeDtypeStruct(shape, bf16)] * 2,
         [
-            pltpu.VMEM((2,) + shape, f32),
+            pltpu.VMEM((2,) + shape, bf16),
             pltpu.VMEM((2,) + shape, bf16),
             pltpu.SemaphoreType.DMA((4,)),
         ],
@@ -837,7 +917,7 @@
 
 def summed(keep, coming, total):
     if keep.shape[0] % ROW_TILE:
-        return ((keep + coming.astype(f32)) / total).astype(bf16)
+        return ((keep.astype(f32) + coming.astype(f32)) / total).astype(bf16)
 
     def kernel(keep_ref, coming_ref, out_ref, kept, came, sem):
         copies = [
@@ -848,13 +928,13 @@
             copy.start()
         for copy in copies:
             copy.wait()
-        out_ref[...] = ((kept[...] + came[...].astype(f32)) / total).astype(bf16)
+        out_ref[...] = ((kept[...].astype(f32) + came[...].astype(f32)) / total).astype(bf16)
 
     return plain_call(
         kernel,
         (keep, coming),
         [jax.ShapeDtypeStruct(keep.shape, bf16)],
-        [pltpu.VMEM(keep.shape, f32), pltpu.VMEM(keep.shape, bf16), pltpu.SemaphoreType.DMA((2,))],
+        [pltpu.VMEM(keep.shape, bf16), pltpu.VMEM(keep.shape, bf16), pltpu.SemaphoreType.DMA((2,))],
         "summed",
     )[0]
 
@@ -905,7 +985,7 @@
 class Exchange:
     def __init__(self, line, send, keep, strides, total):
         self.line, self.keep, self.strides, self.total = line, keep, strides, total
-        self.at, self.value, self.result = 0, None, None
+        self.at, self.half = 0, None
         self.coming = swapped(send, REP, 1)
 
     def advance(self):
@@ -920,34 +1000,43 @@
             self.value = summed(self.keep, coming, self.total)
             self.coming = swapped(self.value, DP, self.strides[-1])
             self.line.passed(self.value)
-        elif self.at <= 2 * count:
-            stride = self.strides[2 * count - self.at]
-            self.value = joined(self.value, coming, stride)
-            if self.at < 2 * count:
-                self.coming = swapped(self.value, DP, self.strides[2 * count - 1 - self.at])
-            else:
-                self.coming = swapped(self.value, REP, 1)
+        elif self.at < 2 * count:
+            self.value = joined(self.value, coming, self.strides[2 * count - self.at])
+            self.coming = swapped(self.value, DP, self.strides[2 * count - 1 - self.at])
             self.line.passed(self.value)
+        elif self.at == 2 * count:
+            self.half = (self.value, coming)
+            self.others = swapped(lax.optimization_barrier(self.half)[0], REP, 1)
+            self.coming = swapped(coming, REP, 1)
         else:
-            self.result = (self.value, coming)
-            self.line.passed(coming)
+            self.half = (self.others, coming)
         self.at += 1
 
 
+def added(value, coming):
+    def kernel(value_ref, coming_ref, out_ref):
+        out_ref[...] = value_ref[...] + coming_ref[...]
+
+    return pl.pallas_call(
+        kernel,
+        out_shape=jax.ShapeDtypeStruct(value.shape, value.dtype),
+        cost_estimate=pl.CostEstimate(flops=COST, bytes_accessed=COST, transcendentals=0),
+        name="added",
+    )(value, coming)
+
+
 class Total:
-    def __init__(self, line, value, strides, total):
-        self.line, self.value, self.total = line, value, total
+    def __init__(self, line, value, strides):
+        self.line, self.value = line, value
         self.partners = [(REP, 1)] + [(DP, stride) for stride in strides]
-        self.at, self.result = 0, None
+        self.at = 0
         self.coming = swapped(value, *self.partners[0])
 
     def advance(self):
-        self.value = self.value + self.line.gate(self.coming)
+        self.value = added(self.value, self.line.gate(self.coming))
         self.at += 1
         if self.at < len(self.partners):
             self.coming = swapped(self.value, *self.partners[self.at])
-        else:
-            self.result = self.value / self.total
         self.line.passed(self.value)
 
 
@@ -977,18 +1066,25 @@
     rows_in = boundary[0]
 
     line = Line()
+    assert images == 3
+    section = lax.axis_index(SECTION).astype(jnp.int32)
+    scalars = jnp.concatenate([keep_count, section[None]])
     carry, received = None, []
-    for image in range(images):
+    for image in range(2):
         carry, first_output = first_forward(image, carry, keep_count, keep_index, rows_in, vectors, weights)
         received.append(lax.ppermute(first_output, SECTION, [(0, 1)]))
     saved, output = carry[:-1], carry[-1]
     made, sums, returned = None, None, []
-    for image in range(images):
-        saved, made, sums, grad_first = middle(
-            image, saved, made, sums, keep_count, received[image], rows_in, vectors, weights
+    for image, first, late in ((0, 2, None), (1, None, None), (2, None, 0)):
+        saved, made, output, sums, sent = tick(
+            first, image, late, saved, made, output, sums, scalars, keep_index, line.gate(received[image]),
+            rows_in, vectors, weights,
         )
-        returned.append(lax.ppermute(grad_first, SECTION, [(1, 0)]))
-    line.passed(grad_first)
+        line.passed(sent)
+        both = [(1, 0)] + ([(0, 1)] if first is not None else [])
+        returned.append(lax.ppermute(sent, SECTION, both))
+        if first is not None:
+            received.append(returned[-1])
 
     def flat(name):
         array = saved[SAVED.index(name)] if name in SAVED else made[MADE.index(name)]
@@ -999,7 +1095,7 @@
     near_first = strides_of(lax.axis_size(DP))
     far_first = near_first[1::-1] + near_first[2:]
     square, many = (width, width), hidden // width
-    forwards, attentions = list(range(images)), list(range(images))
+    forwards, attentions = [1, 2], [1, 2]
     residual = [None] * images
     exchanges, outs = {}, {}
 
@@ -1011,7 +1107,8 @@
         nonlocal made, output, sums
         image = forwards.pop(0)
         made, output, sums, residual[image] = late_feed_forward(
-            image, saved, made, output, sums, line.gate(keep_count), returned[image], vectors, weights
+            image, (0, 1) if image == 1 else (2,), saved, made, output, sums, keep_count, line.gate(returned[image]),
+            vectors, weights,
         )
         line.passed(residual[image])
 
@@ -1019,57 +1116,63 @@
         nonlocal made, sums
         image = attentions.pop(0)
         made, sums = late_attention(
-            image, saved, made, sums, residual[image], line.gate(keep_count), keep_index, vectors, weights
+            image, saved, made, sums, line.gate(residual[image]), keep_count, keep_index, vectors, weights
         )
         line.passed(sums)
 
     def grad_down():
-        pair = down_gradient(line.gate(side), keep_count, saved[SAVED.index(M)], rows_in, returned)
+        pair = down_gradient(side, keep_count, line.gate(saved[SAVED.index(M)]), rows_in, returned)
         begin(DOWN, pair, near_first)
 
     def grad_up():
         blocks = [(0, 1, column) for column in range(many)]
-        begin(UP, weight_gradient(line.gate(side), (flat(C), flat(GZ)), blocks, "grad_up"), near_first)
+        begin(UP, weight_gradient(side, (line.gate(flat(C)), flat(GZ)), blocks, "grad_up"), far_first)
 
     def grad_query_value():
-        exchanges[SUMS] = Total(line, sums, near_first, total)
-        pair = weight_gradient(line.gate(side), (flat(A), flat(GQKV)), [(0, 1, 0), (0, 1, 2)], "grad_query_value")
-        begin(QUERY_VALUE, pair, far_first)
+        exchanges[SUMS] = Total(line, sums, near_first)
+        pair = weight_gradient(side, (line.gate(flat(A)), flat(GQKV)), [(0, 1, 0), (0, 1, 2)], "grad_query_value")
+        begin(QUERY_VALUE, pair, near_first)
 
     def grad_key_out():
-        arrays = (flat(A), flat(GQKV), flat(O), flat(GB))
-        pair = weight_gradient(line.gate(side), arrays, [(0, 1, 1), (2, 3, 0)], "grad_key_out")
+        arrays = (line.gate(flat(A)), flat(GQKV), flat(O), flat(GB))
+        pair = weight_gradient(side, arrays, [(0, 1, 1), (2, 3, 0)], "grad_key_out")
         begin(KEY_OUT, pair, near_first)
 
-    def end(name):
-        places, shapes = {
-            DOWN: ([(0, k, 0) for k in range(many)], [(hidden, width)]),
-            UP: ([(0, 0, k) for k in range(many)], [(width, hidden)]),
-            QUERY_VALUE: ([(0, 0, 0), (0, 0, 2)], [(width, 3 * width)]),
-            KEY_OUT: ([(0, 0, 1), (1, 0, 0)], [(width, 3 * width), square]),
+    def widen(name):
+        places, kinds = {
+            DOWN: ([(0, k, 0) for k in range(many)], {DOWN: (hidden, width)}),
+            UP: ([(0, 0, k) for k in range(many)], {UP: (width, hidden)}),
+            QUERY_VALUE: ([(0, 0, 0), (0, 1, 0), (0, 0, 2), (0, 1, 2)], {QKV: (width, 3 * width)}),
+            KEY_OUT: ([(0, 0, 1), (0, 1, 1), (1, 0, 0), (1, 1, 0)], {QKV: (width, 3 * width), OUT: (width, width)}),
         }[name]
-        part = name in (QUERY_VALUE, KEY_OUT)
-        before = {0: outs[QKV]} if part and QKV in outs else {}
-        mine, other = exchanges[name].result
-        whole = assembled(line.gate(side), mine, other, places, shapes, f"whole_{name}", before)
-        line.passed(whole[0])
-        outs[QKV if part else name] = whole[0]
-        outs.update({OUT: piece for piece in whole[1:]})
+        exchange = exchanges[name]
+        before = [outs[kind] for kind in kinds if kind in outs]
+        first, second = exchange.half
+        wholes = assembled(
+            exchange.at == stages - 1,
+            exchange.strides[0],
+            (first, line.gate(second)),
+            places,
+            list(kinds.values()),
+            before,
+        )
+        line.passed(wholes[0])
+        outs.update(zip(kinds, wholes))
 
     steps = dict(zip("FAGUQK", (feed_forward, attention, grad_down, grad_up, grad_query_value, grad_key_out)))
     transfers = dict(zip("duqks", (DOWN, UP, QUERY_VALUE, KEY_OUT, SUMS)))
     stages = 2 * len(near_first) + 2
-    plain = "FA" * images + "GUQK" + "duqk" * stages + "s" * (stages // 2)
+    plain = "FAFAGUQK" + "duqk" * stages + "s" * (stages // 2)
     for step in ORDER if (images, stages) == (3, 8) else plain:
         if step in steps:
             steps[step]()
             continue
         name = transfers[step]
         exchanges[name].advance()
-        if exchanges[name].result is not None and name != SUMS:
-            end(name)
-    assert all(exchange.result is not None for exchange in exchanges.values())
-    sums = exchanges[SUMS].result
+        if name != SUMS and exchanges[name].half is not None:
+            widen(name)
+    assert all(exchange.at == (stages // 2 if name == SUMS else stages) for name, exchange in exchanges.items())
+    sums = exchanges[SUMS].value / total
     small = [sums[at : at + 1] for at in VECTORS[:-1]]
     return (
         output[None],

time: 387 us -> 343 us (0.89)
  Pallas kernels: 242 us -> 210 us
  waiting for transfers between devices: 75.7 us -> 56 us
  starting transfers between devices: 47.5 us -> 63.3 us
  other arithmetic: 5.73 us -> 1.39 us
    pallas_call x20 -> x13, Pallas kernels: 173 us -> 131 us  [call(): pl.pallas_call(kernel, out_shape=outs, grid_spec=pltpu.PrefetchScalarGrid...]
    pallas_call x0 -> x12, Pallas kernels: none -> 30.7 us  [the longest x8 24.9 us: assembled(): pl.pallas_call(kernel, out_shape=[jax.ShapeDtypeStruct(whole, f32) for wh...]
    pallas_call x28 -> x24, Pallas kernels: 69.5 us -> 47.9 us  [plain_call(): pl.pallas_call(kernel, out_shape=outs, in_specs=[ANY] * len(ins), out_spe...]
    ppermute x36 -> x40, starting transfers between devices: 31.9 us -> 49 us  [swapped(): return lax.ppermute(value, axis, [(i, i ^ stride) for i in range(length)])]
    ppermute x3, waiting for transfers between devices: 13.9 us -> 0.01 us  [shards(): returned.append(lax.ppermute(sent, SECTION, both))]
    ppermute x36 -> x40, waiting for transfers between devices: 61.8 us -> 56 us  [swapped(): return lax.ppermute(value, axis, [(i, i ^ stride) for i in range(length)])]
    add x3 -> x0, other arithmetic: 4.31 us -> none  [advance(): self.value = self.value + self.line.gate(self.coming)]
  transfers between devices with their start and end apart: 42 -> 45, of which waited for: 15 -> 14; matrix products, arithmetic and copies ran while one was open for 2% -> 1% of each run, Pallas kernels for 55% -> 54%
where the time goes in v3:
time: 343 us; the launch traced here: 336 us
  Pallas kernels  210 us (61%)
  starting transfers between devices  63.3 us (18%)
  waiting for transfers between devices  56 us (16%)
  local copies, waits for them, and re-layouts  4.15 us (1%)
    pallas_call x13, Pallas kernels, call(): pl.pallas_call(kernel, out_shape=outs, grid_spec=pltpu.PrefetchScalarGrid...  131 us
    ppermute x40, waiting for transfers between devices, swapped(): return lax.ppermute(value, axis, [(i, i ^ stride) for i in range(length)])  56 us
    ppermute x40, starting transfers between devices, swapped(): return lax.ppermute(value, axis, [(i, i ^ stride) for i in range(length)])  49 us
    pallas_call x24, Pallas kernels, plain_call(): pl.pallas_call(kernel, out_shape=outs, in_specs=[ANY] * len(ins), out_spe...  47.9 us
    pallas_call x8, Pallas kernels, assembled(): pl.pallas_call(kernel, out_shape=[jax.ShapeDtypeStruct(whole, f32) for wh...  24.9 us
    ppermute x3, starting transfers between devices, shards(): returned.append(lax.ppermute(sent, SECTION, both))  11.7 us
  transfers between devices with their start and end apart: 45, of which 14 were waited for; matrix products, arithmetic and copies ran while one was open for 1% of the time, Pallas kernels for 54%

profile of v3, /device:TPU:0, one launch (start us, length us, event | category | flops | bytes accessed | tf_op | source)
XLA Modules:
  0.0 336.2 jit_solution(13741376361667424560)
XLA Ops:
  0.6 12.7 %first_forward_0.1 = (bf16[3,208,768]{2,1,0:T(8,128)(2,1)}, bf16[3,208,768]{2,1,0:T(8,128)(2,1)}, bf16[3,208,2304]{2,1,0:T(8,128)(2,1)}, bf16[3,208,768]{2,1,0:T...) custom-call(s32[3]{0:T(128)} %count_ref.11, ...), custom_call_target="tpu_custom_call" | custom-call | flops 99999997952 | bytes 99999997952 | tf_op jit(solution)/shard_map/first_forward_0/pallas_call | solution.py:287
  14.7 13.3 %first_forward_1.1 = (bf16[3,208,768]{2,1,0:T(8,128)(2,1)}, bf16[3,208,768]{2,1,0:T(8,128)(2,1)}, bf16[3,208,2304]{2,1,0:T(8,128)(2,1)}, bf16[3,208,768]{2,1,0:T...) custom-call(s32[3]{0:T(128)} %count_ref.11, ...), custom_call_target="tpu_custom_call", output_to_operand_aliasing={{0}: (16, {}), {1}: (17, {}), {2}: (18, {}), {3}: (19, {}),... | custom-call | flops 99999997952 | bytes 99999997952 | tf_op jit(solution)/shard_map/first_forward_1/pallas_call | solution.py:287
  30.6 12.1 %tick_0.1 = (bf16[3,208,768]{2,1,0:T(8,128)(2,1)}, bf16[3,208,768]{2,1,0:T(8,128)(2,1)}, bf16[3,208,2304]{2,1,0:T(8,128)(2,1)}, bf16[3,208,768]{2,1,0:T(8,128)(2...) custom-call(s32[4]{0:T(128)} %get-tuple-element.372.scalar_ref, ...), custom_call_target="tpu_custom_call", output_to_operand_aliasing={{0}: (17, {}), {1}: (18, {}), {2}: (19, {}), {3}: (20, {}),... | custom-call | flops 99999997952 | bytes 99999997952 | tf_op jit(solution)/shard_map/tick_0/pallas_call | solution.py:287
  46.1 3.4 %tick_1.1 = (bf16[3,208,768]{2,1,0:T(8,128)(2,1)}, bf16[3,208,768]{2,1,0:T(8,128)(2,1)}, bf16[3,208,2304]{2,1,0:T(8,128)(2,1)}, bf16[3,208,768]{2,1,0:T(8,128)(2...) custom-call(s32[4]{0:T(128)} %get-tuple-element.372.scalar_ref, ...), custom_call_target="tpu_custom_call", output_to_operand_aliasing={{0}: (17, {}), {1}: (18, {}), {2}: (19, {}), {3}: (20, {}),... | custom-call | flops 99999997952 | bytes 99999997952 | tf_op jit(solution)/shard_map/tick_1/pallas_call | solution.py:287
  49.5 7.8 %collective-permute-start.4 = (bf16[1,196,768]{2,1,0:T(8,128)(2,1)}, bf16[1,196,768]{2,1,0:T(8,128)(2,1)S(1)}, u32[]{:S(2)}, u32[]{:S(2)}) collective-permute-start(bf16[1,196,768]{2,1,0:T(8,128)(2,1)} %get-tuple-element.225), channel_id=1, source_target_pairs={{16,0},{17,1},{18,2},{19,3},{20,4},{21,5},{22,6},{23,7},{24,8},{25... | collective-permute-start | bytes 903176 | tf_op jit(solution)/shard_map/ppermute | solution.py:1085
  58.0 18.7 %tick_2.1 = (bf16[3,208,768]{2,1,0:T(8,128)(2,1)}, bf16[3,208,768]{2,1,0:T(8,128)(2,1)}, bf16[3,208,2304]{2,1,0:T(8,128)(2,1)}, bf16[3,208,768]{2,1,0:T(8,128)(2...) custom-call(s32[4]{0:T(128)} %get-tuple-element.372.scalar_ref, ...), custom_call_target="tpu_custom_call", output_to_operand_aliasing={{0}: (17, {}), {1}: (18, {}), {2}: (19, {}), {3}: (20, {}),... | custom-call | flops 99999997952 | bytes 99999997952 | tf_op jit(solution)/shard_map/tick_2/pallas_call | solution.py:287
  78.8 10.5 %late_feed_forward_1.1 = (bf16[3,208,3072]{2,1,0:T(8,128)(2,1)}, bf16[3,208,768]{2,1,0:T(8,128)(2,1)}, bf16[3,196,768]{2,1,0:T(8,128)(2,1)}, f32[16,768]{1,0:T(8,128)}, f32[1,208,768]{2,1,0:T(8,128)}) custom-call(s32[3]{0:T(128)} %count_ref.11, ...), custom_call_target="tpu_custom_call", output_to_operand_aliasing={{0}: (16, {}), {1}: (17, {}), {2}: (18, {}), {3}: (19, {})} | custom-call | flops 99999997952 | bytes 99999997952 | tf_op jit(solution)/shard_map/late_feed_forward_1/pallas_call | solution.py:287
  89.3 10.6 %late_attention_1.1 = (bf16[3,208,2304]{2,1,0:T(8,128)(2,1)}, bf16[3,196,768]{2,1,0:T(8,128)(2,1)}, f32[16,768]{1,0:T(8,128)}) custom-call(s32[3]{0:T(128)} %count_ref.11, s32[3,196]{1,0:T(4,128)} %index_ref.13, f32[1,208,768]{2,1,0:T(8,128)} %get-tuple-element.250.gr_ref, ...), custom_call_target="tpu_custom_call", output_to_operand_aliasing={{0}: (17, {}), {1}: (18, {}), {2}: (19, {})} | custom-call | flops 99999997952 | bytes 99999997952 | tf_op jit(solution)/shard_map/late_attention_1/pallas_call | solution.py:287
  99.9 9.3 %grad_down.1 = (bf16[1536,768]{1,0:T(8,128)(2,1)}, bf16[1536,768]{1,0:T(8,128)(2,1)}) custom-call(s32[4]{0:T(128)} %get-tuple-element.371.scalar_ref, bf16[3,208,3072]{2,1,0:T(8,128)(2,1)} %get-tuple-element.258.rest_11_.m_ref, bf16[3,196,768]{2,1,0:T(8,128)(2,1)} %bitcast.57, bf16[1,196,768]{2,1,0:T(8,128)(2,1)} %copy-done.5, ...), custom_call_target="tpu_custom_call" | custom-call | flops 99999997952 | bytes 99999997952 | tf_op jit(solution)/shard_map/grad_down/pallas_call | solution.py:287
  109.7 10.6 %late_feed_forward_2.1 = (bf16[3,208,3072]{2,1,0:T(8,128)(2,1)}, bf16[3,208,768]{2,1,0:T(8,128)(2,1)}, bf16[3,196,768]{2,1,0:T(8,128)(2,1)}, f32[16,768]{1,0:T(8,128)}, f32[1,208,768]{2,1,0:T(8,128)}) custom-call(s32[3]{0:T(128)} %count_ref.11, ...), custom_call_target="tpu_custom_call", output_to_operand_aliasing={{0}: (16, {}), {1}: (17, {}), {2}: (18, {}), {3}: (19, {})} | custom-call | flops 99999997952 | bytes 99999997952 | tf_op jit(solution)/shard_map/late_feed_forward_2/pallas_call | solution.py:287
  120.3 8.2 %grad_up.1 = (bf16[1536,768]{1,0:T(8,128)(2,1)}, bf16[1536,768]{1,0:T(8,128)(2,1)}) custom-call(s32[1]{0:T(128)} %bitcast.6.scalar_ref, bf16[624,768]{1,0:T(8,128)(2,1)} %bitcast.69, bf16[624,3072]{1,0:T(8,128)(2,1)} %bitcast.61), custom_call_target="tpu_custom_call" | custom-call | flops 99999997952 | bytes 99999997952 | tf_op jit(solution)/shard_map/grad_up/pallas_call | solution.py:287
  128.5 3.1 halved_1.4
  135.5 2.7 collective-permute-start.11
  139.8 10.7 %late_attention_2.1 = (bf16[3,208,2304]{2,1,0:T(8,128)(2,1)}, bf16[3,196,768]{2,1,0:T(8,128)(2,1)}, f32[16,768]{1,0:T(8,128)}) custom-call(s32[3]{0:T(128)} %count_ref.11, s32[3,196]{1,0:T(4,128)} %index_ref.13, f32[1,208,768]{2,1,0:T(8,128)} %get-tuple-element.275.gr_ref, ...), custom_call_target="tpu_custom_call", output_to_operand_aliasing={{0}: (17, {}), {1}: (18, {}), {2}: (19, {})} | custom-call | flops 99999997952 | bytes 99999997952 | tf_op jit(solution)/shard_map/late_attention_2/pallas_call | solution.py:287
  150.6 5.3 %grad_query_value.1 = (bf16[768,768]{1,0:T(8,128)(2,1)}, bf16[768,768]{1,0:T(8,128)(2,1)}) custom-call(s32[1]{0:T(128)} %bitcast.6.scalar_ref, bf16[624,768]{1,0:T(8,128)(2,1)} %bitcast.66, bf16[624,2304]{1,0:T(8,128)(2,1)} %bitcast.62), custom_call_target="tpu_custom_call" | custom-call | flops 99999997952 | bytes 99999997952 | tf_op jit(solution)/shard_map/grad_query_value/pallas_call | solution.py:287
  156.3 10.2 %collective-permute-done.8.coming_ref = bf16[768,768]{1,0:T(8,128)(2,1)} collective-permute-done((bf16[768,768]{1,0:T(8,128)(2,1)}, bf16[768,768]{1,0:T(8,128)(2,1)}, u32[]{:S(2)}, u32[]{:S(2)}) %collective-permute-start.8) | collective-permute-done | bytes 1179680 | tf_op jit(solution)/shard_map/ppermute | solution.py:873
  175.9 7.7 %collective-permute-done.9.coming_ref = bf16[384,768]{1,0:T(8,128)(2,1)} collective-permute-done((bf16[384,768]{1,0:T(8,128)(2,1)}, bf16[384,768]{1,0:T(8,128)(2,1)}, u32[]{:S(2)}, u32[]{:S(2)}) %collective-permute-start.9) | collective-permute-done | bytes 589856 | tf_op jit(solution)/shard_map/ppermute | solution.py:873
  188.2 5.8 %grad_key_out.1 = (bf16[768,768]{1,0:T(8,128)(2,1)}, bf16[768,768]{1,0:T(8,128)(2,1)}) custom-call(s32[1]{0:T(128)} %bitcast.6.scalar_ref, bf16[624,768]{1,0:T(8,128)(2,1)} %bitcast.67, bf16[624,2304]{1,0:T(8,128)(2,1)} %bitcast.63, bf16[624,768]{1,0:T(8,128)(2,1)} %bitcast.68, bf16[624,768]{1,0:T(8,128)(2,1)} %bitcast.65), custom_call_target="tpu_custom_call" | custom-call | flops 99999997952 | bytes 99999997952 | tf_op jit(solution)/shard_map/grad_key_out/pallas_call | solution.py:287
  200.1 9.8 %collective-permute-done.12.coming_ref = bf16[192,768]{1,0:T(8,128)(2,1)} collective-permute-done((bf16[192,768]{1,0:T(8,128)(2,1)}, bf16[192,768]{1,0:T(8,128)(2,1)}, u32[]{:S(2)}, u32[]{:S(2)}) %collective-permute-start.12) | collective-permute-done | bytes 294944 | tf_op jit(solution)/shard_map/ppermute | solution.py:873
  213.8 4.2 %collective-permute-start.17 = (bf16[192,768]{1,0:T(8,128)(2,1)}, bf16[192,768]{1,0:T(8,128)(2,1)}, u32[]{:S(2)}, u32[]{:S(2)}) collective-permute-start(bf16[192,768]{1,0:T(8,128)(2,1)} %get-tuple-element.312), channel_id=1, source_target_pairs={{0,4},{2,6},{4,0},{6,2},{8,12},{10,14},{12,8},{14,10},{1,5},{3,7},... | collective-permute-start | bytes 884744 | tf_op jit(solution)/shard_map/ppermute | solution.py:873
  221.8 5.7 %collective-permute-start.23 = (bf16[192,768]{1,0:T(8,128)(2,1)}, bf16[192,768]{1,0:T(8,128)(2,1)}, u32[]{:S(2)}, u32[]{:S(2)}) collective-permute-start(bf16[192,768]{1,0:T(8,128)(2,1)} %get-tuple-element.317), channel_id=1, source_target_pairs={{0,4},{2,6},{4,0},{6,2},{8,12},{10,14},{12,8},{14,10},{1,5},{3,7},... | collective-permute-start | bytes 884744 | tf_op jit(solution)/shard_map/ppermute | solution.py:873
  229.8 3.2 collective-permute-start.21
  234.9 3.0 collective-permute-start.26
  239.4 2.8 collective-permute-start.20
  242.2 4.8 %collective-permute-done.23.coming_ref = bf16[192,768]{1,0:T(8,128)(2,1)} collective-permute-done((bf16[192,768]{1,0:T(8,128)(2,1)}, bf16[192,768]{1,0:T(8,128)(2,1)}, u32[]{:S(2)}, u32[]{:S(2)}) %collective-permute-start.23) | collective-permute-done | bytes 294944 | tf_op jit(solution)/shard_map/ppermute | solution.py:873
  255.8 6.8 %collective-permute-done.26.other_ref = bf16[384,768]{1,0:T(8,128)(2,1)} collective-permute-done((bf16[384,768]{1,0:T(8,128)(2,1)}, bf16[384,768]{1,0:T(8,128)(2,1)}, u32[]{:S(2)}, u32[]{:S(2)}) %collective-permute-start.26) | collective-permute-done | bytes 589856 | tf_op jit(solution)/shard_map/ppermute | solution.py:873
  286.2 4.8 %collective-permute-done.30.other_ref = bf16[192,768]{1,0:T(8,128)(2,1)} collective-permute-done((bf16[192,768]{1,0:T(8,128)(2,1)}, bf16[192,768]{1,0:T(8,128)(2,1)}, u32[]{:S(2)}, u32[]{:S(2)}) %collective-permute-start.30) | collective-permute-done | bytes 294944 | tf_op jit(solution)/shard_map/ppermute | solution.py:873
  294.2 3.6 %assembled.8.refs_2_ = f32[3072,768]{1,0:T(8,128)} custom-call(bf16[768,768]{1,0:T(8,128)(2,1)} %joined_2.3.refs_0_, bf16[768,768]{1,0:T(8,128)(2,1)} %collective-permute-done.28.refs_1_), custom_call_target="tpu_custom_call" | custom-call | flops 99999997952 | bytes 99999997952 | tf_op jit(solution)/shard_map/assembled/pallas_call | solution.py:854
  302.1 3.7 %assembled.9 = f32[3072,768]{1,0:T(8,128)} custom-call(bf16[768,768]{1,0:T(8,128)(2,1)S(1)} %collective-permute-done.36.refs_0_, bf16[768,768]{1,0:T(8,128)(2,1)} %collective-permute-done.37.refs_1_, f32[3072,768]{1,0:T(8,128)} %assembled.8.refs_2_), custom_call_target="tpu_custom_call", output_to_operand_aliasing={{}: (2, {})} | custom-call | flops 99999997952 | bytes 99999997952 | tf_op jit(solution)/shard_map/assembled/pallas_call | solution.py:854
  309.4 6.7 %collective-permute-done.34.refs_1_ = bf16[768,768]{1,0:T(8,128)(2,1)} collective-permute-done((bf16[768,768]{1,0:T(8,128)(2,1)}, bf16[768,768]{1,0:T(8,128)(2,1)}, u32[]{:S(2)}, u32[]{:S(2)}) %collective-permute-start.34) | collective-permute-done | bytes 1179680 | tf_op jit(solution)/shard_map/ppermute | solution.py:873
  316.7 3.6 %assembled.11.refs_2_ = f32[768,3072]{1,0:T(8,128)} custom-call(bf16[768,768]{1,0:T(8,128)(2,1)} %joined_1.1.refs_0_, bf16[768,768]{1,0:T(8,128)(2,1)} %collective-permute-done.34.refs_1_), custom_call_target="tpu_custom_call" | custom-call | flops 99999997952 | bytes 99999997952 | tf_op jit(solution)/shard_map/assembled/pallas_call | solution.py:854
  326.2 3.6 %assembled.14 = f32[768,3072]{1,0:T(8,128)} custom-call(bf16[768,768]{1,0:T(8,128)(2,1)} %collective-permute-done.38.refs_0_, bf16[768,768]{1,0:T(8,128)(2,1)} %collective-permute-done.39.refs_1_, f32[768,3072]{1,0:T(8,128)} %assembled.11.refs_2_), custom_call_target="tpu_custom_call", output_to_operand_aliasing={{}: (2, {})} | custom-call | flops 99999997952 | bytes 99999997952 | tf_op jit(solution)/shard_map/assembled/pallas_call | solution.py:854
  (130 shorter events, 105.3 us)
Async XLA Ops:
  13.4 16.5 %collective-permute-start = (bf16[1,196,768]{2,1,0:T(8,128)(2,1)}, bf16[1,196,768]{2,1,0:T(8,128)(2,1)S(1)}, u32[]{:S(2)}, u32[]{:S(2)}) collective-permute-start(bf16[1,196,768]{2,1,0:T(8,128)(2,1)} %get-tuple-element.189), channel_id=1, source_target_pairs={{0,16},{1,17},{2,18},{3,19},{4,20},{5,21},{6,22},{7,23},{8,24},{9,... | collective-permute-start | bytes 903176 | tf_op jit(solution)/shard_map/ppermute | solution.py:1075
  28.0 17.4 %collective-permute-start.2 = (bf16[1,196,768]{2,1,0:T(8,128)(2,1)}, bf16[1,196,768]{2,1,0:T(8,128)(2,1)S(1)}, u32[]{:S(2)}, u32[]{:S(2)}) collective-permute-start(bf16[1,196,768]{2,1,0:T(8,128)(2,1)} %get-tuple-element.209), channel_id=1, source_target_pairs={{0,16},{1,17},{2,18},{3,19},{4,20},{5,21},{6,22},{7,23},{8,24},{9,... | collective-permute-start | bytes 903176 | tf_op jit(solution)/shard_map/ppermute | solution.py:1075
  42.8 14.5 %collective-permute-start.1 = (bf16[1,196,768]{2,1,0:T(8,128)(2,1)}, bf16[1,196,768]{2,1,0:T(8,128)(2,1)S(1)}, u32[]{:S(2)}, u32[]{:S(2)}) collective-permute-start(bf16[1,196,768]{2,1,0:T(8,128)(2,1)} %get-tuple-element.208), channel_id=1, source_target_pairs={{16,0},{0,16},{17,1},{1,17},{18,2},{2,18},{19,3},{3,19},{20,4},{4,... | collective-permute-start | bytes 903176 | tf_op jit(solution)/shard_map/ppermute | solution.py:1085
  49.5 28.6 %collective-permute-start.4 = (bf16[1,196,768]{2,1,0:T(8,128)(2,1)}, bf16[1,196,768]{2,1,0:T(8,128)(2,1)S(1)}, u32[]{:S(2)}, u32[]{:S(2)}) collective-permute-start(bf16[1,196,768]{2,1,0:T(8,128)(2,1)} %get-tuple-element.225), channel_id=1, source_target_pairs={{16,0},{17,1},{18,2},{19,3},{20,4},{21,5},{22,6},{23,7},{24,8},{25... | collective-permute-start | bytes 903176 | tf_op jit(solution)/shard_map/ppermute | solution.py:1085
  76.8 23.1 %collective-permute-start.3 = (bf16[1,196,768]{2,1,0:T(8,128)(2,1)}, bf16[1,196,768]{2,1,0:T(8,128)(2,1)}, u32[]{:S(2)}, u32[]{:S(2)}) collective-permute-start(bf16[1,196,768]{2,1,0:T(8,128)(2,1)} %get-tuple-element.241), channel_id=1, source_target_pairs={{16,0},{17,1},{18,2},{19,3},{20,4},{21,5},{22,6},{23,7},{24,8},{25... | collective-permute-start | bytes 903176 | tf_op jit(solution)/shard_map/ppermute | solution.py:1085
  109.3 19.3 %collective-permute-start.6 = (bf16[1536,768]{1,0:T(8,128)(2,1)}, bf16[1536,768]{1,0:T(8,128)(2,1)}, u32[]{:S(2)}, u32[]{:S(2)}) collective-permute-start(bf16[1536,768]{1,0:T(8,128)(2,1)} %get-tuple-element.259), channel_id=1, source_target_pairs={{0,1},{1,0},{2,3},{3,2},{4,5},{5,4},{6,7},{7,6},{8,9},{9,8},{10,11... | collective-permute-start | bytes 7077896 | tf_op jit(solution)/shard_map/ppermute | solution.py:873
  135.5 33.7 %collective-permute-start.11 = (bf16[768,768]{1,0:T(8,128)(2,1)}, bf16[768,768]{1,0:T(8,128)(2,1)}, u32[]{:S(2)}, u32[]{:S(2)}) collective-permute-start(bf16[768,768]{1,0:T(8,128)(2,1)} %get-tuple-element.274), channel_id=1, source_target_pairs={{0,4},{2,6},{4,0},{6,2},{8,12},{10,14},{12,8},{14,10},{1,5},{3,7},... | collective-permute-start | bytes 3538952 | tf_op jit(solution)/shard_map/ppermute | solution.py:873
  138.3 28.3 %collective-permute-start.8 = (bf16[768,768]{1,0:T(8,128)(2,1)}, bf16[768,768]{1,0:T(8,128)(2,1)}, u32[]{:S(2)}, u32[]{:S(2)}) collective-permute-start(bf16[768,768]{1,0:T(8,128)(2,1)} %get-tuple-element.272), channel_id=1, source_target_pairs={{0,2},{2,0},{4,6},{6,4},{8,10},{10,8},{12,14},{14,12},{1,3},{3,1},... | collective-permute-start | bytes 3538952 | tf_op jit(solution)/shard_map/ppermute | solution.py:873
  150.5 87.4 %collective-permute-start.7 = (f32[16,768]{1,0:T(8,128)}, f32[16,768]{1,0:T(8,128)}, u32[]{:S(2)}, u32[]{:S(2)}) collective-permute-start(f32[16,768]{1,0:T(8,128)} %get-tuple-element.281.value_ref), channel_id=1, source_target_pairs={{0,1},{1,0},{2,3},{3,2},{4,5},{5,4},{6,7},{7,6},{8,9},{9,8},{10,11... | collective-permute-start | bytes 147464 | tf_op jit(solution)/shard_map/ppermute | solution.py:873
  155.9 17.3 %collective-permute-start.10 = (bf16[768,768]{1,0:T(8,128)(2,1)}, bf16[768,768]{1,0:T(8,128)(2,1)}, u32[]{:S(2)}, u32[]{:S(2)}) collective-permute-start(bf16[768,768]{1,0:T(8,128)(2,1)} %get-tuple-element.286), channel_id=1, source_target_pairs={{0,1},{1,0},{2,3},{3,2},{4,5},{5,4},{6,7},{7,6},{8,9},{9,8},{10,11... | collective-permute-start | bytes 3538952 | tf_op jit(solution)/shard_map/ppermute | solution.py:873
  168.8 14.9 %collective-permute-start.9 = (bf16[384,768]{1,0:T(8,128)(2,1)}, bf16[384,768]{1,0:T(8,128)(2,1)}, u32[]{:S(2)}, u32[]{:S(2)}) collective-permute-start(bf16[384,768]{1,0:T(8,128)(2,1)} %get-tuple-element.289), channel_id=1, source_target_pairs={{0,4},{2,6},{4,0},{6,2},{8,12},{10,14},{12,8},{14,10},{1,5},{3,7},... | collective-permute-start | bytes 1769480 | tf_op jit(solution)/shard_map/ppermute | solution.py:873
  171.5 22.5 %collective-permute-start.14 = (bf16[384,768]{1,0:T(8,128)(2,1)}, bf16[384,768]{1,0:T(8,128)(2,1)}, u32[]{:S(2)}, u32[]{:S(2)}) collective-permute-start(bf16[384,768]{1,0:T(8,128)(2,1)} %get-tuple-element.293), channel_id=1, source_target_pairs={{0,2},{2,0},{4,6},{6,4},{8,10},{10,8},{12,14},{14,12},{1,3},{3,1},... | collective-permute-start | bytes 1769480 | tf_op jit(solution)/shard_map/ppermute | solution.py:873
  175.5 36.4 %collective-permute-start.16 = (bf16[384,768]{1,0:T(8,128)(2,1)}, bf16[384,768]{1,0:T(8,128)(2,1)}, u32[]{:S(2)}, u32[]{:S(2)}) collective-permute-start(bf16[384,768]{1,0:T(8,128)(2,1)} %get-tuple-element.295), channel_id=1, source_target_pairs={{0,2},{2,0},{4,6},{6,4},{8,10},{10,8},{12,14},{14,12},{1,3},{3,1},... | collective-permute-start | bytes 1769480 | tf_op jit(solution)/shard_map/ppermute | solution.py:873
  185.5 24.4 %collective-permute-start.12 = (bf16[192,768]{1,0:T(8,128)(2,1)}, bf16[192,768]{1,0:T(8,128)(2,1)}, u32[]{:S(2)}, u32[]{:S(2)}) collective-permute-start(bf16[192,768]{1,0:T(8,128)(2,1)} %get-tuple-element.298), channel_id=1, source_target_pairs={{0,8},{2,10},{4,12},{6,14},{8,0},{10,2},{12,4},{14,6},{1,9},{3,11}... | collective-permute-start | bytes 884744 | tf_op jit(solution)/shard_map/ppermute | solution.py:873
  196.0 22.0 %collective-permute-start.19 = (bf16[192,768]{1,0:T(8,128)(2,1)}, bf16[192,768]{1,0:T(8,128)(2,1)}, u32[]{:S(2)}, u32[]{:S(2)}) collective-permute-start(bf16[192,768]{1,0:T(8,128)(2,1)} %get-tuple-element.305), channel_id=1, source_target_pairs={{0,8},{2,10},{4,12},{6,14},{8,0},{10,2},{12,4},{14,6},{1,9},{3,11}... | collective-permute-start | bytes 884744 | tf_op jit(solution)/shard_map/ppermute | solution.py:873
  198.5 21.4 %collective-permute-start.18 = (bf16[384,768]{1,0:T(8,128)(2,1)}, bf16[384,768]{1,0:T(8,128)(2,1)}, u32[]{:S(2)}, u32[]{:S(2)}) collective-permute-start(bf16[384,768]{1,0:T(8,128)(2,1)} %get-tuple-element.307), channel_id=1, source_target_pairs={{0,2},{2,0},{4,6},{6,4},{8,10},{10,8},{12,14},{14,12},{1,3},{3,1},... | collective-permute-start | bytes 1769480 | tf_op jit(solution)/shard_map/ppermute | solution.py:873
  211.8 21.2 %collective-permute-start.15 = (bf16[192,768]{1,0:T(8,128)(2,1)}, bf16[192,768]{1,0:T(8,128)(2,1)}, u32[]{:S(2)}, u32[]{:S(2)}) collective-permute-start(bf16[192,768]{1,0:T(8,128)(2,1)} %summed.4.mine_ref), channel_id=1, source_target_pairs={{0,8},{2,10},{4,12},{6,14},{8,0},{10,2},{12,4},{14,6},{1,9},{3,11}... | collective-permute-start | bytes 884744 | tf_op jit(solution)/shard_map/ppermute | solution.py:873
  213.8 14.0 %collective-permute-start.17 = (bf16[192,768]{1,0:T(8,128)(2,1)}, bf16[192,768]{1,0:T(8,128)(2,1)}, u32[]{:S(2)}, u32[]{:S(2)}) collective-permute-start(bf16[192,768]{1,0:T(8,128)(2,1)} %get-tuple-element.312), channel_id=1, source_target_pairs={{0,4},{2,6},{4,0},{6,2},{8,12},{10,14},{12,8},{14,10},{1,5},{3,7},... | collective-permute-start | bytes 884744 | tf_op jit(solution)/shard_map/ppermute | solution.py:873
  219.8 30.7 %collective-permute-start.22 = (bf16[192,768]{1,0:T(8,128)(2,1)}, bf16[192,768]{1,0:T(8,128)(2,1)}, u32[]{:S(2)}, u32[]{:S(2)}) collective-permute-start(bf16[192,768]{1,0:T(8,128)(2,1)} %summed.5.mine_ref), channel_id=1, source_target_pairs={{0,8},{2,10},{4,12},{6,14},{8,0},{10,2},{12,4},{14,6},{1,9},{3,11}... | collective-permute-start | bytes 884744 | tf_op jit(solution)/shard_map/ppermute | solution.py:873
  221.8 25.2 %collective-permute-start.23 = (bf16[192,768]{1,0:T(8,128)(2,1)}, bf16[192,768]{1,0:T(8,128)(2,1)}, u32[]{:S(2)}, u32[]{:S(2)}) collective-permute-start(bf16[192,768]{1,0:T(8,128)(2,1)} %get-tuple-element.317), channel_id=1, source_target_pairs={{0,4},{2,6},{4,0},{6,2},{8,12},{10,14},{12,8},{14,10},{1,5},{3,7},... | collective-permute-start | bytes 884744 | tf_op jit(solution)/shard_map/ppermute | solution.py:873
  229.8 23.2 %collective-permute-start.21 = (bf16[96,768]{1,0:T(8,128)(2,1)}, bf16[96,768]{1,0:T(8,128)(2,1)}, u32[]{:S(2)}, u32[]{:S(2)}) collective-permute-start(bf16[96,768]{1,0:T(8,128)(2,1)} %get-tuple-element.319), channel_id=1, source_target_pairs={{0,8},{2,10},{4,12},{6,14},{8,0},{10,2},{12,4},{14,6},{1,9},{3,11}... | collective-permute-start | bytes 442376 | tf_op jit(solution)/shard_map/ppermute | solution.py:873
  234.9 27.8 %collective-permute-start.26 = (bf16[384,768]{1,0:T(8,128)(2,1)}, bf16[384,768]{1,0:T(8,128)(2,1)}, u32[]{:S(2)}, u32[]{:S(2)}) collective-permute-start(bf16[384,768]{1,0:T(8,128)(2,1)} %joined_4.4.mine_ref), channel_id=1, source_target_pairs={{0,4},{2,6},{4,0},{6,2},{8,12},{10,14},{12,8},{14,10},{1,5},{3,7},... | collective-permute-start | bytes 1769480 | tf_op jit(solution)/shard_map/ppermute | solution.py:873
  239.4 36.0 %collective-permute-start.20 = (f32[16,768]{1,0:T(8,128)}, f32[16,768]{1,0:T(8,128)}, u32[]{:S(2)}, u32[]{:S(2)}) collective-permute-start(f32[16,768]{1,0:T(8,128)} %added.4.value_ref), channel_id=1, source_target_pairs={{0,2},{2,0},{4,6},{6,4},{8,10},{10,8},{12,14},{14,12},{1,3},{3,1},... | collective-permute-start | bytes 147464 | tf_op jit(solution)/shard_map/ppermute | solution.py:873
  249.0 17.7 %collective-permute-start.25 = (bf16[96,768]{1,0:T(8,128)(2,1)}, bf16[96,768]{1,0:T(8,128)(2,1)}, u32[]{:S(2)}, u32[]{:S(2)}) collective-permute-start(bf16[96,768]{1,0:T(8,128)(2,1)} %get-tuple-element.325), channel_id=1, source_target_pairs={{0,8},{2,10},{4,12},{6,14},{8,0},{10,2},{12,4},{14,6},{1,9},{3,11}... | collective-permute-start | bytes 442376 | tf_op jit(solution)/shard_map/ppermute | solution.py:873
  252.4 28.2 %collective-permute-start.32 = (bf16[384,768]{1,0:T(8,128)(2,1)}, bf16[384,768]{1,0:T(8,128)(2,1)}, u32[]{:S(2)}, u32[]{:S(2)}) collective-permute-start(bf16[384,768]{1,0:T(8,128)(2,1)} %joined_4.5.mine_ref), channel_id=1, source_target_pairs={{0,2},{2,0},{4,6},{6,4},{8,10},{10,8},{12,14},{14,12},{1,3},{3,1},... | collective-permute-start | bytes 1769480 | tf_op jit(solution)/shard_map/ppermute | solution.py:873
  254.8 16.3 %collective-permute-start.24 = (bf16[96,768]{1,0:T(8,128)(2,1)}, bf16[96,768]{1,0:T(8,128)(2,1)}, u32[]{:S(2)}, u32[]{:S(2)}) collective-permute-start(bf16[96,768]{1,0:T(8,128)(2,1)} %summed.6.mine_ref), channel_id=1, source_target_pairs={{0,8},{2,10},{4,12},{6,14},{8,0},{10,2},{12,4},{14,6},{1,9},{3,11}... | collective-permute-start | bytes 442376 | tf_op jit(solution)/shard_map/ppermute | solution.py:873
  264.9 29.3 %collective-permute-start.28 = (bf16[768,768]{1,0:T(8,128)(2,1)}, bf16[768,768]{1,0:T(8,128)(2,1)}, u32[]{:S(2)}, u32[]{:S(2)}) collective-permute-start(bf16[768,768]{1,0:T(8,128)(2,1)} %joined_2.3.refs_0_), channel_id=1, source_target_pairs={{0,2},{2,0},{4,6},{6,4},{8,10},{10,8},{12,14},{14,12},{1,3},{3,1},... | collective-permute-start | bytes 3538952 | tf_op jit(solution)/shard_map/ppermute | solution.py:873
  276.8 21.1 %collective-permute-start.27 = (f32[16,768]{1,0:T(8,128)}, f32[16,768]{1,0:T(8,128)}, u32[]{:S(2)}, u32[]{:S(2)}) collective-permute-start(f32[16,768]{1,0:T(8,128)} %added.5.value_ref), channel_id=1, source_target_pairs={{0,4},{2,6},{4,0},{6,2},{8,12},{10,14},{12,8},{14,10},{1,5},{3,7},... | collective-permute-start | bytes 147464 | tf_op jit(solution)/shard_map/ppermute | solution.py:873
  282.9 33.3 %collective-permute-start.34 = (bf16[768,768]{1,0:T(8,128)(2,1)}, bf16[768,768]{1,0:T(8,128)(2,1)}, u32[]{:S(2)}, u32[]{:S(2)}) collective-permute-start(bf16[768,768]{1,0:T(8,128)(2,1)} %joined_1.1.refs_0_), channel_id=1, source_target_pairs={{0,4},{2,6},{4,0},{6,2},{8,12},{10,14},{12,8},{14,10},{1,5},{3,7},... | collective-permute-start | bytes 3538952 | tf_op jit(solution)/shard_map/ppermute | solution.py:873
  285.5 21.3 %collective-permute-start.35 = (bf16[384,768]{1,0:T(8,128)(2,1)}, bf16[384,768]{1,0:T(8,128)(2,1)}, u32[]{:S(2)}, u32[]{:S(2)}) collective-permute-start(bf16[384,768]{1,0:T(8,128)(2,1)} %joined_2.4.refs_0_), channel_id=1, source_target_pairs={{0,2},{2,0},{4,6},{6,4},{8,10},{10,8},{12,14},{14,12},{1,3},{3,1},... | collective-permute-start | bytes 1769480 | tf_op jit(solution)/shard_map/ppermute | solution.py:873
  292.9 30.1 %collective-permute-start.40 = (bf16[384,768]{1,0:T(8,128)(2,1)}, bf16[384,768]{1,0:T(8,128)(2,1)}, u32[]{:S(2)}, u32[]{:S(2)}) collective-permute-start(bf16[384,768]{1,0:T(8,128)(2,1)} %joined_2.5.refs_0_), channel_id=1, source_target_pairs={{0,2},{2,0},{4,6},{6,4},{8,10},{10,8},{12,14},{14,12},{1,3},{3,1},... | collective-permute-start | bytes 1769480 | tf_op jit(solution)/shard_map/ppermute | solution.py:873
  299.9 30.0 %collective-permute-start.33 = (f32[16,768]{1,0:T(8,128)}, f32[16,768]{1,0:T(8,128)}, u32[]{:S(2)}, u32[]{:S(2)}) collective-permute-start(f32[16,768]{1,0:T(8,128)} %added.6.value_ref), channel_id=1, source_target_pairs={{0,8},{2,10},{4,12},{6,14},{8,0},{10,2},{12,4},{14,6},{1,9},{3,11}... | collective-permute-start | bytes 147464 | tf_op jit(solution)/shard_map/ppermute | solution.py:873
  (22 other events, 140.7 us)

commit v4 on v3

--- a/solution.py
+++ b/solution.py
@@ -30,8 +30,9 @@
 WEIGHTS = range(19, 23)
 W_QKV, W_OUT, W_UP, W_DOWN = WEIGHTS
 DOWN, UP, QUERY_VALUE, KEY_OUT, SUMS, OUT = range(100, 106)
-ORDER = "FAGFUduAQduqdKukdqukqdskuqdkqskuqkdsdquqkusk"
+ORDER = "FAGFUduAQdKudqukdqsukqdskuqdkqkuqsdksdquqkuk"
 COST = 10**11
+LATE_COST = 10**10
 ANY = pl.BlockSpec(memory_space=pl.ANY)
 
 
@@ -434,9 +435,19 @@
             forward_part(refs, fetch.wait, store.start, vec, near, live)
             fetch.wait(W_DOWN)
 
-        def backward(near):
-            feed_forward_back(refs, nothing, store.start, vec, near, live, add)
-            attention_back(refs, nothing, store.start, vec, near, live, add)
+        def backward(near, wait=nothing):
+            feed_forward_back(refs, wait, store.start, vec, near, live, add)
+            attention_back(refs, wait, store.start, vec, near, live, add)
+
+        def fetched():
+            weights_in = fetch_weights(sem, hbm, local, (W_DOWN, W_UP, W_OUT, W_QKV))[0]
+            return weights_in, Copies(out_sem, {name: (place[name], refs[name]) for name in (SLOPE, R, QKV, U)})
+
+        def await_early(*names):
+            @pl.when(early)
+            def _():
+                for copies in fetched():
+                    copies.wait(*names)
 
         def sent():
             refs[GRAD][...] = refs[GU][:slots, :]
@@ -453,7 +464,7 @@
 
             @pl.when(later)
             def _():
-                pad_rows(refs[U], received_ref)
+                pad_rows(refs[U], received_ref.at[0])
 
             forward(fetch, near)
 
@@ -477,7 +488,7 @@
         def _():
             fetch, near = fetch_weights(sem, hbm, local)
             fetch.start()
-            pad_rows(refs[U], received_ref)
+            pad_rows(refs[U], received_ref.at[0])
             pad_rows(refs[E], source_ref)
             forward(fetch, near)
             if late is None:
@@ -490,15 +501,11 @@
 
         @pl.when(early)
         def _():
-            fetch, _ = fetch_weights(sem, hbm, local, (W_DOWN, W_UP, W_OUT, W_QKV))
-            load = Copies(out_sem, {name: (place[name], refs[name]) for name in (SLOPE, R, QKV, U)})
-            fetch.start()
-            load.start()
-            pad_rows(refs[E], received_ref)
-            fetch.wait()
-            load.wait()
-
-        backward(dict(zip(WEIGHTS, local)))
+            for copies in fetched():
+                copies.start()
+            pad_rows(refs[E], received_ref.at[0])
+
+        backward(dict(zip(WEIGHTS, local)), await_early)
 
         @pl.when(early)
         def _():
@@ -520,7 +527,7 @@
         (index, received, source) + vectors + weights + old,
         [
             fixed_block(index.shape),
-            image_block((slots, width), 0),
+            pl.BlockSpec(memory_space=pltpu.VMEM),
             pl.BlockSpec(
                 (pl.Squeezed(), slots, width), lambda i, s: (jnp.where(s[images] == 0, other, image), 0, 0)
             ),
@@ -571,7 +578,6 @@
             fetch = Copies(
                 sem,
                 {
-                    E: (received_ref.at[0], refs[Y]),
                     W_DOWN: (far[W_DOWN], near[W_DOWN]),
                     SLOPE: (source[SLOPE], refs[SLOPE]),
                     W_UP: (far[W_UP], near[W_UP]),
@@ -580,8 +586,7 @@
             )
             fetch.start()
             store = Copies(sem.at[pl.ds(5, 2)], {name: (refs[name], place[name]) for name in (GZ, GB)})
-            fetch.wait(E)
-            pad_rows(refs[E], refs[Y])
+            pad_rows(refs[E], received_ref.at[0])
             feed_forward_back(refs, fetch.wait, store.start, vec, near, live, vector_adder(sums_ref))
             store.wait()
 
@@ -611,7 +616,7 @@
         + tuple(saved[SAVED.index(name)] for name in loads)
         + tuple(weights[WEIGHTS.index(name)] for name in near_names)
         + tuple(old),
-        [ANY]
+        [pl.BlockSpec(memory_space=pltpu.VMEM)]
         + [fixed_block(vector.shape) for vector in vectors]
         + [ANY] * (len(loads) + len(near_names) + len(old) - 1)
         + [fixed_block(sums.shape)],
@@ -811,12 +816,12 @@
     )
 
 
-def plain_call(kernel, ins, outs, scratch, name):
+def plain_call(kernel, ins, outs, scratch, name, out_specs=None):
     return pl.pallas_call(
         kernel,
         out_shape=outs,
         in_specs=[ANY] * len(ins),
-        out_specs=[pl.BlockSpec(memory_space=pltpu.VMEM)] * len(outs),
+        out_specs=out_specs or [pl.BlockSpec(memory_space=pltpu.VMEM)] * len(outs),
         scratch_shapes=scratch,
         compiler_params=pltpu.CompilerParams(vmem_limit_bytes=16 << 20),
         cost_estimate=pl.CostEstimate(flops=COST, bytes_accessed=COST, transcendentals=0),
@@ -863,9 +868,13 @@
         ],
         input_output_aliases={2 + k: k for k in range(len(before))},
         compiler_params=pltpu.CompilerParams(vmem_limit_bytes=16 << 20),
-        cost_estimate=pl.CostEstimate(flops=COST, bytes_accessed=COST, transcendentals=0),
+        cost_estimate=pl.CostEstimate(flops=LATE_COST, bytes_accessed=LATE_COST, transcendentals=0),
         name="assembled",
     )(*pieces, *before)
+
+
+def in_vmem(value):
+    return pltpu.with_memory_space_constraint(value, pltpu.VMEM)
 
 
 def swapped(value, axis, stride):
@@ -885,7 +894,7 @@
         send = lax.dynamic_slice_in_dim(pair, (1 - bit) * height, height, axis=0)
         return send, lax.dynamic_slice_in_dim(pair, bit * height, height, axis=0)
 
-    def kernel(keep_ref, coming_ref, send_ref, stay_ref, kept, came, sem):
+    def kernel(keep_ref, coming_ref, send_ref, stay_ref, kept, came, made, sem):
         bit = bit_of(DP, stride)
         copies = []
         for at, half in enumerate((1 - bit, bit)):
@@ -896,10 +905,13 @@
             copy.start()
         for copy in copies[:2]:
             copy.wait()
-        send_ref[...] = (kept[0].astype(f32) + came[0].astype(f32)).astype(bf16)
+        made[...] = (kept[0].astype(f32) + came[0].astype(f32)).astype(bf16)
+        store = pltpu.make_async_copy(made, send_ref, sem.at[4])
+        store.start()
         for copy in copies[2:]:
             copy.wait()
         stay_ref[...] = (kept[1].astype(f32) + came[1].astype(f32)).astype(bf16)
+        store.wait()
 
     shape = (height, width)
     return plain_call(
@@ -909,9 +921,11 @@
         [
             pltpu.VMEM((2,) + shape, bf16),
             pltpu.VMEM((2,) + shape, bf16),
-            pltpu.SemaphoreType.DMA((4,)),
+            pltpu.VMEM(shape, bf16),
+            pltpu.SemaphoreType.DMA((5,)),
         ],
         f"halved_{stride}",
+        [ANY, pl.BlockSpec(memory_space=pltpu.VMEM)],
     )
 
 
@@ -945,23 +959,28 @@
         first = bit_of(DP, stride) == 0
         return jnp.concatenate([jnp.where(first, mine, other), jnp.where(first, other, mine)], axis=0)
 
-    def kernel(mine_ref, other_ref, out_ref, sem):
+    def kernel(mine_ref, other_ref, out_ref, held, sem):
         bit = bit_of(DP, stride)
-        copies = []
+        loads, stores = [], []
         for at, (half, source) in enumerate(((bit, mine_ref), (1 - bit, other_ref))):
             rows = pl.ds(pl.multiple_of(half * height, ROW_TILE), height)
-            copies.append(pltpu.make_async_copy(source, out_ref.at[rows, :], sem.at[at]))
-        for copy in copies:
-            copy.start()
-        for copy in copies:
-            copy.wait()
+            loads.append(pltpu.make_async_copy(source, held.at[at], sem.at[at]))
+            stores.append(pltpu.make_async_copy(held.at[at], out_ref.at[rows, :], sem.at[2 + at]))
+        for load in loads:
+            load.start()
+        for load, store in zip(loads, stores):
+            load.wait()
+            store.start()
+        for store in stores:
+            store.wait()
 
     return plain_call(
         kernel,
         (mine, other),
         [jax.ShapeDtypeStruct((2 * height, width), bf16)],
-        [pltpu.SemaphoreType.DMA((2,))],
+        [pltpu.VMEM((2, height, width), bf16), pltpu.SemaphoreType.DMA((4,))],
         f"joined_{stride}",
+        [ANY],
     )[0]
 
 
@@ -1020,7 +1039,7 @@
     return pl.pallas_call(
         kernel,
         out_shape=jax.ShapeDtypeStruct(value.shape, value.dtype),
-        cost_estimate=pl.CostEstimate(flops=COST, bytes_accessed=COST, transcendentals=0),
+        cost_estimate=pl.CostEstimate(flops=LATE_COST, bytes_accessed=LATE_COST, transcendentals=0),
         name="added",
     )(value, coming)
 
@@ -1077,7 +1096,7 @@
     made, sums, returned = None, None, []
     for image, first, late in ((0, 2, None), (1, None, None), (2, None, 0)):
         saved, made, output, sums, sent = tick(
-            first, image, late, saved, made, output, sums, scalars, keep_index, line.gate(received[image]),
+            first, image, late, saved, made, output, sums, scalars, keep_index, in_vmem(line.gate(received[image])),
             rows_in, vectors, weights,
         )
         line.passed(sent)
@@ -1107,7 +1126,7 @@
         nonlocal made, output, sums
         image = forwards.pop(0)
         made, output, sums, residual[image] = late_feed_forward(
-            image, (0, 1) if image == 1 else (2,), saved, made, output, sums, keep_count, line.gate(returned[image]),
+            image, (0, 1) if image == 1 else (2,), saved, made, output, sums, keep_count, in_vmem(line.gate(returned[image])),
             vectors, weights,
         )
         line.passed(residual[image])

time: 343 us -> 340 us (level)
  the two profiles are of different devices: /device:TPU:0 before, /device:TPU:11 now
where the time goes in v4:
time: 340 us; the launch traced here: 334 us
  Pallas kernels  191 us (56%)
  waiting for transfers between devices  81.9 us (24%)
  starting transfers between devices  56.9 us (17%)
    pallas_call x13, Pallas kernels, call(): pl.pallas_call(kernel, out_shape=outs, grid_spec=pltpu.PrefetchScalarGrid...  119 us
    ppermute x40, waiting for transfers between devices, swapped(): return lax.ppermute(value, axis, [(i, i ^ stride) for i in range(length)])  69.2 us
    ppermute x40, starting transfers between devices, swapped(): return lax.ppermute(value, axis, [(i, i ^ stride) for i in range(length)])  50.2 us
    pallas_call x24, Pallas kernels, plain_call(): pl.pallas_call(kernel, out_shape=outs, in_specs=[ANY] * len(ins), out_spe...  44.8 us
    pallas_call x8, Pallas kernels, assembled(): pl.pallas_call(kernel, out_shape=[jax.ShapeDtypeStruct(whole, f32) for wh...  21.6 us
    ppermute x2, waiting for transfers between devices, shards(): received.append(lax.ppermute(first_output, SECTION, [(0, 1)]))  12.7 us
  transfers between devices with their start and end apart: 45, of which 13 were waited for; matrix products, arithmetic and copies ran while one was open for 1% of the time, Pallas kernels for 52%

profile of v4, /device:TPU:11, one launch (start us, length us, event | category | flops | bytes accessed | tf_op | source)
XLA Modules:
  0.0 333.7 jit_solution(15543942810179738999)
XLA Ops:
  4.5 3.0 first_forward_1.1
  9.4 12.7 %collective-permute-done.received_ref = bf16[1,196,768]{2,1,0:T(8,128)(2,1)S(1)} collective-permute-done((bf16[1,196,768]{2,1,0:T(8,128)(2,1)}, bf16[1,196,768]{2,1,0:T(8,128)(2,1)S(1)}, u32[]{:S(2)}, u32[]{:S(2)}) %collective-permute-start) | collective-permute-done | bytes 301088 | tf_op jit(solution)/shard_map/ppermute | solution.py:1094
  22.0 19.6 %tick_0.1 = (bf16[3,208,768]{2,1,0:T(8,128)(2,1)}, bf16[3,208,768]{2,1,0:T(8,128)(2,1)}, bf16[3,208,2304]{2,1,0:T(8,128)(2,1)}, bf16[3,208,768]{2,1,0:T(8,128)(2...) custom-call(s32[4]{0:T(128)} %get-tuple-element.372.scalar_ref, ...), custom_call_target="tpu_custom_call", output_to_operand_aliasing={{0}: (17, {}), {1}: (18, {}), {2}: (19, {}), {3}: (20, {}),... | custom-call | flops 99999997952 | bytes 99999997952 | tf_op jit(solution)/shard_map/tick_0/pallas_call | solution.py:288
  42.1 20.1 %tick_1.1 = (bf16[3,208,768]{2,1,0:T(8,128)(2,1)}, bf16[3,208,768]{2,1,0:T(8,128)(2,1)}, bf16[3,208,2304]{2,1,0:T(8,128)(2,1)}, bf16[3,208,768]{2,1,0:T(8,128)(2...) custom-call(s32[4]{0:T(128)} %get-tuple-element.372.scalar_ref, ...), custom_call_target="tpu_custom_call", output_to_operand_aliasing={{0}: (17, {}), {1}: (18, {}), {2}: (19, {}), {3}: (20, {}),... | custom-call | flops 99999997952 | bytes 99999997952 | tf_op jit(solution)/shard_map/tick_1/pallas_call | solution.py:288
  64.0 20.5 %tick_2.1 = (bf16[3,208,768]{2,1,0:T(8,128)(2,1)}, bf16[3,208,768]{2,1,0:T(8,128)(2,1)}, bf16[3,208,2304]{2,1,0:T(8,128)(2,1)}, bf16[3,208,768]{2,1,0:T(8,128)(2...) custom-call(s32[4]{0:T(128)} %get-tuple-element.372.scalar_ref, ...), custom_call_target="tpu_custom_call", output_to_operand_aliasing={{0}: (17, {}), {1}: (18, {}), {2}: (19, {}), {3}: (20, {}),... | custom-call | flops 99999997952 | bytes 99999997952 | tf_op jit(solution)/shard_map/tick_2/pallas_call | solution.py:288
  86.5 11.4 %late_feed_forward_1.1 = (bf16[3,208,3072]{2,1,0:T(8,128)(2,1)}, bf16[3,208,768]{2,1,0:T(8,128)(2,1)}, bf16[3,196,768]{2,1,0:T(8,128)(2,1)}, f32[16,768]{1,0:T(8,128)}, f32[1,208,768]{2,1,0:T(8,128)}) custom-call(s32[3]{0:T(128)} %count_ref.11, ...), custom_call_target="tpu_custom_call", output_to_operand_aliasing={{0}: (16, {}), {1}: (17, {}), {2}: (18, {}), {3}: (19, {})} | custom-call | flops 99999997952 | bytes 99999997952 | tf_op jit(solution)/shard_map/late_feed_forward_1/pallas_call | solution.py:288
  97.9 2.9 late_attention_1.1
  100.8 9.3 %grad_down.1 = (bf16[1536,768]{1,0:T(8,128)(2,1)}, bf16[1536,768]{1,0:T(8,128)(2,1)}) custom-call(s32[4]{0:T(128)} %get-tuple-element.371.scalar_ref, bf16[3,208,3072]{2,1,0:T(8,128)(2,1)} %get-tuple-element.258.rest_11_.m_ref, bf16[3,196,768]{2,1,0:T(8,128)(2,1)} %bitcast.57, bf16[1,196,768]{2,1,0:T(8,128)(2,1)} %copy-done, bf16[1,196,768]{2,1,0:T(8,128)(2,1)} %copy-done.1, ...), custom_call_target="tpu_custom_call" | custom-call | flops 99999997952 | bytes 99999997952 | tf_op jit(solution)/shard_map/grad_down/pallas_call | solution.py:288
  111.1 7.5 %late_feed_forward_2.1 = (bf16[3,208,3072]{2,1,0:T(8,128)(2,1)}, bf16[3,208,768]{2,1,0:T(8,128)(2,1)}, bf16[3,196,768]{2,1,0:T(8,128)(2,1)}, f32[16,768]{1,0:T(8,128)}, f32[1,208,768]{2,1,0:T(8,128)}) custom-call(s32[3]{0:T(128)} %count_ref.11, ...), custom_call_target="tpu_custom_call", output_to_operand_aliasing={{0}: (16, {}), {1}: (17, {}), {2}: (18, {}), {3}: (19, {})} | custom-call | flops 99999997952 | bytes 99999997952 | tf_op jit(solution)/shard_map/late_feed_forward_2/pallas_call | solution.py:288
  118.6 8.2 %grad_up.1 = (bf16[1536,768]{1,0:T(8,128)(2,1)}, bf16[1536,768]{1,0:T(8,128)(2,1)}) custom-call(s32[1]{0:T(128)} %bitcast.6.scalar_ref, bf16[624,768]{1,0:T(8,128)(2,1)} %bitcast.69, bf16[624,3072]{1,0:T(8,128)(2,1)} %bitcast.61), custom_call_target="tpu_custom_call" | custom-call | flops 99999997952 | bytes 99999997952 | tf_op jit(solution)/shard_map/grad_up/pallas_call | solution.py:288
  126.8 3.0 halved_1.4
  135.4 2.6 late_attention_2.1
  138.8 5.2 %grad_query_value.1 = (bf16[768,768]{1,0:T(8,128)(2,1)}, bf16[768,768]{1,0:T(8,128)(2,1)}) custom-call(s32[1]{0:T(128)} %bitcast.6.scalar_ref, bf16[624,768]{1,0:T(8,128)(2,1)} %bitcast.66, bf16[624,2304]{1,0:T(8,128)(2,1)} %bitcast.62), custom_call_target="tpu_custom_call" | custom-call | flops 99999997952 | bytes 99999997952 | tf_op jit(solution)/shard_map/grad_query_value/pallas_call | solution.py:288
  144.1 17.7 %collective-permute-done.9.coming_ref = bf16[768,768]{1,0:T(8,128)(2,1)} collective-permute-done((bf16[768,768]{1,0:T(8,128)(2,1)}, bf16[768,768]{1,0:T(8,128)(2,1)}, u32[]{:S(2)}, u32[]{:S(2)}) %collective-permute-start.9) | collective-permute-done | bytes 1179680 | tf_op jit(solution)/shard_map/ppermute | solution.py:882
  165.2 5.8 %grad_key_out.1 = (bf16[768,768]{1,0:T(8,128)(2,1)}, bf16[768,768]{1,0:T(8,128)(2,1)}) custom-call(s32[1]{0:T(128)} %bitcast.6.scalar_ref, bf16[624,768]{1,0:T(8,128)(2,1)} %bitcast.67, bf16[624,2304]{1,0:T(8,128)(2,1)} %bitcast.63, bf16[624,768]{1,0:T(8,128)(2,1)} %bitcast.68, bf16[624,768]{1,0:T(8,128)(2,1)} %bitcast.65), custom_call_target="tpu_custom_call" | custom-call | flops 99999997952 | bytes 99999997952 | tf_op jit(solution)/shard_map/grad_key_out/pallas_call | solution.py:288
  185.5 4.5 %collective-permute-done.15.coming_ref = bf16[384,768]{1,0:T(8,128)(2,1)} collective-permute-done((bf16[384,768]{1,0:T(8,128)(2,1)}, bf16[384,768]{1,0:T(8,128)(2,1)}, u32[]{:S(2)}, u32[]{:S(2)}) %collective-permute-start.15) | collective-permute-done | bytes 589856 | tf_op jit(solution)/shard_map/ppermute | solution.py:882
  199.8 2.9 collective-permute-done.12.coming_ref
  206.1 4.2 %collective-permute-start.16 = (f32[16,768]{1,0:T(8,128)}, f32[16,768]{1,0:T(8,128)}, u32[]{:S(2)}, u32[]{:S(2)}) collective-permute-start(f32[16,768]{1,0:T(8,128)} %added.4.value_ref), channel_id=1, source_target_pairs={{0,2},{2,0},{4,6},{6,4},{8,10},{10,8},{12,14},{14,12},{1,3},{3,1},... | collective-permute-start | bytes 147464 | tf_op jit(solution)/shard_map/ppermute | solution.py:882
  210.3 3.9 %collective-permute-done.20.coming_ref = bf16[192,768]{1,0:T(8,128)(2,1)} collective-permute-done((bf16[192,768]{1,0:T(8,128)(2,1)}, bf16[192,768]{1,0:T(8,128)(2,1)}, u32[]{:S(2)}, u32[]{:S(2)}) %collective-permute-start.20) | collective-permute-done | bytes 294944 | tf_op jit(solution)/shard_map/ppermute | solution.py:882
  216.0 3.2 collective-permute-start.23
  223.1 3.6 %collective-permute-done.17.other_ref = bf16[192,768]{1,0:T(8,128)(2,1)} collective-permute-done((bf16[192,768]{1,0:T(8,128)(2,1)}, bf16[192,768]{1,0:T(8,128)(2,1)}, u32[]{:S(2)}, u32[]{:S(2)}) %collective-permute-start.17) | collective-permute-done | bytes 294944 | tf_op jit(solution)/shard_map/ppermute | solution.py:882
  244.5 11.7 %collective-permute-done.27.other_ref = bf16[384,768]{1,0:T(8,128)(2,1)} collective-permute-done((bf16[384,768]{1,0:T(8,128)(2,1)}, bf16[384,768]{1,0:T(8,128)(2,1)}, u32[]{:S(2)}, u32[]{:S(2)}) %collective-permute-start.27) | collective-permute-done | bytes 589856 | tf_op jit(solution)/shard_map/ppermute | solution.py:882
  258.3 2.9 collective-permute-start.33
  268.9 4.7 %collective-permute-start.32 = (bf16[192,768]{1,0:T(8,128)(2,1)}, bf16[192,768]{1,0:T(8,128)(2,1)}, u32[]{:S(2)}, u32[]{:S(2)}) collective-permute-start(bf16[192,768]{1,0:T(8,128)(2,1)} %joined_4.7.mine_ref), channel_id=1, source_target_pairs={{0,4},{2,6},{4,0},{6,2},{8,12},{10,14},{12,8},{14,10},{1,5},{3,7},... | collective-permute-start | bytes 884744 | tf_op jit(solution)/shard_map/ppermute | solution.py:882
  280.2 5.8 %collective-permute-done.33.refs_1_ = bf16[768,768]{1,0:T(8,128)(2,1)} collective-permute-done((bf16[768,768]{1,0:T(8,128)(2,1)}, bf16[768,768]{1,0:T(8,128)(2,1)}, u32[]{:S(2)}, u32[]{:S(2)}) %collective-permute-start.33) | collective-permute-done | bytes 1179680 | tf_op jit(solution)/shard_map/ppermute | solution.py:882
  286.1 4.4 %collective-permute-start.37 = (bf16[768,768]{1,0:T(8,128)(2,1)}, bf16[768,768]{1,0:T(8,128)(2,1)S(1)}, u32[]{:S(2)}, u32[]{:S(2)}) collective-permute-start(bf16[768,768]{1,0:T(8,128)(2,1)} %collective-permute-done.33.refs_1_), channel_id=1, source_target_pairs={{0,1},{1,0},{2,3},{3,2},{4,5},{5,4},{6,7},{7,6},{8,9},{9,8},{10,11... | collective-permute-start | bytes 3538952 | tf_op jit(solution)/shard_map/ppermute | solution.py:882
  290.4 3.6 %assembled.8.refs_2_ = f32[3072,768]{1,0:T(8,128)} custom-call(bf16[768,768]{1,0:T(8,128)(2,1)} %joined_2.3.refs_0_, bf16[768,768]{1,0:T(8,128)(2,1)} %collective-permute-done.33.refs_1_), custom_call_target="tpu_custom_call" | custom-call | flops 10000000000 | bytes 10000000000 | tf_op jit(solution)/shard_map/assembled/pallas_call | solution.py:859
  295.3 11.6 %collective-permute-done.31.coming_ref = f32[16,768]{1,0:T(8,128)} collective-permute-done((f32[16,768]{1,0:T(8,128)}, f32[16,768]{1,0:T(8,128)}, u32[]{:S(2)}, u32[]{:S(2)}) %collective-permute-start.31) | collective-permute-done | bytes 49184 | tf_op jit(solution)/shard_map/ppermute | solution.py:882
  311.3 2.9 assembled.9
  314.2 2.9 collective-permute-start.39
  320.3 3.6 %assembled.11.refs_2_ = f32[768,3072]{1,0:T(8,128)} custom-call(bf16[768,768]{1,0:T(8,128)(2,1)} %joined_1.1.refs_0_, bf16[768,768]{1,0:T(8,128)(2,1)} %collective-permute-done.40.refs_1_), custom_call_target="tpu_custom_call" | custom-call | flops 10000000000 | bytes 10000000000 | tf_op jit(solution)/shard_map/assembled/pallas_call | solution.py:859
  328.8 2.9 assembled.14
  (126 shorter events, 103.6 us)
Async XLA Ops:
  3.1 18.9 %collective-permute-start = (bf16[1,196,768]{2,1,0:T(8,128)(2,1)}, bf16[1,196,768]{2,1,0:T(8,128)(2,1)S(1)}, u32[]{:S(2)}, u32[]{:S(2)}) collective-permute-start(bf16[1,196,768]{2,1,0:T(8,128)(2,1)} %get-tuple-element.189), channel_id=1, source_target_pairs={{0,16},{1,17},{2,18},{3,19},{4,20},{5,21},{6,22},{7,23},{8,24},{9,... | collective-permute-start | bytes 903176 | tf_op jit(solution)/shard_map/ppermute | solution.py:1094
  7.5 34.6 %collective-permute-start.2 = (bf16[1,196,768]{2,1,0:T(8,128)(2,1)}, bf16[1,196,768]{2,1,0:T(8,128)(2,1)S(1)}, u32[]{:S(2)}, u32[]{:S(2)}) collective-permute-start(bf16[1,196,768]{2,1,0:T(8,128)(2,1)} %get-tuple-element.209), channel_id=1, source_target_pairs={{0,16},{1,17},{2,18},{3,19},{4,20},{5,21},{6,22},{7,23},{8,24},{9,... | collective-permute-start | bytes 903176 | tf_op jit(solution)/shard_map/ppermute | solution.py:1094
  41.7 22.3 %collective-permute-start.1 = (bf16[1,196,768]{2,1,0:T(8,128)(2,1)}, bf16[1,196,768]{2,1,0:T(8,128)(2,1)S(1)}, u32[]{:S(2)}, u32[]{:S(2)}) collective-permute-start(bf16[1,196,768]{2,1,0:T(8,128)(2,1)} %get-tuple-element.208), channel_id=1, source_target_pairs={{16,0},{0,16},{17,1},{1,17},{18,2},{2,18},{19,3},{3,19},{20,4},{4,... | collective-permute-start | bytes 903176 | tf_op jit(solution)/shard_map/ppermute | solution.py:1104
  62.2 24.3 %collective-permute-start.4 = (bf16[1,196,768]{2,1,0:T(8,128)(2,1)}, bf16[1,196,768]{2,1,0:T(8,128)(2,1)S(1)}, u32[]{:S(2)}, u32[]{:S(2)}) collective-permute-start(bf16[1,196,768]{2,1,0:T(8,128)(2,1)} %get-tuple-element.225), channel_id=1, source_target_pairs={{16,0},{17,1},{18,2},{19,3},{20,4},{21,5},{22,6},{23,7},{24,8},{25... | collective-permute-start | bytes 903176 | tf_op jit(solution)/shard_map/ppermute | solution.py:1104
  110.1 16.7 %collective-permute-start.6 = (bf16[1536,768]{1,0:T(8,128)(2,1)}, bf16[1536,768]{1,0:T(8,128)(2,1)}, u32[]{:S(2)}, u32[]{:S(2)}) collective-permute-start(bf16[1536,768]{1,0:T(8,128)(2,1)} %get-tuple-element.259), channel_id=1, source_target_pairs={{0,1},{1,0},{2,3},{3,2},{4,5},{5,4},{6,7},{7,6},{8,9},{9,8},{10,11... | collective-permute-start | bytes 7077896 | tf_op jit(solution)/shard_map/ppermute | solution.py:882
  133.9 38.6 %collective-permute-start.11 = (bf16[768,768]{1,0:T(8,128)(2,1)}, bf16[768,768]{1,0:T(8,128)(2,1)}, u32[]{:S(2)}, u32[]{:S(2)}) collective-permute-start(bf16[768,768]{1,0:T(8,128)(2,1)} %get-tuple-element.274), channel_id=1, source_target_pairs={{0,4},{2,6},{4,0},{6,2},{8,12},{10,14},{12,8},{14,10},{1,5},{3,7},... | collective-permute-start | bytes 3538952 | tf_op jit(solution)/shard_map/ppermute | solution.py:882
  134.0 27.8 %collective-permute-start.9 = (bf16[768,768]{1,0:T(8,128)(2,1)}, bf16[768,768]{1,0:T(8,128)(2,1)}, u32[]{:S(2)}, u32[]{:S(2)}) collective-permute-start(bf16[768,768]{1,0:T(8,128)(2,1)} %get-tuple-element.272), channel_id=1, source_target_pairs={{0,2},{2,0},{4,6},{6,4},{8,10},{10,8},{12,14},{14,12},{1,3},{3,1},... | collective-permute-start | bytes 3538952 | tf_op jit(solution)/shard_map/ppermute | solution.py:882
  138.1 66.6 %collective-permute-start.7 = (f32[16,768]{1,0:T(8,128)}, f32[16,768]{1,0:T(8,128)}, u32[]{:S(2)}, u32[]{:S(2)}) collective-permute-start(f32[16,768]{1,0:T(8,128)} %get-tuple-element.281.value_ref), channel_id=1, source_target_pairs={{0,1},{1,0},{2,3},{3,2},{4,5},{5,4},{6,7},{7,6},{8,9},{9,8},{10,11... | collective-permute-start | bytes 147464 | tf_op jit(solution)/shard_map/ppermute | solution.py:882
  144.1 38.0 %collective-permute-start.8 = (bf16[768,768]{1,0:T(8,128)(2,1)}, bf16[768,768]{1,0:T(8,128)(2,1)}, u32[]{:S(2)}, u32[]{:S(2)}) collective-permute-start(bf16[768,768]{1,0:T(8,128)(2,1)} %get-tuple-element.286), channel_id=1, source_target_pairs={{0,1},{1,0},{2,3},{3,2},{4,5},{5,4},{6,7},{7,6},{8,9},{9,8},{10,11... | collective-permute-start | bytes 3538952 | tf_op jit(solution)/shard_map/ppermute | solution.py:882
  171.0 23.4 %collective-permute-start.14 = (bf16[768,768]{1,0:T(8,128)(2,1)}, bf16[768,768]{1,0:T(8,128)(2,1)}, u32[]{:S(2)}, u32[]{:S(2)}) collective-permute-start(bf16[768,768]{1,0:T(8,128)(2,1)} %get-tuple-element.294), channel_id=1, source_target_pairs={{0,1},{1,0},{2,3},{3,2},{4,5},{5,4},{6,7},{7,6},{8,9},{9,8},{10,11... | collective-permute-start | bytes 3538952 | tf_op jit(solution)/shard_map/ppermute | solution.py:882
  180.2 17.6 %collective-permute-start.13 = (bf16[192,768]{1,0:T(8,128)(2,1)}, bf16[192,768]{1,0:T(8,128)(2,1)}, u32[]{:S(2)}, u32[]{:S(2)}) collective-permute-start(bf16[192,768]{1,0:T(8,128)(2,1)} %get-tuple-element.298), channel_id=1, source_target_pairs={{0,8},{2,10},{4,12},{6,14},{8,0},{10,2},{12,4},{14,6},{1,9},{3,11}... | collective-permute-start | bytes 884744 | tf_op jit(solution)/shard_map/ppermute | solution.py:882
  184.2 18.5 %collective-permute-start.12 = (bf16[384,768]{1,0:T(8,128)(2,1)}, bf16[384,768]{1,0:T(8,128)(2,1)}, u32[]{:S(2)}, u32[]{:S(2)}) collective-permute-start(bf16[384,768]{1,0:T(8,128)(2,1)} %get-tuple-element.301), channel_id=1, source_target_pairs={{0,2},{2,0},{4,6},{6,4},{8,10},{10,8},{12,14},{14,12},{1,3},{3,1},... | collective-permute-start | bytes 1769480 | tf_op jit(solution)/shard_map/ppermute | solution.py:882
  192.0 22.2 %collective-permute-start.20 = (bf16[192,768]{1,0:T(8,128)(2,1)}, bf16[192,768]{1,0:T(8,128)(2,1)}, u32[]{:S(2)}, u32[]{:S(2)}) collective-permute-start(bf16[192,768]{1,0:T(8,128)(2,1)} %get-tuple-element.306), channel_id=1, source_target_pairs={{0,8},{2,10},{4,12},{6,14},{8,0},{10,2},{12,4},{14,6},{1,9},{3,11}... | collective-permute-start | bytes 884744 | tf_op jit(solution)/shard_map/ppermute | solution.py:882
  196.6 22.7 %collective-permute-start.19 = (bf16[384,768]{1,0:T(8,128)(2,1)}, bf16[384,768]{1,0:T(8,128)(2,1)}, u32[]{:S(2)}, u32[]{:S(2)}) collective-permute-start(bf16[384,768]{1,0:T(8,128)(2,1)} %get-tuple-element.308), channel_id=1, source_target_pairs={{0,2},{2,0},{4,6},{6,4},{8,10},{10,8},{12,14},{14,12},{1,3},{3,1},... | collective-permute-start | bytes 1769480 | tf_op jit(solution)/shard_map/ppermute | solution.py:882
  199.7 27.0 %collective-permute-start.17 = (bf16[192,768]{1,0:T(8,128)(2,1)}, bf16[192,768]{1,0:T(8,128)(2,1)}, u32[]{:S(2)}, u32[]{:S(2)}) collective-permute-start(bf16[192,768]{1,0:T(8,128)(2,1)} %summed.4.mine_ref), channel_id=1, source_target_pairs={{0,8},{2,10},{4,12},{6,14},{8,0},{10,2},{12,4},{14,6},{1,9},{3,11}... | collective-permute-start | bytes 884744 | tf_op jit(solution)/shard_map/ppermute | solution.py:882
  204.5 16.6 %collective-permute-start.18 = (bf16[192,768]{1,0:T(8,128)(2,1)}, bf16[192,768]{1,0:T(8,128)(2,1)}, u32[]{:S(2)}, u32[]{:S(2)}) collective-permute-start(bf16[192,768]{1,0:T(8,128)(2,1)} %get-tuple-element.311), channel_id=1, source_target_pairs={{0,4},{2,6},{4,0},{6,2},{8,12},{10,14},{12,8},{14,10},{1,5},{3,7},... | collective-permute-start | bytes 884744 | tf_op jit(solution)/shard_map/ppermute | solution.py:882
  206.1 23.6 %collective-permute-start.16 = (f32[16,768]{1,0:T(8,128)}, f32[16,768]{1,0:T(8,128)}, u32[]{:S(2)}, u32[]{:S(2)}) collective-permute-start(f32[16,768]{1,0:T(8,128)} %added.4.value_ref), channel_id=1, source_target_pairs={{0,2},{2,0},{4,6},{6,4},{8,10},{10,8},{12,14},{14,12},{1,3},{3,1},... | collective-permute-start | bytes 147464 | tf_op jit(solution)/shard_map/ppermute | solution.py:882
  216.0 22.0 %collective-permute-start.23 = (bf16[192,768]{1,0:T(8,128)(2,1)}, bf16[192,768]{1,0:T(8,128)(2,1)}, u32[]{:S(2)}, u32[]{:S(2)}) collective-permute-start(bf16[192,768]{1,0:T(8,128)(2,1)} %summed.5.mine_ref), channel_id=1, source_target_pairs={{0,8},{2,10},{4,12},{6,14},{8,0},{10,2},{12,4},{14,6},{1,9},{3,11}... | collective-permute-start | bytes 884744 | tf_op jit(solution)/shard_map/ppermute | solution.py:882
  223.0 17.7 %collective-permute-start.22 = (bf16[96,768]{1,0:T(8,128)(2,1)}, bf16[96,768]{1,0:T(8,128)(2,1)}, u32[]{:S(2)}, u32[]{:S(2)}) collective-permute-start(bf16[96,768]{1,0:T(8,128)(2,1)} %get-tuple-element.320), channel_id=1, source_target_pairs={{0,8},{2,10},{4,12},{6,14},{8,0},{10,2},{12,4},{14,6},{1,9},{3,11}... | collective-permute-start | bytes 442376 | tf_op jit(solution)/shard_map/ppermute | solution.py:882
  228.6 27.6 %collective-permute-start.27 = (bf16[384,768]{1,0:T(8,128)(2,1)}, bf16[384,768]{1,0:T(8,128)(2,1)}, u32[]{:S(2)}, u32[]{:S(2)}) collective-permute-start(bf16[384,768]{1,0:T(8,128)(2,1)} %joined_4.4.mine_ref), channel_id=1, source_target_pairs={{0,4},{2,6},{4,0},{6,2},{8,12},{10,14},{12,8},{14,10},{1,5},{3,7},... | collective-permute-start | bytes 1769480 | tf_op jit(solution)/shard_map/ppermute | solution.py:882
  231.2 46.0 %collective-permute-start.21 = (f32[16,768]{1,0:T(8,128)}, f32[16,768]{1,0:T(8,128)}, u32[]{:S(2)}, u32[]{:S(2)}) collective-permute-start(f32[16,768]{1,0:T(8,128)} %added.5.value_ref), channel_id=1, source_target_pairs={{0,4},{2,6},{4,0},{6,2},{8,12},{10,14},{12,8},{14,10},{1,5},{3,7},... | collective-permute-start | bytes 147464 | tf_op jit(solution)/shard_map/ppermute | solution.py:882
  235.4 25.8 %collective-permute-start.26 = (bf16[96,768]{1,0:T(8,128)(2,1)}, bf16[96,768]{1,0:T(8,128)(2,1)}, u32[]{:S(2)}, u32[]{:S(2)}) collective-permute-start(bf16[96,768]{1,0:T(8,128)(2,1)} %get-tuple-element.326), channel_id=1, source_target_pairs={{0,8},{2,10},{4,12},{6,14},{8,0},{10,2},{12,4},{14,6},{1,9},{3,11}... | collective-permute-start | bytes 442376 | tf_op jit(solution)/shard_map/ppermute | solution.py:882
  239.8 33.9 %collective-permute-start.29 = (bf16[384,768]{1,0:T(8,128)(2,1)}, bf16[384,768]{1,0:T(8,128)(2,1)}, u32[]{:S(2)}, u32[]{:S(2)}) collective-permute-start(bf16[384,768]{1,0:T(8,128)(2,1)} %joined_4.5.mine_ref), channel_id=1, source_target_pairs={{0,2},{2,0},{4,6},{6,4},{8,10},{10,8},{12,14},{14,12},{1,3},{3,1},... | collective-permute-start | bytes 1769480 | tf_op jit(solution)/shard_map/ppermute | solution.py:882
  242.5 21.2 %collective-permute-start.25 = (bf16[96,768]{1,0:T(8,128)(2,1)}, bf16[96,768]{1,0:T(8,128)(2,1)}, u32[]{:S(2)}, u32[]{:S(2)}) collective-permute-start(bf16[96,768]{1,0:T(8,128)(2,1)} %summed.6.mine_ref), channel_id=1, source_target_pairs={{0,8},{2,10},{4,12},{6,14},{8,0},{10,2},{12,4},{14,6},{1,9},{3,11}... | collective-permute-start | bytes 442376 | tf_op jit(solution)/shard_map/ppermute | solution.py:882
  258.3 27.7 %collective-permute-start.33 = (bf16[768,768]{1,0:T(8,128)(2,1)}, bf16[768,768]{1,0:T(8,128)(2,1)}, u32[]{:S(2)}, u32[]{:S(2)}) collective-permute-start(bf16[768,768]{1,0:T(8,128)(2,1)} %joined_2.3.refs_0_), channel_id=1, source_target_pairs={{0,2},{2,0},{4,6},{6,4},{8,10},{10,8},{12,14},{14,12},{1,3},{3,1},... | collective-permute-start | bytes 3538952 | tf_op jit(solution)/shard_map/ppermute | solution.py:882
  268.9 25.1 %collective-permute-start.32 = (bf16[192,768]{1,0:T(8,128)(2,1)}, bf16[192,768]{1,0:T(8,128)(2,1)}, u32[]{:S(2)}, u32[]{:S(2)}) collective-permute-start(bf16[192,768]{1,0:T(8,128)(2,1)} %joined_4.7.mine_ref), channel_id=1, source_target_pairs={{0,4},{2,6},{4,0},{6,2},{8,12},{10,14},{12,8},{14,10},{1,5},{3,7},... | collective-permute-start | bytes 884744 | tf_op jit(solution)/shard_map/ppermute | solution.py:882
  275.8 43.8 %collective-permute-start.40 = (bf16[768,768]{1,0:T(8,128)(2,1)}, bf16[768,768]{1,0:T(8,128)(2,1)}, u32[]{:S(2)}, u32[]{:S(2)}) collective-permute-start(bf16[768,768]{1,0:T(8,128)(2,1)} %joined_1.1.refs_0_), channel_id=1, source_target_pairs={{0,4},{2,6},{4,0},{6,2},{8,12},{10,14},{12,8},{14,10},{1,5},{3,7},... | collective-permute-start | bytes 3538952 | tf_op jit(solution)/shard_map/ppermute | solution.py:882
  277.1 37.1 %collective-permute-start.35 = (bf16[384,768]{1,0:T(8,128)(2,1)S(1)}, bf16[384,768]{1,0:T(8,128)(2,1)}, u32[]{:S(2)}, u32[]{:S(2)}) collective-permute-start(bf16[384,768]{1,0:T(8,128)(2,1)S(1)} %joined_2.4.refs_0_), channel_id=1, source_target_pairs={{0,2},{2,0},{4,6},{6,4},{8,10},{10,8},{12,14},{14,12},{1,3},{3,1},... | collective-permute-start | bytes 1769480 | tf_op jit(solution)/shard_map/ppermute | solution.py:882
  278.6 28.3 %collective-permute-start.31 = (f32[16,768]{1,0:T(8,128)}, f32[16,768]{1,0:T(8,128)}, u32[]{:S(2)}, u32[]{:S(2)}) collective-permute-start(f32[16,768]{1,0:T(8,128)} %added.6.value_ref), channel_id=1, source_target_pairs={{0,8},{2,10},{4,12},{6,14},{8,0},{10,2},{12,4},{14,6},{1,9},{3,11}... | collective-permute-start | bytes 147464 | tf_op jit(solution)/shard_map/ppermute | solution.py:882
  286.1 25.2 %collective-permute-start.37 = (bf16[768,768]{1,0:T(8,128)(2,1)}, bf16[768,768]{1,0:T(8,128)(2,1)S(1)}, u32[]{:S(2)}, u32[]{:S(2)}) collective-permute-start(bf16[768,768]{1,0:T(8,128)(2,1)} %collective-permute-done.33.refs_1_), channel_id=1, source_target_pairs={{0,1},{1,0},{2,3},{3,2},{4,5},{5,4},{6,7},{7,6},{8,9},{9,8},{10,11... | collective-permute-start | bytes 3538952 | tf_op jit(solution)/shard_map/ppermute | solution.py:882
  294.1 17.2 %collective-permute-start.36 = (bf16[768,768]{1,0:T(8,128)(2,1)}, bf16[768,768]{1,0:T(8,128)(2,1)S(1)}, u32[]{:S(2)}, u32[]{:S(2)}) collective-permute-start(bf16[768,768]{1,0:T(8,128)(2,1)} %joined_2.3.refs_0_), channel_id=1, source_target_pairs={{0,1},{1,0},{2,3},{3,2},{4,5},{5,4},{6,7},{7,6},{8,9},{9,8},{10,11... | collective-permute-start | bytes 3538952 | tf_op jit(solution)/shard_map/ppermute | solution.py:882
  306.9 18.9 %collective-permute-start.34 = (bf16[384,768]{1,0:T(8,128)(2,1)S(1)}, bf16[384,768]{1,0:T(8,128)(2,1)}, u32[]{:S(2)}, u32[]{:S(2)}) collective-permute-start(bf16[384,768]{1,0:T(8,128)(2,1)S(1)} %joined_2.5.refs_0_), channel_id=1, source_target_pairs={{0,2},{2,0},{4,6},{6,4},{8,10},{10,8},{12,14},{14,12},{1,3},{3,1},... | collective-permute-start | bytes 1769480 | tf_op jit(solution)/shard_map/ppermute | solution.py:882
  (20 other events, 179.7 us)

commit v5 on v4

--- a/solution.py
+++ b/solution.py
@@ -816,17 +816,16 @@
     )
 
 
-def plain_call(kernel, ins, outs, scratch, name, out_specs=None):
+def plain_call(kernel, ins, outs, name):
     return pl.pallas_call(
         kernel,
         out_shape=outs,
-        in_specs=[ANY] * len(ins),
-        out_specs=out_specs or [pl.BlockSpec(memory_space=pltpu.VMEM)] * len(outs),
-        scratch_shapes=scratch,
+        in_specs=[pl.BlockSpec(memory_space=pltpu.VMEM)] * len(ins),
+        out_specs=[pl.BlockSpec(memory_space=pltpu.VMEM)] * len(outs),
         compiler_params=pltpu.CompilerParams(vmem_limit_bytes=16 << 20),
         cost_estimate=pl.CostEstimate(flops=COST, bytes_accessed=COST, transcendentals=0),
         name=name,
-    )(*ins)
+    )(*(in_vmem(value) for value in ins))
 
 
 def assembled(own, stride, pieces, places, shapes, before):
@@ -894,63 +893,24 @@
         send = lax.dynamic_slice_in_dim(pair, (1 - bit) * height, height, axis=0)
         return send, lax.dynamic_slice_in_dim(pair, bit * height, height, axis=0)
 
-    def kernel(keep_ref, coming_ref, send_ref, stay_ref, kept, came, made, sem):
+    def kernel(keep_ref, coming_ref, send_ref, stay_ref):
         bit = bit_of(DP, stride)
-        copies = []
-        for at, half in enumerate((1 - bit, bit)):
+        for half, out_ref in ((1 - bit, send_ref), (bit, stay_ref)):
             rows = pl.ds(pl.multiple_of(half * height, ROW_TILE), height)
-            copies.append(pltpu.make_async_copy(keep_ref.at[rows, :], kept.at[at], sem.at[2 * at]))
-            copies.append(pltpu.make_async_copy(coming_ref.at[rows, :], came.at[at], sem.at[2 * at + 1]))
-        for copy in copies:
-            copy.start()
-        for copy in copies[:2]:
-            copy.wait()
-        made[...] = (kept[0].astype(f32) + came[0].astype(f32)).astype(bf16)
-        store = pltpu.make_async_copy(made, send_ref, sem.at[4])
-        store.start()
-        for copy in copies[2:]:
-            copy.wait()
-        stay_ref[...] = (kept[1].astype(f32) + came[1].astype(f32)).astype(bf16)
-        store.wait()
-
-    shape = (height, width)
-    return plain_call(
-        kernel,
-        (keep, coming),
-        [jax.ShapeDtypeStruct(shape, bf16)] * 2,
-        [
-            pltpu.VMEM((2,) + shape, bf16),
-            pltpu.VMEM((2,) + shape, bf16),
-            pltpu.VMEM(shape, bf16),
-            pltpu.SemaphoreType.DMA((5,)),
-        ],
-        f"halved_{stride}",
-        [ANY, pl.BlockSpec(memory_space=pltpu.VMEM)],
-    )
+            out_ref[...] = (keep_ref[rows, :].astype(f32) + coming_ref[rows, :].astype(f32)).astype(bf16)
+
+    shape = jax.ShapeDtypeStruct((height, width), bf16)
+    return plain_call(kernel, (keep, coming), [shape] * 2, f"halved_{stride}")
 
 
 def summed(keep, coming, total):
     if keep.shape[0] % ROW_TILE:
         return ((keep.astype(f32) + coming.astype(f32)) / total).astype(bf16)
 
-    def kernel(keep_ref, coming_ref, out_ref, kept, came, sem):
-        copies = [
-            pltpu.make_async_copy(keep_ref, kept, sem.at[0]),
-            pltpu.make_async_copy(coming_ref, came, sem.at[1]),
-        ]
-        for copy in copies:
-            copy.start()
-        for copy in copies:
-            copy.wait()
-        out_ref[...] = ((kept[...].astype(f32) + came[...].astype(f32)) / total).astype(bf16)
-
-    return plain_call(
-        kernel,
-        (keep, coming),
-        [jax.ShapeDtypeStruct(keep.shape, bf16)],
-        [pltpu.VMEM(keep.shape, bf16), pltpu.VMEM(keep.shape, bf16), pltpu.SemaphoreType.DMA((2,))],
-        "summed",
-    )[0]
+    def kernel(keep_ref, coming_ref, out_ref):
+        out_ref[...] = ((keep_ref[...].astype(f32) + coming_ref[...].astype(f32)) / total).astype(bf16)
+
+    return plain_call(kernel, (keep, coming), [jax.ShapeDtypeStruct(keep.shape, bf16)], "summed")[0]
 
 
 def joined(mine, other, stride):
@@ -959,29 +919,13 @@
         first = bit_of(DP, stride) == 0
         return jnp.concatenate([jnp.where(first, mine, other), jnp.where(first, other, mine)], axis=0)
 
-    def kernel(mine_ref, other_ref, out_ref, held, sem):
+    def kernel(mine_ref, other_ref, out_ref):
         bit = bit_of(DP, stride)
-        loads, stores = [], []
-        for at, (half, source) in enumerate(((bit, mine_ref), (1 - bit, other_ref))):
-            rows = pl.ds(pl.multiple_of(half * height, ROW_TILE), height)
-            loads.append(pltpu.make_async_copy(source, held.at[at], sem.at[at]))
-            stores.append(pltpu.make_async_copy(held.at[at], out_ref.at[rows, :], sem.at[2 + at]))
-        for load in loads:
-            load.start()
-        for load, store in zip(loads, stores):
-            load.wait()
-            store.start()
-        for store in stores:
-            store.wait()
-
-    return plain_call(
-        kernel,
-        (mine, other),
-        [jax.ShapeDtypeStruct((2 * height, width), bf16)],
-        [pltpu.VMEM((2, height, width), bf16), pltpu.SemaphoreType.DMA((4,))],
-        f"joined_{stride}",
-        [ANY],
-    )[0]
+        for half, source in ((bit, mine_ref), (1 - bit, other_ref)):
+            out_ref[pl.ds(pl.multiple_of(half * height, ROW_TILE), height), :] = source[...]
+
+    shape = jax.ShapeDtypeStruct((2 * height, width), bf16)
+    return plain_call(kernel, (mine, other), [shape], f"joined_{stride}")[0]
 
 
 def strides_of(size):

time: 340 us -> 340 us (level)
  starting transfers between devices: 56.9 us -> 51.7 us
  waiting for transfers between devices: 81.9 us -> 86.9 us
    ppermute x40, starting transfers between devices: 50.2 us -> 44.9 us  [swapped(): return lax.ppermute(value, axis, [(i, i ^ stride) for i in range(length)])]
    ppermute x40, waiting for transfers between devices: 69.2 us -> 74.2 us  [swapped(): return lax.ppermute(value, axis, [(i, i ^ stride) for i in range(length)])]
  transfers between devices with their start and end apart: 45 -> 45, of which waited for: 13 -> 13; matrix products, arithmetic and copies ran while one was open for 1% -> 1% of each run, Pallas kernels for 52% -> 53%
where the time goes in v5:
time: 340 us; the launch traced here: 333 us
  Pallas kernels  190 us (56%)
  waiting for transfers between devices  86.9 us (26%)
  starting transfers between devices  51.7 us (15%)
    pallas_call x13, Pallas kernels, call(): pl.pallas_call(kernel, out_shape=outs, grid_spec=pltpu.PrefetchScalarGrid...  119 us
    ppermute x40, waiting for transfers between devices, swapped(): return lax.ppermute(value, axis, [(i, i ^ stride) for i in range(length)])  74.2 us
    ppermute x40, starting transfers between devices, swapped(): return lax.ppermute(value, axis, [(i, i ^ stride) for i in range(length)])  44.9 us
    pallas_call x24, Pallas kernels, plain_call(): pl.pallas_call(kernel, out_shape=outs, in_specs=[pl.BlockSpec(memory_spac...  44.3 us
    pallas_call x8, Pallas kernels, assembled(): pl.pallas_call(kernel, out_shape=[jax.ShapeDtypeStruct(whole, f32) for wh...  21.6 us
    ppermute x2, waiting for transfers between devices, shards(): received.append(lax.ppermute(first_output, SECTION, [(0, 1)]))  12.7 us
  transfers between devices with their start and end apart: 45, of which 13 were waited for; matrix products, arithmetic and copies ran while one was open for 1% of the time, Pallas kernels for 53%

profile of v5, /device:TPU:11, one launch (start us, length us, event | category | flops | bytes accessed | tf_op | source)
XLA Modules:
  0.0 332.8 jit_solution(17309732952009056834)
XLA Ops:
  4.5 3.0 first_forward_1.1
  9.4 12.7 %collective-permute-done.received_ref = bf16[1,196,768]{2,1,0:T(8,128)(2,1)S(1)} collective-permute-done((bf16[1,196,768]{2,1,0:T(8,128)(2,1)}, bf16[1,196,768]{2,1,0:T(8,128)(2,1)S(1)}, u32[]{:S(2)}, u32[]{:S(2)}) %collective-permute-start) | collective-permute-done | bytes 301088 | tf_op jit(solution)/shard_map/ppermute | solution.py:1038
  22.0 19.6 %tick_0.1 = (bf16[3,208,768]{2,1,0:T(8,128)(2,1)}, bf16[3,208,768]{2,1,0:T(8,128)(2,1)}, bf16[3,208,2304]{2,1,0:T(8,128)(2,1)}, bf16[3,208,768]{2,1,0:T(8,128)(2...) custom-call(s32[4]{0:T(128)} %get-tuple-element.372.scalar_ref, ...), custom_call_target="tpu_custom_call", output_to_operand_aliasing={{0}: (17, {}), {1}: (18, {}), {2}: (19, {}), {3}: (20, {}),... | custom-call | flops 99999997952 | bytes 99999997952 | tf_op jit(solution)/shard_map/tick_0/pallas_call | solution.py:288
  42.1 20.1 %tick_1.1 = (bf16[3,208,768]{2,1,0:T(8,128)(2,1)}, bf16[3,208,768]{2,1,0:T(8,128)(2,1)}, bf16[3,208,2304]{2,1,0:T(8,128)(2,1)}, bf16[3,208,768]{2,1,0:T(8,128)(2...) custom-call(s32[4]{0:T(128)} %get-tuple-element.372.scalar_ref, ...), custom_call_target="tpu_custom_call", output_to_operand_aliasing={{0}: (17, {}), {1}: (18, {}), {2}: (19, {}), {3}: (20, {}),... | custom-call | flops 99999997952 | bytes 99999997952 | tf_op jit(solution)/shard_map/tick_1/pallas_call | solution.py:288
  64.0 20.5 %tick_2.1 = (bf16[3,208,768]{2,1,0:T(8,128)(2,1)}, bf16[3,208,768]{2,1,0:T(8,128)(2,1)}, bf16[3,208,2304]{2,1,0:T(8,128)(2,1)}, bf16[3,208,768]{2,1,0:T(8,128)(2...) custom-call(s32[4]{0:T(128)} %get-tuple-element.372.scalar_ref, ...), custom_call_target="tpu_custom_call", output_to_operand_aliasing={{0}: (17, {}), {1}: (18, {}), {2}: (19, {}), {3}: (20, {}),... | custom-call | flops 99999997952 | bytes 99999997952 | tf_op jit(solution)/shard_map/tick_2/pallas_call | solution.py:288
  86.5 11.4 %late_feed_forward_1.1 = (bf16[3,208,3072]{2,1,0:T(8,128)(2,1)}, bf16[3,208,768]{2,1,0:T(8,128)(2,1)}, bf16[3,196,768]{2,1,0:T(8,128)(2,1)}, f32[16,768]{1,0:T(8,128)}, f32[1,208,768]{2,1,0:T(8,128)}) custom-call(s32[3]{0:T(128)} %count_ref.11, ...), custom_call_target="tpu_custom_call", output_to_operand_aliasing={{0}: (16, {}), {1}: (17, {}), {2}: (18, {}), {3}: (19, {})} | custom-call | flops 99999997952 | bytes 99999997952 | tf_op jit(solution)/shard_map/late_feed_forward_1/pallas_call | solution.py:288
  97.9 2.9 late_attention_1.1
  100.8 9.3 %grad_down.1 = (bf16[1536,768]{1,0:T(8,128)(2,1)}, bf16[1536,768]{1,0:T(8,128)(2,1)}) custom-call(s32[4]{0:T(128)} %get-tuple-element.371.scalar_ref, bf16[3,208,3072]{2,1,0:T(8,128)(2,1)} %get-tuple-element.258.rest_11_.m_ref, bf16[3,196,768]{2,1,0:T(8,128)(2,1)} %bitcast.57, bf16[1,196,768]{2,1,0:T(8,128)(2,1)} %copy-done, bf16[1,196,768]{2,1,0:T(8,128)(2,1)} %copy-done.1, ...), custom_call_target="tpu_custom_call" | custom-call | flops 99999997952 | bytes 99999997952 | tf_op jit(solution)/shard_map/grad_down/pallas_call | solution.py:288
  111.1 7.5 %late_feed_forward_2.1 = (bf16[3,208,3072]{2,1,0:T(8,128)(2,1)}, bf16[3,208,768]{2,1,0:T(8,128)(2,1)}, bf16[3,196,768]{2,1,0:T(8,128)(2,1)}, f32[16,768]{1,0:T(8,128)}, f32[1,208,768]{2,1,0:T(8,128)}) custom-call(s32[3]{0:T(128)} %count_ref.11, ...), custom_call_target="tpu_custom_call", output_to_operand_aliasing={{0}: (16, {}), {1}: (17, {}), {2}: (18, {}), {3}: (19, {})} | custom-call | flops 99999997952 | bytes 99999997952 | tf_op jit(solution)/shard_map/late_feed_forward_2/pallas_call | solution.py:288
  118.6 8.2 %grad_up.1 = (bf16[1536,768]{1,0:T(8,128)(2,1)}, bf16[1536,768]{1,0:T(8,128)(2,1)}) custom-call(s32[1]{0:T(128)} %bitcast.6.scalar_ref, bf16[624,768]{1,0:T(8,128)(2,1)} %bitcast.69, bf16[624,3072]{1,0:T(8,128)(2,1)} %bitcast.61), custom_call_target="tpu_custom_call" | custom-call | flops 99999997952 | bytes 99999997952 | tf_op jit(solution)/shard_map/grad_up/pallas_call | solution.py:288
  126.8 3.3 halved_1.4
  134.6 2.6 late_attention_2.1
  138.0 5.2 %grad_query_value.1 = (bf16[768,768]{1,0:T(8,128)(2,1)}, bf16[768,768]{1,0:T(8,128)(2,1)}) custom-call(s32[1]{0:T(128)} %bitcast.6.scalar_ref, bf16[624,768]{1,0:T(8,128)(2,1)} %bitcast.66, bf16[624,2304]{1,0:T(8,128)(2,1)} %bitcast.62), custom_call_target="tpu_custom_call" | custom-call | flops 99999997952 | bytes 99999997952 | tf_op jit(solution)/shard_map/grad_query_value/pallas_call | solution.py:288
  143.2 17.6 %collective-permute-done.9.coming_ref = bf16[768,768]{1,0:T(8,128)(2,1)} collective-permute-done((bf16[768,768]{1,0:T(8,128)(2,1)}, bf16[768,768]{1,0:T(8,128)(2,1)}, u32[]{:S(2)}, u32[]{:S(2)}) %collective-permute-start.9) | collective-permute-done | bytes 1179680 | tf_op jit(solution)/shard_map/ppermute | solution.py:881
  164.3 5.8 %grad_key_out.1 = (bf16[768,768]{1,0:T(8,128)(2,1)}, bf16[768,768]{1,0:T(8,128)(2,1)}) custom-call(s32[1]{0:T(128)} %bitcast.6.scalar_ref, bf16[624,768]{1,0:T(8,128)(2,1)} %bitcast.67, bf16[624,2304]{1,0:T(8,128)(2,1)} %bitcast.63, bf16[624,768]{1,0:T(8,128)(2,1)} %bitcast.68, bf16[624,768]{1,0:T(8,128)(2,1)} %bitcast.65), custom_call_target="tpu_custom_call" | custom-call | flops 99999997952 | bytes 99999997952 | tf_op jit(solution)/shard_map/grad_key_out/pallas_call | solution.py:288
  184.7 4.6 %collective-permute-done.15.coming_ref = bf16[384,768]{1,0:T(8,128)(2,1)} collective-permute-done((bf16[384,768]{1,0:T(8,128)(2,1)}, bf16[384,768]{1,0:T(8,128)(2,1)}, u32[]{:S(2)}, u32[]{:S(2)}) %collective-permute-start.15) | collective-permute-done | bytes 589856 | tf_op jit(solution)/shard_map/ppermute | solution.py:881
  198.9 3.0 collective-permute-done.12.coming_ref
  205.2 3.9 %collective-permute-start.16 = (f32[16,768]{1,0:T(8,128)}, f32[16,768]{1,0:T(8,128)}, u32[]{:S(2)}, u32[]{:S(2)}) collective-permute-start(f32[16,768]{1,0:T(8,128)} %added.4.value_ref), channel_id=1, source_target_pairs={{0,2},{2,0},{4,6},{6,4},{8,10},{10,8},{12,14},{14,12},{1,3},{3,1},... | collective-permute-start | bytes 147464 | tf_op jit(solution)/shard_map/ppermute | solution.py:881
  209.1 4.3 %collective-permute-done.20.coming_ref = bf16[192,768]{1,0:T(8,128)(2,1)} collective-permute-done((bf16[192,768]{1,0:T(8,128)(2,1)}, bf16[192,768]{1,0:T(8,128)(2,1)}, u32[]{:S(2)}, u32[]{:S(2)}) %collective-permute-start.20) | collective-permute-done | bytes 294944 | tf_op jit(solution)/shard_map/ppermute | solution.py:881
  215.2 3.1 collective-permute-start.23
  221.8 4.3 %collective-permute-done.17.other_ref = bf16[192,768]{1,0:T(8,128)(2,1)} collective-permute-done((bf16[192,768]{1,0:T(8,128)(2,1)}, bf16[192,768]{1,0:T(8,128)(2,1)}, u32[]{:S(2)}, u32[]{:S(2)}) %collective-permute-start.17) | collective-permute-done | bytes 294944 | tf_op jit(solution)/shard_map/ppermute | solution.py:881
  230.9 2.6 collective-permute-done.24.coming_ref
  243.5 12.3 %collective-permute-done.27.other_ref = bf16[384,768]{1,0:T(8,128)(2,1)} collective-permute-done((bf16[384,768]{1,0:T(8,128)(2,1)}, bf16[384,768]{1,0:T(8,128)(2,1)}, u32[]{:S(2)}, u32[]{:S(2)}) %collective-permute-start.27) | collective-permute-done | bytes 589856 | tf_op jit(solution)/shard_map/ppermute | solution.py:881
  265.4 3.9 %collective-permute-done.30.other_ref = bf16[96,768]{1,0:T(8,128)(2,1)S(1)} collective-permute-done((bf16[96,768]{1,0:T(8,128)(2,1)S(1)}, bf16[96,768]{1,0:T(8,128)(2,1)S(1)}, u32[]{:S(2)}, u32[]{:S(2)}) %collective-permute-start.30) | collective-permute-done | bytes 147488 | tf_op jit(solution)/shard_map/ppermute | solution.py:881
  279.7 5.4 %collective-permute-done.33.refs_1_ = bf16[768,768]{1,0:T(8,128)(2,1)} collective-permute-done((bf16[768,768]{1,0:T(8,128)(2,1)}, bf16[768,768]{1,0:T(8,128)(2,1)}, u32[]{:S(2)}, u32[]{:S(2)}) %collective-permute-start.33) | collective-permute-done | bytes 1179680 | tf_op jit(solution)/shard_map/ppermute | solution.py:881
  285.1 4.7 %collective-permute-start.37 = (bf16[768,768]{1,0:T(8,128)(2,1)}, bf16[768,768]{1,0:T(8,128)(2,1)S(1)}, u32[]{:S(2)}, u32[]{:S(2)}) collective-permute-start(bf16[768,768]{1,0:T(8,128)(2,1)} %collective-permute-done.33.refs_1_), channel_id=1, source_target_pairs={{0,1},{1,0},{2,3},{3,2},{4,5},{5,4},{6,7},{7,6},{8,9},{9,8},{10,11... | collective-permute-start | bytes 3538952 | tf_op jit(solution)/shard_map/ppermute | solution.py:881
  289.8 3.6 %assembled.8.refs_2_ = f32[3072,768]{1,0:T(8,128)} custom-call(bf16[768,768]{1,0:T(8,128)(2,1)} %joined_2.3.refs_0_, bf16[768,768]{1,0:T(8,128)(2,1)} %collective-permute-done.33.refs_1_), custom_call_target="tpu_custom_call" | custom-call | flops 10000000000 | bytes 10000000000 | tf_op jit(solution)/shard_map/assembled/pallas_call | solution.py:858
  294.6 12.6 %collective-permute-done.31.coming_ref = f32[16,768]{1,0:T(8,128)} collective-permute-done((f32[16,768]{1,0:T(8,128)}, f32[16,768]{1,0:T(8,128)}, u32[]{:S(2)}, u32[]{:S(2)}) %collective-permute-start.31) | collective-permute-done | bytes 49184 | tf_op jit(solution)/shard_map/ppermute | solution.py:881
  310.7 2.9 assembled.9
  313.6 2.6 collective-permute-start.39
  319.4 3.6 %assembled.11.refs_2_ = f32[768,3072]{1,0:T(8,128)} custom-call(bf16[768,768]{1,0:T(8,128)(2,1)} %joined_1.1.refs_0_, bf16[768,768]{1,0:T(8,128)(2,1)} %collective-permute-done.40.refs_1_), custom_call_target="tpu_custom_call" | custom-call | flops 10000000000 | bytes 10000000000 | tf_op jit(solution)/shard_map/assembled/pallas_call | solution.py:858
  327.9 2.9 assembled.14
  (126 shorter events, 101.7 us)
Async XLA Ops:
  3.1 18.9 %collective-permute-start = (bf16[1,196,768]{2,1,0:T(8,128)(2,1)}, bf16[1,196,768]{2,1,0:T(8,128)(2,1)S(1)}, u32[]{:S(2)}, u32[]{:S(2)}) collective-permute-start(bf16[1,196,768]{2,1,0:T(8,128)(2,1)} %get-tuple-element.189), channel_id=1, source_target_pairs={{0,16},{1,17},{2,18},{3,19},{4,20},{5,21},{6,22},{7,23},{8,24},{9,... | collective-permute-start | bytes 903176 | tf_op jit(solution)/shard_map/ppermute | solution.py:1038
  7.5 34.6 %collective-permute-start.2 = (bf16[1,196,768]{2,1,0:T(8,128)(2,1)}, bf16[1,196,768]{2,1,0:T(8,128)(2,1)S(1)}, u32[]{:S(2)}, u32[]{:S(2)}) collective-permute-start(bf16[1,196,768]{2,1,0:T(8,128)(2,1)} %get-tuple-element.209), channel_id=1, source_target_pairs={{0,16},{1,17},{2,18},{3,19},{4,20},{5,21},{6,22},{7,23},{8,24},{9,... | collective-permute-start | bytes 903176 | tf_op jit(solution)/shard_map/ppermute | solution.py:1038
  41.7 22.3 %collective-permute-start.1 = (bf16[1,196,768]{2,1,0:T(8,128)(2,1)}, bf16[1,196,768]{2,1,0:T(8,128)(2,1)S(1)}, u32[]{:S(2)}, u32[]{:S(2)}) collective-permute-start(bf16[1,196,768]{2,1,0:T(8,128)(2,1)} %get-tuple-element.208), channel_id=1, source_target_pairs={{16,0},{0,16},{17,1},{1,17},{18,2},{2,18},{19,3},{3,19},{20,4},{4,... | collective-permute-start | bytes 903176 | tf_op jit(solution)/shard_map/ppermute | solution.py:1048
  62.2 24.3 %collective-permute-start.4 = (bf16[1,196,768]{2,1,0:T(8,128)(2,1)}, bf16[1,196,768]{2,1,0:T(8,128)(2,1)S(1)}, u32[]{:S(2)}, u32[]{:S(2)}) collective-permute-start(bf16[1,196,768]{2,1,0:T(8,128)(2,1)} %get-tuple-element.225), channel_id=1, source_target_pairs={{16,0},{17,1},{18,2},{19,3},{20,4},{21,5},{22,6},{23,7},{24,8},{25... | collective-permute-start | bytes 903176 | tf_op jit(solution)/shard_map/ppermute | solution.py:1048
  110.1 16.7 %collective-permute-start.6 = (bf16[1536,768]{1,0:T(8,128)(2,1)}, bf16[1536,768]{1,0:T(8,128)(2,1)}, u32[]{:S(2)}, u32[]{:S(2)}) collective-permute-start(bf16[1536,768]{1,0:T(8,128)(2,1)} %get-tuple-element.259), channel_id=1, source_target_pairs={{0,1},{1,0},{2,3},{3,2},{4,5},{5,4},{6,7},{7,6},{8,9},{9,8},{10,11... | collective-permute-start | bytes 7077896 | tf_op jit(solution)/shard_map/ppermute | solution.py:881
  133.1 38.6 %collective-permute-start.11 = (bf16[768,768]{1,0:T(8,128)(2,1)}, bf16[768,768]{1,0:T(8,128)(2,1)}, u32[]{:S(2)}, u32[]{:S(2)}) collective-permute-start(bf16[768,768]{1,0:T(8,128)(2,1)} %get-tuple-element.274), channel_id=1, source_target_pairs={{0,4},{2,6},{4,0},{6,2},{8,12},{10,14},{12,8},{14,10},{1,5},{3,7},... | collective-permute-start | bytes 3538952 | tf_op jit(solution)/shard_map/ppermute | solution.py:881
  133.1 27.7 %collective-permute-start.9 = (bf16[768,768]{1,0:T(8,128)(2,1)}, bf16[768,768]{1,0:T(8,128)(2,1)}, u32[]{:S(2)}, u32[]{:S(2)}) collective-permute-start(bf16[768,768]{1,0:T(8,128)(2,1)} %get-tuple-element.272), channel_id=1, source_target_pairs={{0,2},{2,0},{4,6},{6,4},{8,10},{10,8},{12,14},{14,12},{1,3},{3,1},... | collective-permute-start | bytes 3538952 | tf_op jit(solution)/shard_map/ppermute | solution.py:881
  137.2 66.6 %collective-permute-start.7 = (f32[16,768]{1,0:T(8,128)}, f32[16,768]{1,0:T(8,128)}, u32[]{:S(2)}, u32[]{:S(2)}) collective-permute-start(f32[16,768]{1,0:T(8,128)} %get-tuple-element.281.value_ref), channel_id=1, source_target_pairs={{0,1},{1,0},{2,3},{3,2},{4,5},{5,4},{6,7},{7,6},{8,9},{9,8},{10,11... | collective-permute-start | bytes 147464 | tf_op jit(solution)/shard_map/ppermute | solution.py:881
  143.2 38.0 %collective-permute-start.8 = (bf16[768,768]{1,0:T(8,128)(2,1)}, bf16[768,768]{1,0:T(8,128)(2,1)}, u32[]{:S(2)}, u32[]{:S(2)}) collective-permute-start(bf16[768,768]{1,0:T(8,128)(2,1)} %get-tuple-element.286), channel_id=1, source_target_pairs={{0,1},{1,0},{2,3},{3,2},{4,5},{5,4},{6,7},{7,6},{8,9},{9,8},{10,11... | collective-permute-start | bytes 3538952 | tf_op jit(solution)/shard_map/ppermute | solution.py:881
  170.2 23.4 %collective-permute-start.14 = (bf16[768,768]{1,0:T(8,128)(2,1)}, bf16[768,768]{1,0:T(8,128)(2,1)}, u32[]{:S(2)}, u32[]{:S(2)}) collective-permute-start(bf16[768,768]{1,0:T(8,128)(2,1)} %get-tuple-element.294), channel_id=1, source_target_pairs={{0,1},{1,0},{2,3},{3,2},{4,5},{5,4},{6,7},{7,6},{8,9},{9,8},{10,11... | collective-permute-start | bytes 3538952 | tf_op jit(solution)/shard_map/ppermute | solution.py:881
  179.3 17.7 %collective-permute-start.13 = (bf16[192,768]{1,0:T(8,128)(2,1)}, bf16[192,768]{1,0:T(8,128)(2,1)}, u32[]{:S(2)}, u32[]{:S(2)}) collective-permute-start(bf16[192,768]{1,0:T(8,128)(2,1)} %get-tuple-element.298), channel_id=1, source_target_pairs={{0,8},{2,10},{4,12},{6,14},{8,0},{10,2},{12,4},{14,6},{1,9},{3,11}... | collective-permute-start | bytes 884744 | tf_op jit(solution)/shard_map/ppermute | solution.py:881
  183.4 18.5 %collective-permute-start.12 = (bf16[384,768]{1,0:T(8,128)(2,1)}, bf16[384,768]{1,0:T(8,128)(2,1)}, u32[]{:S(2)}, u32[]{:S(2)}) collective-permute-start(bf16[384,768]{1,0:T(8,128)(2,1)} %get-tuple-element.301), channel_id=1, source_target_pairs={{0,2},{2,0},{4,6},{6,4},{8,10},{10,8},{12,14},{14,12},{1,3},{3,1},... | collective-permute-start | bytes 1769480 | tf_op jit(solution)/shard_map/ppermute | solution.py:881
  191.2 22.2 %collective-permute-start.20 = (bf16[192,768]{1,0:T(8,128)(2,1)}, bf16[192,768]{1,0:T(8,128)(2,1)}, u32[]{:S(2)}, u32[]{:S(2)}) collective-permute-start(bf16[192,768]{1,0:T(8,128)(2,1)} %get-tuple-element.306), channel_id=1, source_target_pairs={{0,8},{2,10},{4,12},{6,14},{8,0},{10,2},{12,4},{14,6},{1,9},{3,11}... | collective-permute-start | bytes 884744 | tf_op jit(solution)/shard_map/ppermute | solution.py:881
  195.8 22.4 %collective-permute-start.19 = (bf16[384,768]{1,0:T(8,128)(2,1)}, bf16[384,768]{1,0:T(8,128)(2,1)}, u32[]{:S(2)}, u32[]{:S(2)}) collective-permute-start(bf16[384,768]{1,0:T(8,128)(2,1)} %get-tuple-element.308), channel_id=1, source_target_pairs={{0,2},{2,0},{4,6},{6,4},{8,10},{10,8},{12,14},{14,12},{1,3},{3,1},... | collective-permute-start | bytes 1769480 | tf_op jit(solution)/shard_map/ppermute | solution.py:881
  198.8 27.2 %collective-permute-start.17 = (bf16[192,768]{1,0:T(8,128)(2,1)}, bf16[192,768]{1,0:T(8,128)(2,1)}, u32[]{:S(2)}, u32[]{:S(2)}) collective-permute-start(bf16[192,768]{1,0:T(8,128)(2,1)} %summed.4.mine_ref), channel_id=1, source_target_pairs={{0,8},{2,10},{4,12},{6,14},{8,0},{10,2},{12,4},{14,6},{1,9},{3,11}... | collective-permute-start | bytes 884744 | tf_op jit(solution)/shard_map/ppermute | solution.py:881
  203.8 16.4 %collective-permute-start.18 = (bf16[192,768]{1,0:T(8,128)(2,1)}, bf16[192,768]{1,0:T(8,128)(2,1)}, u32[]{:S(2)}, u32[]{:S(2)}) collective-permute-start(bf16[192,768]{1,0:T(8,128)(2,1)} %get-tuple-element.311), channel_id=1, source_target_pairs={{0,4},{2,6},{4,0},{6,2},{8,12},{10,14},{12,8},{14,10},{1,5},{3,7},... | collective-permute-start | bytes 884744 | tf_op jit(solution)/shard_map/ppermute | solution.py:881
  205.2 24.0 %collective-permute-start.16 = (f32[16,768]{1,0:T(8,128)}, f32[16,768]{1,0:T(8,128)}, u32[]{:S(2)}, u32[]{:S(2)}) collective-permute-start(f32[16,768]{1,0:T(8,128)} %added.4.value_ref), channel_id=1, source_target_pairs={{0,2},{2,0},{4,6},{6,4},{8,10},{10,8},{12,14},{14,12},{1,3},{3,1},... | collective-permute-start | bytes 147464 | tf_op jit(solution)/shard_map/ppermute | solution.py:881
  215.2 21.7 %collective-permute-start.23 = (bf16[192,768]{1,0:T(8,128)(2,1)}, bf16[192,768]{1,0:T(8,128)(2,1)}, u32[]{:S(2)}, u32[]{:S(2)}) collective-permute-start(bf16[192,768]{1,0:T(8,128)(2,1)} %summed.5.mine_ref), channel_id=1, source_target_pairs={{0,8},{2,10},{4,12},{6,14},{8,0},{10,2},{12,4},{14,6},{1,9},{3,11}... | collective-permute-start | bytes 884744 | tf_op jit(solution)/shard_map/ppermute | solution.py:881
  221.8 17.6 %collective-permute-start.22 = (bf16[96,768]{1,0:T(8,128)(2,1)}, bf16[96,768]{1,0:T(8,128)(2,1)}, u32[]{:S(2)}, u32[]{:S(2)}) collective-permute-start(bf16[96,768]{1,0:T(8,128)(2,1)} %get-tuple-element.320), channel_id=1, source_target_pairs={{0,8},{2,10},{4,12},{6,14},{8,0},{10,2},{12,4},{14,6},{1,9},{3,11}... | collective-permute-start | bytes 442376 | tf_op jit(solution)/shard_map/ppermute | solution.py:881
  228.0 27.9 %collective-permute-start.27 = (bf16[384,768]{1,0:T(8,128)(2,1)}, bf16[384,768]{1,0:T(8,128)(2,1)}, u32[]{:S(2)}, u32[]{:S(2)}) collective-permute-start(bf16[384,768]{1,0:T(8,128)(2,1)} %joined_4.4.mine_ref), channel_id=1, source_target_pairs={{0,4},{2,6},{4,0},{6,2},{8,12},{10,14},{12,8},{14,10},{1,5},{3,7},... | collective-permute-start | bytes 1769480 | tf_op jit(solution)/shard_map/ppermute | solution.py:881
  230.7 45.9 %collective-permute-start.21 = (f32[16,768]{1,0:T(8,128)}, f32[16,768]{1,0:T(8,128)}, u32[]{:S(2)}, u32[]{:S(2)}) collective-permute-start(f32[16,768]{1,0:T(8,128)} %added.5.value_ref), channel_id=1, source_target_pairs={{0,4},{2,6},{4,0},{6,2},{8,12},{10,14},{12,8},{14,10},{1,5},{3,7},... | collective-permute-start | bytes 147464 | tf_op jit(solution)/shard_map/ppermute | solution.py:881
  235.1 25.3 %collective-permute-start.26 = (bf16[96,768]{1,0:T(8,128)(2,1)}, bf16[96,768]{1,0:T(8,128)(2,1)}, u32[]{:S(2)}, u32[]{:S(2)}) collective-permute-start(bf16[96,768]{1,0:T(8,128)(2,1)} %get-tuple-element.326), channel_id=1, source_target_pairs={{0,8},{2,10},{4,12},{6,14},{8,0},{10,2},{12,4},{14,6},{1,9},{3,11}... | collective-permute-start | bytes 442376 | tf_op jit(solution)/shard_map/ppermute | solution.py:881
  238.8 33.4 %collective-permute-start.29 = (bf16[384,768]{1,0:T(8,128)(2,1)}, bf16[384,768]{1,0:T(8,128)(2,1)}, u32[]{:S(2)}, u32[]{:S(2)}) collective-permute-start(bf16[384,768]{1,0:T(8,128)(2,1)} %joined_4.5.mine_ref), channel_id=1, source_target_pairs={{0,2},{2,0},{4,6},{6,4},{8,10},{10,8},{12,14},{14,12},{1,3},{3,1},... | collective-permute-start | bytes 1769480 | tf_op jit(solution)/shard_map/ppermute | solution.py:881
  241.0 22.3 %collective-permute-start.25 = (bf16[96,768]{1,0:T(8,128)(2,1)}, bf16[96,768]{1,0:T(8,128)(2,1)}, u32[]{:S(2)}, u32[]{:S(2)}) collective-permute-start(bf16[96,768]{1,0:T(8,128)(2,1)} %summed.6.mine_ref), channel_id=1, source_target_pairs={{0,8},{2,10},{4,12},{6,14},{8,0},{10,2},{12,4},{14,6},{1,9},{3,11}... | collective-permute-start | bytes 442376 | tf_op jit(solution)/shard_map/ppermute | solution.py:881
  258.2 26.9 %collective-permute-start.33 = (bf16[768,768]{1,0:T(8,128)(2,1)}, bf16[768,768]{1,0:T(8,128)(2,1)}, u32[]{:S(2)}, u32[]{:S(2)}) collective-permute-start(bf16[768,768]{1,0:T(8,128)(2,1)} %joined_2.3.refs_0_), channel_id=1, source_target_pairs={{0,2},{2,0},{4,6},{6,4},{8,10},{10,8},{12,14},{14,12},{1,3},{3,1},... | collective-permute-start | bytes 3538952 | tf_op jit(solution)/shard_map/ppermute | solution.py:881
  270.1 23.3 %collective-permute-start.32 = (bf16[192,768]{1,0:T(8,128)(2,1)}, bf16[192,768]{1,0:T(8,128)(2,1)}, u32[]{:S(2)}, u32[]{:S(2)}) collective-permute-start(bf16[192,768]{1,0:T(8,128)(2,1)} %joined_4.7.mine_ref), channel_id=1, source_target_pairs={{0,4},{2,6},{4,0},{6,2},{8,12},{10,14},{12,8},{14,10},{1,5},{3,7},... | collective-permute-start | bytes 884744 | tf_op jit(solution)/shard_map/ppermute | solution.py:881
  274.7 44.0 %collective-permute-start.40 = (bf16[768,768]{1,0:T(8,128)(2,1)}, bf16[768,768]{1,0:T(8,128)(2,1)}, u32[]{:S(2)}, u32[]{:S(2)}) collective-permute-start(bf16[768,768]{1,0:T(8,128)(2,1)} %joined_1.1.refs_0_), channel_id=1, source_target_pairs={{0,4},{2,6},{4,0},{6,2},{8,12},{10,14},{12,8},{14,10},{1,5},{3,7},... | collective-permute-start | bytes 3538952 | tf_op jit(solution)/shard_map/ppermute | solution.py:881
  275.8 37.8 %collective-permute-start.35 = (bf16[384,768]{1,0:T(8,128)(2,1)S(1)}, bf16[384,768]{1,0:T(8,128)(2,1)}, u32[]{:S(2)}, u32[]{:S(2)}) collective-permute-start(bf16[384,768]{1,0:T(8,128)(2,1)S(1)} %joined_2.4.refs_0_), channel_id=1, source_target_pairs={{0,2},{2,0},{4,6},{6,4},{8,10},{10,8},{12,14},{14,12},{1,3},{3,1},... | collective-permute-start | bytes 1769480 | tf_op jit(solution)/shard_map/ppermute | solution.py:881
  278.1 29.2 %collective-permute-start.31 = (f32[16,768]{1,0:T(8,128)}, f32[16,768]{1,0:T(8,128)}, u32[]{:S(2)}, u32[]{:S(2)}) collective-permute-start(f32[16,768]{1,0:T(8,128)} %added.6.value_ref), channel_id=1, source_target_pairs={{0,8},{2,10},{4,12},{6,14},{8,0},{10,2},{12,4},{14,6},{1,9},{3,11}... | collective-permute-start | bytes 147464 | tf_op jit(solution)/shard_map/ppermute | solution.py:881
  285.1 25.6 %collective-permute-start.37 = (bf16[768,768]{1,0:T(8,128)(2,1)}, bf16[768,768]{1,0:T(8,128)(2,1)S(1)}, u32[]{:S(2)}, u32[]{:S(2)}) collective-permute-start(bf16[768,768]{1,0:T(8,128)(2,1)} %collective-permute-done.33.refs_1_), channel_id=1, source_target_pairs={{0,1},{1,0},{2,3},{3,2},{4,5},{5,4},{6,7},{7,6},{8,9},{9,8},{10,11... | collective-permute-start | bytes 3538952 | tf_op jit(solution)/shard_map/ppermute | solution.py:881
  293.4 17.3 %collective-permute-start.36 = (bf16[768,768]{1,0:T(8,128)(2,1)}, bf16[768,768]{1,0:T(8,128)(2,1)S(1)}, u32[]{:S(2)}, u32[]{:S(2)}) collective-permute-start(bf16[768,768]{1,0:T(8,128)(2,1)} %joined_2.3.refs_0_), channel_id=1, source_target_pairs={{0,1},{1,0},{2,3},{3,2},{4,5},{5,4},{6,7},{7,6},{8,9},{9,8},{10,11... | collective-permute-start | bytes 3538952 | tf_op jit(solution)/shard_map/ppermute | solution.py:881
  307.2 17.6 %collective-permute-start.34 = (bf16[384,768]{1,0:T(8,128)(2,1)S(1)}, bf16[384,768]{1,0:T(8,128)(2,1)}, u32[]{:S(2)}, u32[]{:S(2)}) collective-permute-start(bf16[384,768]{1,0:T(8,128)(2,1)S(1)} %joined_2.5.refs_0_), channel_id=1, source_target_pairs={{0,2},{2,0},{4,6},{6,4},{8,10},{10,8},{12,14},{14,12},{1,3},{3,1},... | collective-permute-start | bytes 1769480 | tf_op jit(solution)/shard_map/ppermute | solution.py:881
  (20 other events, 181.6 us)
